TPU v7x, 32 devices: a whole 2x2x4 slice. The times are simulated.
32 devices in a mesh: seq: 4 (over y, x), batch: 8 (over z, core).
Axes of the slice: x: 2, y: 2, z: 4, core: 2. Of those that a mesh axis runs over, the one named last changes fastest.
Arguments:
- tokens: bfloat16 [8, 1024, 2048], P('batch', 'seq'), may hold values from -6 to 6
- cotangent: bfloat16 [8, 1024, 2048], P('batch', 'seq'), may hold values from -6 to 6
- segment_ids: int32 [8, 1024], P('batch'), may hold values from 0 to 4, as said below
- positions: int32 [8, 1024], P('batch'), may hold values from 0 to 511, as said below
- attn_gain: float32 [2048], replicated, may hold values from 0.5 to 1.5
- qkv_weight: bfloat16 [2048, 2560], P('batch'), may hold values from -0.125 to 0.125
- out_weight: bfloat16 [2048, 2048], P('batch'), may hold values from -0.75 to 0.75
- mlp_gain: float32 [2048], replicated, may hold values from 0.5 to 1.5
- gate_up_weight: bfloat16 [2048, 11264], P('batch'), may hold values from -0.125 to 0.125
- down_weight: bfloat16 [5632, 2048], P('batch'), may hold values from -0.078125 to 0.078125
Outputs:
- output: bfloat16 [8, 1024, 2048], P('batch', 'seq')
- tokens_grad: bfloat16 [8, 1024, 2048], P('batch', 'seq')
- attn_gain_grad: float32 [2048], replicated
- qkv_weight_grad: float32 [2048, 2560], P('batch')
- out_weight_grad: float32 [2048, 2048], P('batch')
- mlp_gain_grad: float32 [2048], replicated
- gate_up_weight_grad: float32 [2048, 11264], P('batch')
- down_weight_grad: float32 [5632, 2048], P('batch')
Inputs may be any that keep to these rules, and one draw needn't show every extreme that they name: `segment_ids`: within each packed sequence the ids start at 0, rise by one at each new document and never fall; a document has 1 to 512 tokens and never crosses a multiple of 512 tokens; every sequence holds one document of exactly 512 tokens and 5 documents in all. `positions`: A token's position within its document: 0 at the document's first token, rising by one per token; consistent with segment_ids.
All inputs are finite; a program needn't handle non-finite values.
Results may differ from a plain program's by a relative error of at most 0.02.
Values may be sent and summed in bfloat16 or wider, within the bound.
A program may use at most 384 MiB of HBM per device.

v0:
```python
import jax
import jax.numpy as jnp
from jax import lax
from jax.sharding import PartitionSpec as P

H = 32
KV = 4
HD = 64
BLOCK_ROWS = 512


def rms_parts(values, gain_vector):
    inv_rms = lax.rsqrt(jnp.mean(values * values, axis=-1, keepdims=True) + 1e-05)
    return (values * inv_rms * gain_vector, inv_rms)


def norm_back(grad_normed, values, inv_rms, gain_vector):
    weighted = grad_normed * gain_vector
    inner_sum = jnp.mean(weighted * values, axis=-1, keepdims=True)
    return inv_rms * weighted - values * (inv_rms * inv_rms * inv_rms) * inner_sum


def rotary_tables(seq_positions, head_dim):
    half_dim = head_dim // 2
    frequency = 10000.0 ** (-jnp.arange(half_dim, dtype=jnp.float32) * 2.0 / head_dim)
    angles = seq_positions.astype(jnp.float32)[:, None] * frequency[None, :]
    return (jnp.cos(angles)[:, None, :], jnp.sin(angles)[:, None, :])


def rotate(values, cosine, sine_part):
    half_dim = values.shape[-1] // 2
    first_half = values[..., :half_dim]
    second_half = values[..., half_dim:]
    return jnp.concatenate(
        [
            first_half * cosine - second_half * sine_part,
            second_half * cosine + first_half * sine_part,
        ],
        axis=-1,
    )


def fold_product(inputs, weight):
    return jnp.dot(
        inputs,
        lax.all_gather(weight, "batch", axis=0, tiled=True),
        preferred_element_type=jnp.float32,
    )


def transposed_product(grads_out, weight):
    return lax.dot_general(
        grads_out,
        lax.all_gather(weight, "batch", axis=0, tiled=True),
        (((1,), (1,)), ((), ())),
        preferred_element_type=jnp.float32,
    )


def weight_gradient(inputs, grads_out):
    return lax.psum_scatter(
        lax.dot_general(
            inputs, grads_out, (((0,), (0,)), ((), ())), preferred_element_type=jnp.float32
        ).astype(jnp.bfloat16),
        "batch",
        scatter_dimension=0,
        tiled=True,
    ).astype(jnp.float32)


def column_heads(values):
    return lax.all_to_all(values, "seq", split_axis=1, concat_axis=0, tiled=True)


def local(
    tokens,
    cotangent,
    segment_ids,
    positions,
    attn_gain,
    qkv_weight,
    out_weight,
    mlp_gain,
    gate_up_weight,
    down_weight,
):
    seq_count = lax.axis_size("seq")
    model_width = tokens.shape[2]
    local_rows = tokens.shape[1]
    seq_len = local_rows * seq_count
    heads_local = H // seq_count
    groups_all = max(KV, seq_count)
    kv_local = groups_all // seq_count
    copies_each = groups_all // KV
    group_share = heads_local // kv_local
    block_total = seq_len // BLOCK_ROWS
    scale_factor = HD ** (-0.5)
    inputs = tokens[0].astype(jnp.float32)
    normed, inv_first = rms_parts(inputs, attn_gain)
    normed_low = normed.astype(jnp.bfloat16)
    projected = fold_product(normed_low, qkv_weight)
    queries_low = projected[:, :model_width].astype(jnp.bfloat16)
    key_cols = projected[:, model_width : model_width + KV * HD].reshape(local_rows, KV, HD)
    value_cols = projected[:, model_width + KV * HD :].reshape(local_rows, KV, HD)
    keys_dup = (
        jnp.repeat(key_cols, copies_each, axis=1)
        .reshape(local_rows, groups_all * HD)
        .astype(jnp.bfloat16)
    )
    values_dup = (
        jnp.repeat(value_cols, copies_each, axis=1)
        .reshape(local_rows, groups_all * HD)
        .astype(jnp.bfloat16)
    )
    head_queries, head_keys, head_values = (
        lax.all_to_all(queries_low, "seq", split_axis=1, concat_axis=0, tiled=True),
        lax.all_to_all(keys_dup, "seq", split_axis=1, concat_axis=0, tiled=True),
        lax.all_to_all(values_dup, "seq", split_axis=1, concat_axis=0, tiled=True),
    )
    seq_segments = segment_ids[0]
    cosine, sine_part = rotary_tables(positions[0], HD)
    queries_rot = rotate(
        head_queries.reshape(seq_len, heads_local, HD).astype(jnp.float32), cosine, sine_part
    )
    queries_rot = queries_rot.astype(jnp.bfloat16).reshape(seq_len, kv_local, group_share, HD)
    keys_rot = rotate(
        head_keys.reshape(seq_len, kv_local, HD).astype(jnp.float32), cosine, sine_part
    ).astype(jnp.bfloat16)
    values_heads = head_values.reshape(seq_len, kv_local, HD)
    token_index = jnp.arange(seq_len, dtype=jnp.int32)

    def block_scores(block_index, query_block):
        row_start = block_index * BLOCK_ROWS
        query_ids = lax.dynamic_slice_in_dim(token_index, row_start, BLOCK_ROWS, 0)
        query_segments = lax.dynamic_slice_in_dim(seq_segments, row_start, BLOCK_ROWS, 0)
        allowed = (token_index[None, :] <= query_ids[:, None]) & (
            seq_segments[None, :] == query_segments[:, None]
        )
        scores = (
            jnp.einsum("qgsd,kgd->gsqk", query_block, keys_rot, preferred_element_type=jnp.float32)
            * scale_factor
        )
        return jnp.where(allowed[None, None], scores, -1e30)

    def attend(block_index):
        query_block = lax.dynamic_slice_in_dim(queries_rot, block_index * BLOCK_ROWS, BLOCK_ROWS, 0)
        masked = block_scores(block_index, query_block)
        row_max = jnp.max(masked, axis=-1, keepdims=True)
        log_total = row_max + jnp.log(jnp.sum(jnp.exp(masked - row_max), axis=-1, keepdims=True))
        probs_low = jnp.exp(masked - log_total).astype(jnp.bfloat16)
        attended = jnp.einsum(
            "gsqk,kgd->qgsd", probs_low, values_heads, preferred_element_type=jnp.float32
        )
        return (attended.astype(jnp.bfloat16), log_total[..., 0])

    attended_all, log_totals = lax.map(attend, jnp.arange(block_total, dtype=jnp.int32))
    attended_all = attended_all.reshape(seq_len, heads_local * HD)
    attn_tokens = lax.all_to_all(attended_all, "seq", split_axis=0, concat_axis=1, tiled=True)
    attn_proj = fold_product(attn_tokens, out_weight)
    residual = inputs + attn_proj
    normed_mlp, inv_second = rms_parts(residual, mlp_gain)
    normed_mlp_low = normed_mlp.astype(jnp.bfloat16)
    gate_up = fold_product(normed_mlp_low, gate_up_weight)
    ff_width = gate_up.shape[1] // 2
    gate_part = gate_up[:, :ff_width]
    up_part = gate_up[:, ff_width:]
    sigmoid_gate = jax.nn.sigmoid(gate_part)
    hidden_low = (gate_part * sigmoid_gate * up_part).astype(jnp.bfloat16)
    down_out = fold_product(hidden_low, down_weight)
    output = (residual + down_out).astype(jnp.bfloat16)
    grad_out = cotangent[0].astype(jnp.float32)
    grad_down = grad_out.astype(jnp.bfloat16)
    down_part = weight_gradient(hidden_low, grad_down)
    grad_hidden = transposed_product(grad_down, down_weight)
    grad_gate = grad_hidden * up_part * sigmoid_gate * (1.0 + gate_part * (1.0 - sigmoid_gate))
    grad_up = grad_hidden * gate_part * sigmoid_gate
    grad_gate_up = jnp.concatenate([grad_gate, grad_up], axis=1).astype(jnp.bfloat16)
    gate_up_part = weight_gradient(normed_mlp_low, grad_gate_up)
    grad_normed_mlp = transposed_product(grad_gate_up, gate_up_weight)
    mlp_term = jnp.sum(grad_normed_mlp * residual * inv_second, axis=0)
    grad_resid = grad_out + norm_back(grad_normed_mlp, residual, inv_second, mlp_gain)
    grad_proj = grad_resid.astype(jnp.bfloat16)
    out_part = weight_gradient(attn_tokens, grad_proj)
    grad_attn = transposed_product(grad_proj, out_weight).astype(jnp.bfloat16)
    grad_heads = column_heads(grad_attn)
    grad_heads = grad_heads.reshape(seq_len, kv_local, group_share, HD)

    def attend_back(carried, inputs_block):
        key_acc, value_acc = carried
        block_index, log_total = inputs_block
        query_block = lax.dynamic_slice_in_dim(queries_rot, block_index * BLOCK_ROWS, BLOCK_ROWS, 0)
        grad_block = lax.dynamic_slice_in_dim(grad_heads, block_index * BLOCK_ROWS, BLOCK_ROWS, 0)
        masked = block_scores(block_index, query_block)
        softmax_rows = jnp.exp(masked - log_total[..., None])
        probs_low = softmax_rows.astype(jnp.bfloat16)
        grad_probs = jnp.einsum(
            "qgsd,kgd->gsqk", grad_block, values_heads, preferred_element_type=jnp.float32
        )
        inner_sum = jnp.sum(softmax_rows * grad_probs, axis=-1, keepdims=True)
        grad_scores = (softmax_rows * (grad_probs - inner_sum)).astype(jnp.bfloat16)
        grad_query = (
            jnp.einsum("gsqk,kgd->qgsd", grad_scores, keys_rot, preferred_element_type=jnp.float32)
            * scale_factor
        )
        key_acc = (
            key_acc
            + jnp.einsum(
                "gsqk,qgsd->kgd", grad_scores, query_block, preferred_element_type=jnp.float32
            )
            * scale_factor
        )
        value_acc = value_acc + jnp.einsum(
            "gsqk,qgsd->kgd", probs_low, grad_block, preferred_element_type=jnp.float32
        )
        return ((key_acc, value_acc), grad_query)

    empty_heads = jnp.zeros((seq_len, kv_local, HD), jnp.float32)
    (grad_keys, grad_values), grad_queries = lax.scan(
        attend_back,
        (empty_heads, empty_heads),
        (jnp.arange(block_total, dtype=jnp.int32), log_totals),
    )
    grad_queries = grad_queries.reshape(seq_len, heads_local, HD)
    back_queries = (
        rotate(grad_queries, cosine, -sine_part)
        .reshape(seq_len, heads_local * HD)
        .astype(jnp.bfloat16)
    )
    back_keys = (
        rotate(grad_keys, cosine, -sine_part).reshape(seq_len, kv_local * HD).astype(jnp.bfloat16)
    )
    back_values = grad_values.reshape(seq_len, kv_local * HD).astype(jnp.bfloat16)
    token_queries, token_keys, token_values = (
        lax.all_to_all(back_queries, "seq", split_axis=0, concat_axis=1, tiled=True),
        lax.all_to_all(back_keys, "seq", split_axis=0, concat_axis=1, tiled=True),
        lax.all_to_all(back_values, "seq", split_axis=0, concat_axis=1, tiled=True),
    )
    key_sum = token_keys.astype(jnp.float32).reshape(local_rows, KV, copies_each, HD).sum(axis=2)
    value_sum = (
        token_values.astype(jnp.float32).reshape(local_rows, KV, copies_each, HD).sum(axis=2)
    )
    grad_qkv = jnp.concatenate(
        [
            token_queries,
            key_sum.reshape(local_rows, KV * HD).astype(jnp.bfloat16),
            value_sum.reshape(local_rows, KV * HD).astype(jnp.bfloat16),
        ],
        axis=1,
    )
    qkv_part = weight_gradient(normed_low, grad_qkv)
    grad_normed = transposed_product(grad_qkv, qkv_weight)
    attn_term = jnp.sum(grad_normed * inputs * inv_first, axis=0)
    tokens_grad = (grad_resid + norm_back(grad_normed, inputs, inv_first, attn_gain)).astype(
        jnp.bfloat16
    )
    attn_gain_grad, mlp_gain_grad = lax.psum((attn_term, mlp_term), ("seq", "batch"))
    qkv_grad, out_grad, gate_up_grad, down_grad = (
        lax.psum(qkv_part.astype(jnp.bfloat16), "seq").astype(jnp.float32),
        lax.psum(out_part.astype(jnp.bfloat16), "seq").astype(jnp.float32),
        lax.psum(gate_up_part.astype(jnp.bfloat16), "seq").astype(jnp.float32),
        lax.psum(down_part.astype(jnp.bfloat16), "seq").astype(jnp.float32),
    )
    return (
        output[None],
        tokens_grad[None],
        attn_gain_grad,
        qkv_grad,
        out_grad,
        mlp_gain_grad,
        gate_up_grad,
        down_grad,
    )


def solution(mesh):
    return jax.shard_map(
        local,
        mesh=mesh,
        in_specs=(
            P("batch", "seq", None),
            P("batch", "seq", None),
            P("batch", None),
            P("batch", None),
            P(),
            P("batch", None),
            P("batch", None),
            P(),
            P("batch", None),
            P("batch", None),
        ),
        out_specs=(
            P("batch", "seq", None),
            P("batch", "seq", None),
            P(),
            P("batch", None),
            P("batch", None),
            P(),
            P("batch", None),
            P("batch", None),
        ),
        check_vma=False,
    )
```

profile of v0, /device:TPU:0, one launch (start us, length us, event | category | flops | bytes accessed | tf_op | source)
XLA Modules:
  0.0 2058.5 jit_solution(16051898842681383244)
XLA Ops:
  10.8 100.9 %all-gather.5.cloned.1.call-done = bf16[2048,2560]{1,0:T(8,128)(2,1)} async-done(((bf16[256,2560]{1,0:T(8,128)(2,1)}), bf16[2048,2560]{1,0:T(8,128)(2,1)}) %all-gather.5.cloned.1.call-update) | async-done | bytes 10485776 | tf_op jit(solution)/shard_map/all_gather | solution.py:46
  111.8 6.9 convolution_convert_fusion.4
  123.9 4.2 all-to-all-done.1
  132.7 3.8 all-to-all-done.2
  136.4 4.6 all-to-all-start
  144.6 8.7 all-to-all-done
  159.6 31.4 %while.29 = (s32[]{:T(128)}, bf16[2,512,1,8,64]{1,4,3,2,0:T(8,128)(2,1)}, f32[2,1,8,512]{3,2,1,0:T(8,128)}, s32[1024]{0:T(1024)S(1)}, s32[2]{0:T(128)S(1)}, /*in...) while((s32[]{:T(128)}, ...), condition=%wide.region_4.5_spmd.clone, body=%wide.region_1.4_spmd.clone.sunk | while | flops 1121710080 | bytes 63066468 | solution.py:156
  165.2 4.4 exponential_reduce_fusion.2
  169.7 4.6 fusion.140
  177.2 3.7 fusion.139
  180.9 4.4 exponential_reduce_fusion.2
  185.4 4.6 fusion.140
  201.0 12.5 all-to-all-done.3
  213.6 8.2 multiply_reduce_fusion.2
  221.8 365.3 %all-gather.9.cloned.1.call-done = bf16[2048,11264]{1,0:T(8,128)(2,1)} async-done(((bf16[256,11264]{1,0:T(8,128)(2,1)}), bf16[2048,11264]{1,0:T(8,128)(2,1)}) %all-gather.9.cloned.1.call-update) | async-done | bytes 46137360 | tf_op jit(solution)/shard_map/all_gather | solution.py:46
  587.1 25.8 %fusion.103 = f32[256,11264]{1,0:T(8,128)} fusion(bf16[2048,11264]{1,0:T(8,128)(2,1)} %all-gather.9.cloned.1.call-done, f32[256,2048]{1,0:T(8,128)} %get-tuple-element.333, f32[2048]{0:T(1024)S(1)} %copy-done.25, f32[256]{0:T(256)S(1)} %get-tuple-element.331), kind=kOutput, calls=%fused_computation.150 | convolution fusion | flops 11812732928 | bytes 59778048 | tf_op jit(solution)/shard_map/dot_general | solution.py:44
  612.9 176.7 %all-gather.11.cloned.1.call-done = bf16[5632,2048]{1,0:T(8,128)(2,1)} async-done(((bf16[704,2048]{1,0:T(8,128)(2,1)}), bf16[5632,2048]{1,0:T(8,128)(2,1)}) %all-gather.11.cloned.1.call-update) | async-done | bytes 23068688 | tf_op jit(solution)/shard_map/all_gather | solution.py:46
  789.6 18.5 multiply_convert_fusion.1
  808.1 22.1 %multiply_reduce_fusion = (f32[2048]{0:T(1024)}, f32[256]{0:T(256)S(1)}, f32[256,2048]{1,0:T(8,128)}) fusion(f32[256,2048]{1,0:T(8,128)S(1)} %copy-done.3, f32[256]{0:T(256)S(1)} %get-tuple-element.331, f32[2048]{0:T(1024)S(1)} %copy-done.25, bf16[2048,11264]{1,0:T(8,128)(2,1)} %all-gather.9.cloned.1.call-done, bf16[256,5632]{1,0:T(8,128)(2,1)} %get-tuple-element.313, ...), kind=kOutput, calls=%fused_computation.91 | convolution fusion | flops 11825838080 | bytes 56117248 | tf_op jit(solution)/shard_map/dot_general | solution.py:52
  834.1 5.7 convolution_convert_fusion.3
  841.4 6.4 convolution_convert_fusion.5
  852.4 14.2 all-to-all-done.4
  868.8 128.6 %while.30 = (s32[]{:T(128)}, f32[1024,1,64]{0,2,1:T(8,128)}, f32[1024,1,64]{0,2,1:T(8,128)}, f32[2,512,1,8,64]{1,0,4,3,2:T(2,128)}, s32[2]{0:T(128)S(1)}, /*inde...) while((s32[]{:T(128)}, f32[1024,1,64]{0,2,1:T(8,128)}, ...), condition=%wide.region_9.10_spmd.clone.clone, body=%wide.region_7.9_spmd.clone.clone.sunk | while | flops 2724261888 | bytes 167350704 | solution.py:218
  875.6 10.4 fusion.150
  886.0 9.3 fusion.151
  895.3 5.9 fusion.152
  901.2 7.7 fusion.153
  913.7 19.5 dynamic_update_slice.23
  940.0 10.4 fusion.150
  950.4 9.3 fusion.151
  959.7 5.8 fusion.152
  965.6 7.6 fusion.153
  977.9 19.5 dynamic_update_slice.23
  999.2 4.3 all-to-all-start.7
  1009.2 4.2 all-to-all-start.6
  1014.4 4.0 all-to-all-done.6
  1018.4 14.8 all_to_all.125
  1034.1 6.8 convolution_convert_fusion.2
  1042.2 13.2 convolution_convert_fusion.1
  1057.0 21.3 %convolution_convert_fusion = bf16[2048,11264]{1,0:T(8,128)(2,1)} fusion(bf16[256,5632]{1,0:T(8,128)(2,1)} %get-tuple-element.313, bf16[256,5632]{1,0:T(8,128)(2,1)} %get-tuple-element.312, f32[256,2048]{1,0:T(8,128)S(1)} %copy-done.4, f32[2048]{0:T(1024)S(1)} %copy-done.26, f32[256]{0:T(256)S(1)} %copy-done.28), kind=kOutput, calls=%fused_computation.59 | convolution fusion | flops 11847335936 | bytes 54010880 | tf_op jit(solution)/shard_map/dot_general | solution.py:62
  1078.4 68.7 %reduce-scatter.7.cloned.1.call-done = bf16[256,2560]{1,0:T(8,128)(2,1)} async-done(((bf16[2048,2560]{1,0:T(8,128)(2,1)}), bf16[256,2560]{1,0:T(8,128)(2,1)}) %reduce-scatter.7.cloned.1.call-update) | async-done | bytes 1310736 | tf_op jit(solution)/shard_map/reduce_scatter | solution.py:61
  1147.1 228.2 %reduce-scatter.11.cloned.1.call-done = bf16[704,2048]{1,0:T(8,128)(2,1)} async-done(((bf16[5632,2048]{1,0:T(8,128)(2,1)}), bf16[704,2048]{1,0:T(8,128)(2,1)}) %reduce-scatter.11.cloned.1.call-update) | async-done | bytes 2883600 | tf_op jit(solution)/shard_map/reduce_scatter | solution.py:61
  1375.4 444.5 %reduce-scatter.13.cloned.1.call-done = bf16[256,11264]{1,0:T(8,128)(2,1)} async-done(((bf16[2048,11264]{1,0:T(8,128)(2,1)}), bf16[256,11264]{1,0:T(8,128)(2,1)}) %reduce-scatter.13.cloned.1.call-update) | async-done | bytes 5767184
  1819.9 13.5 fusion.59
  1833.4 9.1 fusion.69
  1842.5 38.8 %all-reduce.1 = (f32[2048]{0:T(1024)}, f32[2048]{0:T(1024)}) all-reduce(f32[2048]{0:T(1024)S(1)} %get-tuple-element.252, f32[2048]{0:T(1024)S(1)} %copy-done.38), channel_id=1, replica_groups=mesh['seq'=4,'batch'=8] {'seq','batch'}, use_global_device_ids=true, to_apply=%region_12.13 | all-reduce | flops 4096 | bytes 32768 | tf_op jit(solution)/shard_map/psum | solution.py:256
  1884.5 153.3 %all-reduce.5.cloned.1.call-done = (bf16[256,2560]{1,0:T(8,128)(2,1)}, bf16[256,2048]{1,0:T(8,128)(2,1)}, bf16[256,11264]{1,0:T(8,128)(2,1)}, bf16[704,2048]{1,0:T(8,128)(2,1)}) async-done(((bf16[256,2560]{1,0:T(8,128)(2,1)}, bf16[256,2048]{1,0:T(8,128)(2,1)}, bf16[256,11264]{1,0:T(8,128)(2,1)}, bf16[704,2048]{1,0:T(8,128)(2,1)}), (bf16[256,2560]{1,0:T(8,128)(2,1)}, bf16[256,2048]{1,0:T(8,128)(2,1)}, ...) | async-done | bytes 11010064 | tf_op jit(solution)/shard_map/psum | solution.py:258
  2042.6 5.8 convert_element_type.193
  (223 shorter events, 99.0 us)
Async XLA Ops:
  7.2 104.6 %all-gather.5.cloned.1.call-start = ((), (), s32[]{:S(2)}) async-start(), calls=%async_computation.12 | async-start | bytes 11796480 | tf_op jit(solution)/shard_map/all_gather | solution.py:46
  7.9 193.1 %all-gather.7.cloned.1.call-start = ((), (), s32[]{:S(2)}) async-start(), calls=%async_computation.13 | async-start | bytes 9437184 | tf_op jit(solution)/shard_map/all_gather | solution.py:46
  8.7 578.5 %all-gather.9.cloned.1.call-start = ((), (), s32[]{:S(2)}) async-start(), calls=%async_computation.14 | async-start | bytes 51904512 | tf_op jit(solution)/shard_map/all_gather | solution.py:46
  9.4 102.4 %copy-start.32 = (f32[2048]{0:T(1024)S(1)}, f32[2048]{0:T(1024)}, u32[]{:S(2)}) copy-start(f32[2048]{0:T(1024)} %param.18) | copy-start | bytes 24580
  9.4 780.2 %all-gather.11.cloned.1.call-start = ((), (), s32[]{:S(2)}) async-start(), calls=%async_computation.15 | async-start | bytes 25952256 | tf_op jit(solution)/shard_map/all_gather | solution.py:46
  10.8 100.9 %copy-start.36 = (f32[256]{0:T(256)}, f32[256]{0:T(256)S(1)}, u32[]{:S(2)}) copy-start(f32[256]{0:T(256)S(1)} %get-tuple-element.329) | copy-start | bytes 3076
  111.8 11.4 copy-start.42
  119.5 8.7 all-to-all-start.1
  123.1 20.2 copy-start.34
  128.1 8.3 all-to-all-start.2
  131.5 11.9 copy-start.39
  136.4 16.8 all-to-all-start
  142.2 16.7 copy-start.19
  185.3 4.7 copy-start.30
  196.9 16.7 all-to-all-start.3
  200.4 878.0 %reduce-scatter.9.cloned.1.call-start = ((), (), s32[]{:S(2)}) async-start(), calls=%async_computation.17 | async-start | bytes 9437184 | tf_op jit(solution)/shard_map/reduce_scatter | solution.py:61
  213.5 8.2 copy-start.8
  213.6 373.6 %copy-start.25 = (f32[2048]{0:T(1024)S(1)}, f32[2048]{0:T(1024)}, u32[]{:S(2)}) copy-start(f32[2048]{0:T(1024)} %param.21) | copy-start | bytes 24580
  221.8 608.4 %copy-start.27 = (f32[256]{0:T(256)}, f32[256]{0:T(256)S(1)}, u32[]{:S(2)}) copy-start(f32[256]{0:T(256)S(1)} %get-tuple-element.331) | copy-start | bytes 3076
  612.9 195.2 %copy-start.3 = (f32[256,2048]{1,0:T(8,128)S(1)}, f32[256,2048]{1,0:T(8,128)}, u32[]{:S(2)}) copy-start(f32[256,2048]{1,0:T(8,128)} %get-tuple-element.333) | copy-start | bytes 6291460
  848.8 17.8 all-to-all-start.4
  895.3 5.9 copy-start
  895.3 5.9 copy-start.10
  895.3 13.7 slice-start
  901.2 7.7 slice-start.1
  959.7 5.8 copy-start
  959.7 5.8 copy-start.10
  959.7 13.4 slice-start
  965.5 7.6 slice-start.1
  997.4 9.2 copy-start.12
  997.4 9.2 copy-start.35
  997.4 9.2 copy-start.40
  997.4 9.8 copy-start.20
  999.2 10.0 all-to-all-start.7
  1009.2 9.2 all-to-all-start.6
  1013.4 133.7 %reduce-scatter.7.cloned.1.call-start = ((), (), s32[]{:S(2)}) async-start(), calls=%async_computation.16 | async-start | bytes 11796480 | tf_op jit(solution)/shard_map/reduce_scatter | solution.py:61
  1013.5 20.7 %copy-start.2 = (bf16[1,256,2048]{2,1,0:T(8,128)(2,1)S(1)}, bf16[1,256,2048]{2,1,0:T(8,128)(2,1)}, u32[]{:S(2)}) copy-start(bf16[1,256,2048]{2,1,0:T(8,128)(2,1)} %param.14) | copy-start | bytes 3145732
  1013.5 20.7 %copy-start.33 = (f32[2048]{0:T(1024)S(1)}, f32[2048]{0:T(1024)}, u32[]{:S(2)}) copy-start(f32[2048]{0:T(1024)} %param.18) | copy-start | bytes 24580
  1013.5 20.7 %copy-start.37 = (f32[256]{0:T(256)S(1)}, f32[256]{0:T(256)}, u32[]{:S(2)}) copy-start(f32[256]{0:T(256)} %copy-done.36) | copy-start | bytes 3076
  1041.0 334.4 %reduce-scatter.11.cloned.1.call-start = ((), (), s32[]{:S(2)}) async-start(), calls=%async_computation.18 | async-start | bytes 25952256 | tf_op jit(solution)/shard_map/reduce_scatter | solution.py:61
  1055.4 764.5 %reduce-scatter.13.cloned.1.call-start = ((), (), s32[]{:S(2)}) async-start(), calls=%async_computation.19 | async-start | bytes 51904512
  1078.3 959.5 %all-reduce.5.cloned.1.call-start = ((), (), s32[]{:S(2)}) async-start(), calls=%async_computation.20 | async-start | bytes 22020096 | tf_op jit(solution)/shard_map/psum | solution.py:258
  1819.9 13.5 copy-start.17
  1833.4 9.1 copy-start.38
  1833.4 47.8 %copy-start.7 = (f32[256,2048]{1,0:T(8,128)S(1)}, f32[256,2048]{1,0:T(8,128)}, u32[]{:S(2)}) copy-start(f32[256,2048]{1,0:T(8,128)} %copy-done.5) | copy-start | bytes 6291460
  1833.4 47.8 %copy-start.41 = (f32[256]{0:T(256)S(1)}, f32[256]{0:T(256)}, u32[]{:S(2)}) copy-start(f32[256]{0:T(256)} %get-tuple-element.328) | copy-start | bytes 3076
  2037.8 4.8 copy-start.13
  2042.6 5.8 copy-start.18
  (24 other events, 66.8 us)
Sparse Core Ops, SparseCore 0:
  9.6 102.0 all-gather.4
  113.3 80.3 all-gather.6
  195.4 391.6 all-gather.8
  588.6 200.9 all-gather.10
  839.9 87.6 reduce-scatter.8
  1041.1 106.0 reduce-scatter.6
  1149.5 225.8 reduce-scatter.10
  1377.7 442.1 reduce-scatter.12
  1823.8 213.9 all-reduce.4
where the time goes:
time: 2070 us; the launch traced here: 2060 us
  waiting for transfers between devices  1590 us (77%)
  matrix products  236 us (11%)
  local copies, waits for them, and re-layouts  77 us (4%)
  other arithmetic  58.8 us (3%)
  blocking collectives  53.5 us (3%)
  starting transfers between devices  28 us (1%)
    all_gather x4, waiting for transfers between devices, fold_product(): lax.all_gather(weight, 'batch', axis=0, tiled=True)  643 us
    unnamed x10, waiting for transfers between devices  447 us
    reduce_scatter x3, waiting for transfers between devices, weight_gradient(): lax.psum_scatter(lax.dot_general(inputs, grads_out, (((0,), (0,)), ((), (...  297 us
    psum x1, waiting for transfers between devices, local(): lax.psum(qkv_part.astype(jnp.bfloat16), 'seq').astype(jnp.float32)  153 us
    dot_general x4, matrix products, transposed_product(): lax.dot_general(grads_out, lax.all_gather(weight, 'batch', axis=0, tiled=...  56 us
    dot_general x4, matrix products, fold_product(): jnp.dot(inputs, lax.all_gather(weight, 'batch', axis=0, tiled=True), pref...  54.3 us
    dot_general x4, matrix products, weight_gradient(): lax.dot_general(inputs, grads_out, (((0,), (0,)), ((), ())), preferred_el...  47 us
  transfers between devices with their start and end apart: 16, of which 13 were waited for; matrix products, arithmetic and copies ran while one was open for 15% of the time, Pallas kernels for 0%

commit v1 on v0

v1 whole, which is shorter than its diff:
```python
import jax
import jax.numpy as jnp
from jax import lax
from jax.sharding import PartitionSpec as P

H = 32
KV = 4
HD = 64
DOC_MAX = 512
F32 = jnp.float32
BF16 = jnp.bfloat16
AXES = ("seq", "batch")


def rms_parts(values, gain_vector):
    inv_rms = lax.rsqrt(jnp.mean(values * values, axis=-1, keepdims=True) + 1e-05)
    return (values * inv_rms * gain_vector, inv_rms)


def norm_back(grad_normed, values, inv_rms, gain_vector):
    weighted = grad_normed * gain_vector
    inner_sum = jnp.mean(weighted * values, axis=-1, keepdims=True)
    return inv_rms * weighted - values * (inv_rms * inv_rms * inv_rms) * inner_sum


def rotary_tables(seq_positions, head_dim):
    half_dim = head_dim // 2
    frequency = 10000.0 ** (-jnp.arange(half_dim, dtype=F32) * 2.0 / head_dim)
    angles = seq_positions.astype(F32)[:, None] * frequency[None, :]
    return (jnp.cos(angles)[:, None, :], jnp.sin(angles)[:, None, :])


def rotate(values, cosine, sine_part):
    half_dim = values.shape[-1] // 2
    first_half = values[..., :half_dim]
    second_half = values[..., half_dim:]
    return jnp.concatenate(
        [
            first_half * cosine - second_half * sine_part,
            second_half * cosine + first_half * sine_part,
        ],
        axis=-1,
    )


def dot(left, right):
    return jnp.dot(left, right, preferred_element_type=F32)


def dot_nt(left, right):
    return lax.dot_general(left, right, (((1,), (1,)), ((), ())), preferred_element_type=F32)


def dot_tn(left, right):
    return lax.dot_general(left, right, (((0,), (0,)), ((), ())), preferred_element_type=F32)


class Links:
    def __init__(self):
        self.seq = lax.axis_size("seq")
        self.batch = lax.axis_size("batch")
        self.chips = self.batch // 2
        self.bits = self.seq.bit_length() - 1
        if self.seq != 1 << self.bits or self.batch % 2:
            raise ValueError("mesh sizes")
        self.s = lax.axis_index("seq")
        place = lax.axis_index("batch")
        self.z = place // 2
        self.core = place % 2
        reverse = jnp.zeros_like(self.s)
        for bit in range(self.bits):
            reverse = reverse + ((self.s >> bit) & 1) * (1 << (self.bits - 1 - bit))
        self.part = jnp.where(self.core == 0, reverse, self.s)

    def send(self, array, target):
        pairs = []
        for z in range(self.chips):
            for core in range(2):
                for s in range(self.seq):
                    tz, tc, ts = target(z, core, s)
                    here, there = z * 2 + core, tz * 2 + tc
                    pairs.append((s * self.batch + here, ts * self.batch + there))
        return lax.ppermute(array, AXES, pairs)

    def up(self, array, shift):
        return self.send(array, lambda z, c, s: ((z + shift) % self.chips, c, s))

    def swap_cores(self, array):
        return self.send(array, lambda z, c, s: (z, 1 - c, s))

    def stage(self, array, step):
        masks = (1 << step, 1 << (self.bits - 1 - step))
        return self.send(array, lambda z, c, s: (z, c, s ^ masks[c]))

    def plane_gather(self, array):
        held = [(0, array)]
        level = [(0, -1, array)]
        while level:
            fresh = [
                (mask ^ (1 << (self.bits - 1 - step)), step, self.stage(one, step))
                for mask, last, one in level
                for step in range(last + 1, self.bits)
            ]
            if not fresh:
                return held
            arrays = yield [one for _, _, one in fresh]
            level = [(mask, step, one) for (mask, step, _), one in zip(fresh, arrays)]
            held = held + [(mask, one) for mask, _, one in level]
        return held

    def total(self, value):
        value = value + self.swap_cores(value)
        for step in range(self.bits):
            value = value + self.stage(value, step)
        step = 1
        while step < self.chips:
            mask = step
            value = value + self.send(value, lambda z, c, s: (z ^ mask, c, s))
            step *= 2
        return value

    def gather(self, shard):
        rows, width = shard.shape
        piece = rows // self.seq
        (mine,) = yield [lax.dynamic_slice(shard, (self.part * piece, 0), (piece, width))]
        along = yield [self.up(mine, -k) for k in range(1, self.chips)]
        held = yield from self.plane_gather(jnp.stack(along))
        whole = jnp.zeros((self.chips, self.seq, piece, width), shard.dtype)
        whole = whole.at[0].set(shard.reshape(self.seq, piece, width))
        for mask, one in held:
            whole = lax.dynamic_update_slice(whole, one[:, None], (1, self.part ^ mask, 0, 0))
        whole = whole.reshape(self.chips * rows, width)
        (other,) = yield [self.swap_cores(whole)]
        return whole, other

    def split(self, values):
        count = values.shape[0]
        rows = values.shape[1] // self.batch
        twice = jnp.concatenate([values, values], axis=1)
        turned = lax.dynamic_slice(twice, (0, self.z * 2 * rows), values.shape)
        turned = turned.reshape(count, self.chips, 2, rows)
        first = turned[:, :, 0].reshape(count, self.chips * rows)
        second = turned[:, :, 1].reshape(count, self.chips * rows)
        even = self.core == 0
        return jnp.where(even, first, second), jnp.where(even, second, first)

    def join(self, own, sibling):
        count = own.shape[0]
        rows = own.shape[1] // self.chips
        even = self.core == 0
        first = jnp.where(even, own, sibling).reshape(count, self.chips, rows)
        second = jnp.where(even, sibling, own).reshape(count, self.chips, rows)
        turned = jnp.stack([first, second], axis=2).reshape(count, self.batch * rows)
        twice = jnp.concatenate([turned, turned], axis=1)
        back = (self.chips - self.z) % self.chips
        return lax.dynamic_slice(twice, (0, back * 2 * rows), turned.shape)

    def weight_gradient(self, pair, grads_out):
        own, sibling = pair
        (away,) = yield [dot_tn(sibling, grads_out).astype(BF16)]
        arrived, held = yield [self.swap_cores(away), dot_tn(own, grads_out).astype(BF16)]
        width = held.shape[1]
        held = held.reshape(self.chips, -1, width)
        arrived = arrived.reshape(held.shape)
        for step in range(self.bits):
            half = held.shape[1] // 2
            shape = (self.chips, half, width)
            bit = (self.part >> (self.bits - 1 - step)) & 1
            keep, leave = [
                (
                    lax.dynamic_slice(held, (0, side * half, 0), shape).astype(F32)
                    + lax.dynamic_slice(arrived, (0, side * half, 0), shape).astype(F32)
                ).astype(BF16)
                for side in (bit, 1 - bit)
            ]
            held, leave = yield [keep, leave]
            (arrived,) = yield [self.stage(leave, step)]
        held = yield list(
            (held.astype(F32) + arrived.astype(F32)).astype(BF16)[k] for k in range(self.chips)
        )
        along = yield [self.up(held[k], k) for k in range(1, self.chips)]
        sums = held[0].astype(F32)
        for one in along:
            sums = sums + one.astype(F32)
        (sums,) = yield [sums.astype(BF16)]
        held = yield from self.plane_gather(sums)
        piece = sums.shape[0]
        whole = jnp.zeros((self.seq, piece, width), F32)
        for mask, one in held:
            whole = lax.dynamic_update_slice(whole, one[None].astype(F32), (self.part ^ mask, 0, 0))
        return whole.reshape(self.seq * piece, width)


class Task:
    def __init__(self, steps):
        self.steps = steps
        self.given = None
        self.result = None
        self.done = False


def run(tasks):
    while any(not task.done for task in tasks):
        wanted = []
        for task in list(tasks):
            if task.done:
                continue
            try:
                asked = task.steps.send(task.given)
                wanted.append((task, asked))
            except StopIteration as stop:
                task.result = stop.value
                task.done = True
        flat = [array for _, asked in wanted for array in asked]
        if flat:
            flat = list(lax.optimization_barrier(tuple(flat)))
        for task, asked in wanted:
            task.given, flat = flat[: len(asked)], flat[len(asked) :]


def local(
    tokens,
    cotangent,
    segment_ids,
    positions,
    attn_gain,
    qkv_weight,
    out_weight,
    mlp_gain,
    gate_up_weight,
    down_weight,
):
    links = Links()
    model_width = tokens.shape[2]
    rows = tokens.shape[1]
    if rows * 2 != DOC_MAX:
        raise ValueError("token shard")
    share = H // KV
    kv_width = KV * HD
    scale_factor = HD ** (-0.5)
    ff_width = gate_up_weight.shape[1] // 2

    tasks = []

    def launch(steps, delay=0):
        def later():
            for _ in range(delay):
                yield []
            return (yield from steps)

        tasks.append(Task(later()))
        return tasks[-1]

    def wait(task):
        while not task.done:
            yield []
        return task.result

    qkv_task = launch(links.gather(qkv_weight))
    out_task = launch(links.gather(out_weight), 1)
    gate_task = launch(links.gather(gate_up_weight[:, :ff_width]), 2)
    up_task = launch(links.gather(gate_up_weight[:, ff_width:]), 3)
    down_task = launch(links.gather(down_weight), 4)

    def product(pair, weights):
        return dot(pair[0], weights[0]) + dot(pair[1], weights[1])

    def main():
        inputs = tokens[0].astype(F32)
        normed, inv_first = rms_parts(inputs, attn_gain)
        normed_pair = yield links.split(normed.astype(BF16))
        qkv_pair = yield from wait(qkv_task)
        projected = product(normed_pair, qkv_pair)

        row_start = links.s * rows
        own_segments = lax.dynamic_slice_in_dim(segment_ids[0], row_start, rows, 0)
        other = links.s ^ 1
        other_segments = lax.dynamic_slice_in_dim(segment_ids[0], other * rows, rows, 0)
        own_positions = lax.dynamic_slice_in_dim(positions[0], row_start, rows, 0)
        cosine, sine_part = rotary_tables(own_positions, HD)
        queries = projected[:, :model_width].astype(BF16).reshape(rows, H, HD)
        queries_rot = rotate(queries.astype(F32), cosine, sine_part).astype(BF16)
        queries_rot = queries_rot.reshape(rows, KV, share, HD)
        keys = projected[:, model_width : model_width + kv_width].astype(BF16).reshape(rows, KV, HD)
        keys_rot = rotate(keys.astype(F32), cosine, sine_part).astype(BF16).reshape(rows, kv_width)
        values = projected[:, model_width + kv_width :].astype(BF16)
        own_kv = jnp.concatenate([keys_rot, values], axis=1)
        own_kv, queries_rot = yield [own_kv, queries_rot]
        (other_kv,) = yield [links.send(own_kv, lambda z, c, s: (z, c, s ^ 1))]
        both_kv = jnp.concatenate([own_kv, other_kv], axis=0)
        all_keys = both_kv[:, :kv_width].reshape(2 * rows, KV, HD)
        all_values = both_kv[:, kv_width:].reshape(2 * rows, KV, HD)
        index = jnp.arange(rows, dtype=jnp.int32)
        allowed = jnp.concatenate(
            [
                (index[None, :] <= index[:, None]) & (own_segments[None, :] == own_segments[:, None]),
                (other < links.s) & (other_segments[None, :] == own_segments[:, None]),
            ],
            axis=1,
        )
        scores = (
            jnp.einsum("qgsd,kgd->gsqk", queries_rot, all_keys, preferred_element_type=F32)
            * scale_factor
        )
        masked = jnp.where(allowed[None, None], scores, -1e30)
        row_max = jnp.max(masked, axis=-1, keepdims=True)
        exps = jnp.exp(masked - row_max)
        probs = exps / jnp.sum(exps, axis=-1, keepdims=True)
        probs_low = probs.astype(BF16)
        attended = jnp.einsum("gsqk,kgd->qgsd", probs_low, all_values, preferred_element_type=F32)
        attended = attended.astype(BF16).reshape(rows, model_width)
        attended, probs, probs_low = yield [attended, probs, probs_low]
        attended_pair = links.split(attended)
        out_pair = yield from wait(out_task)
        residual = inputs + product(attended_pair, out_pair)
        normed_mlp, inv_second = rms_parts(residual, mlp_gain)
        mlp_pair = links.split(normed_mlp.astype(BF16))
        residual, inv_second, *mlp_pair = yield [residual, inv_second, *mlp_pair]
        gate_pair = yield from wait(gate_task)
        (gate_part,) = yield [product(mlp_pair, gate_pair)]
        up_pair = yield from wait(up_task)
        up_part = product(mlp_pair, up_pair)
        sigmoid_gate = jax.nn.sigmoid(gate_part)
        hidden_pair = links.split((gate_part * sigmoid_gate * up_part).astype(BF16))
        up_part, *hidden_pair = yield [up_part, *hidden_pair]

        grad_out = cotangent[0].astype(F32)
        grad_down = cotangent[0]
        down_reduce = launch(links.weight_gradient(hidden_pair, grad_down))
        down_pair = yield from wait(down_task)
        grad_hidden = links.join(dot_nt(grad_down, down_pair[0]), dot_nt(grad_down, down_pair[1]))
        grad_gate = grad_hidden * up_part * sigmoid_gate * (1.0 + gate_part * (1.0 - sigmoid_gate))
        grad_gate = grad_gate.astype(BF16)
        grad_up = (grad_hidden * gate_part * sigmoid_gate).astype(BF16)
        grad_gate, grad_up = yield [grad_gate, grad_up]
        gate_reduce = launch(links.weight_gradient(mlp_pair, grad_gate))
        up_reduce = launch(links.weight_gradient(mlp_pair, grad_up), 2)
        grad_normed_mlp = links.join(
            dot_nt(grad_gate, gate_pair[0]) + dot_nt(grad_up, up_pair[0]),
            dot_nt(grad_gate, gate_pair[1]) + dot_nt(grad_up, up_pair[1]),
        )
        mlp_term = jnp.sum(grad_normed_mlp * residual * inv_second, axis=0)
        grad_resid = grad_out + norm_back(grad_normed_mlp, residual, inv_second, mlp_gain)
        grad_resid, mlp_term, grad_proj = yield [grad_resid, mlp_term, grad_resid.astype(BF16)]
        out_reduce = launch(links.weight_gradient(attended_pair, grad_proj), 1)
        grad_heads = links.join(dot_nt(grad_proj, out_pair[0]), dot_nt(grad_proj, out_pair[1]))
        (grad_heads,) = yield [grad_heads.astype(BF16)]
        grad_heads = grad_heads.reshape(rows, KV, share, HD)

        grad_probs = jnp.einsum("qgsd,kgd->gsqk", grad_heads, all_values, preferred_element_type=F32)
        inner_sum = jnp.sum(probs * grad_probs, axis=-1, keepdims=True)
        grad_scores = (probs * (grad_probs - inner_sum)).astype(BF16)
        grad_queries = (
            jnp.einsum("gsqk,kgd->qgsd", grad_scores, all_keys, preferred_element_type=F32)
            * scale_factor
        )
        grad_keys = (
            jnp.einsum("gsqk,qgsd->kgd", grad_scores, queries_rot, preferred_element_type=F32)
            * scale_factor
        )
        grad_values = jnp.einsum("gsqk,qgsd->kgd", probs_low, grad_heads, preferred_element_type=F32)
        grad_kv = jnp.concatenate(
            [grad_keys.reshape(2 * rows, kv_width), grad_values.reshape(2 * rows, kv_width)], axis=1
        )
        away, grad_kv, grad_queries = yield [grad_kv[rows:].astype(BF16), grad_kv, grad_queries]
        (arrived,) = yield [links.send(away, lambda z, c, s: (z, c, s ^ 1))]
        own_grad_kv = grad_kv[:rows] + arrived.astype(F32)
        back_queries = rotate(grad_queries.reshape(rows, H, HD), cosine, -sine_part)
        back_keys = rotate(own_grad_kv[:, :kv_width].reshape(rows, KV, HD), cosine, -sine_part)
        grad_qkv = jnp.concatenate(
            [
                back_queries.reshape(rows, model_width),
                back_keys.reshape(rows, kv_width),
                own_grad_kv[:, kv_width:],
            ],
            axis=1,
        ).astype(BF16)
        (grad_qkv,) = yield [grad_qkv]
        qkv_reduce = launch(links.weight_gradient(normed_pair, grad_qkv))
        output = (residual + product(hidden_pair, down_pair)).astype(BF16)
        grad_normed = links.join(dot_nt(grad_qkv, qkv_pair[0]), dot_nt(grad_qkv, qkv_pair[1]))
        attn_term = jnp.sum(grad_normed * inputs * inv_first, axis=0)
        tokens_grad = (grad_resid + norm_back(grad_normed, inputs, inv_first, attn_gain)).astype(BF16)
        tokens_grad, attn_term, output = yield [tokens_grad, attn_term, output]
        gains = links.total(jnp.concatenate([attn_term, mlp_term]).reshape(-1, 128)).reshape(-1)
        qkv_grad = yield from wait(qkv_reduce)
        out_grad = yield from wait(out_reduce)
        down_grad = yield from wait(down_reduce)
        gate_grad = yield from wait(gate_reduce)
        up_grad = yield from wait(up_reduce)
        return (
            output[None],
            tokens_grad[None],
            gains[:model_width],
            qkv_grad,
            out_grad,
            gains[model_width:],
            jnp.concatenate([gate_grad, up_grad], axis=1),
            down_grad,
        )

    head = launch(main())
    run(tasks)
    return head.result


def solution(mesh):
    return jax.shard_map(
        local,
        mesh=mesh,
        in_specs=(
            P("batch", "seq", None),
            P("batch", "seq", None),
            P("batch", None),
            P("batch", None),
            P(),
            P("batch", None),
            P("batch", None),
            P(),
            P("batch", None),
            P("batch", None),
        ),
        out_specs=(
            P("batch", "seq", None),
            P("batch", "seq", None),
            P(),
            P("batch", None),
            P("batch", None),
            P(),
            P("batch", None),
            P("batch", None),
        ),
        check_vma=False,
    )
```

time: 2070 us -> 1430 us (0.69)
  waiting for transfers between devices: 1590 us -> 704 us
  other arithmetic: 58.8 us -> 209 us
  starting transfers between devices: 28 us -> 143 us
  blocking collectives: 53.5 us -> 0 us
  local copies, waits for them, and re-layouts: 77 us -> 127 us
    ppermute x0 -> x87, waiting for transfers between devices: none -> 704 us  [send(): return lax.ppermute(array, AXES, pairs)]
    all_gather x4 -> x0, waiting for transfers between devices: 643 us -> none  [fold_product(): lax.all_gather(weight, 'batch', axis=0, tiled=True)]
    unnamed x10 -> x0, waiting for transfers between devices: 447 us -> none
    reduce_scatter x3 -> x0, waiting for transfers between devices: 297 us -> none  [weight_gradient(): lax.psum_scatter(lax.dot_general(inputs, grads_out, (((0,), (0,)), ((), (...]
    psum x1 -> x0, waiting for transfers between devices: 153 us -> none  [local(): lax.psum(qkv_part.astype(jnp.bfloat16), 'seq').astype(jnp.float32)]
    ppermute x0 -> x87, starting transfers between devices: none -> 143 us  [send(): return lax.ppermute(array, AXES, pairs)]
    convert_element_type x8 -> x30, other arithmetic: 16.5 us -> 128 us  [the longest x10 70.6 us: weight_gradient(): keep, leave = [(lax.dynamic_slice(held, (0, side * half, 0), shape).astyp...]
    all_to_all x7 -> x0, waiting for transfers between devices: 47.3 us -> none  [the longest x1 14.2 us: column_heads(): lax.all_to_all(values, 'seq', split_axis=1, concat_axis=0, tiled=True)]
  transfers between devices with their start and end apart: 16 -> 87, of which waited for: 13 -> 40; matrix products, arithmetic and copies ran while one was open for 15% -> 27% of each run, Pallas kernels for 0% -> 0%
where the time goes in v1:
time: 1430 us; the launch traced here: 1410 us
  waiting for transfers between devices  704 us (49%)
  matrix products  227 us (16%)
  other arithmetic  209 us (15%)
  starting transfers between devices  143 us (10%)
  local copies, waits for them, and re-layouts  127 us (9%)
    ppermute x87, waiting for transfers between devices, send(): return lax.ppermute(array, AXES, pairs)  704 us
    ppermute x87, starting transfers between devices, send(): return lax.ppermute(array, AXES, pairs)  143 us
    convert_element_type x10, other arithmetic, weight_gradient(): keep, leave = [(lax.dynamic_slice(held, (0, side * half, 0), shape).astyp...  70.6 us
    dot_general x10, matrix products, dot(): return jnp.dot(left, right, preferred_element_type=F32)  63.5 us
    dot_general x10, matrix products, dot_nt(): lax.dot_general(left, right, (((1,), (1,)), ((), ())), preferred_element_...  63.4 us
    dot_general x10, matrix products, dot_tn(): lax.dot_general(left, right, (((0,), (0,)), ((), ())), preferred_element_...  57.3 us
    dynamic_update_slice x15, local copies, waits for them, and re-layouts, gather(): lax.dynamic_update_slice(whole, one[:, None], (1, self.part ^ mask, 0, 0))  29.3 us
  transfers between devices with their start and end apart: 87, of which 40 were waited for; matrix products, arithmetic and copies ran while one was open for 27% of the time, Pallas kernels for 0%

profile of v1, /device:TPU:0, one launch (start us, length us, event | category | flops | bytes accessed | tf_op | source)
XLA Modules:
  0.0 1412.2 jit_solution(4624712119720206834)
XLA Ops:
  24.9 16.6 %collective-permute-done.1 = bf16[64,2560]{1,0:T(8,128)(2,1)} collective-permute-done((bf16[64,2560]{1,0:T(8,128)(2,1)}, bf16[64,2560]{1,0:T(8,128)(2,1)}, u32[]{:S(2)}, u32[]{:S(2)}) %collective-permute-start.1) | collective-permute-done | bytes 327712 | tf_op jit(solution)/shard_map/ppermute | solution.py:83
  54.0 17.7 %collective-permute-done.6 = bf16[64,2048]{1,0:T(8,128)(2,1)S(1)} collective-permute-done((bf16[64,2048]{1,0:T(8,128)(2,1)S(1)}, bf16[64,2048]{1,0:T(8,128)(2,1)S(1)}, u32[]{:S(2)}, u32[]{:S(2)}) %collective-permute-start.6) | collective-permute-done | bytes 262176 | tf_op jit(solution)/shard_map/ppermute | solution.py:83
  75.5 14.0 collective-permute-done.11
  92.9 42.0 %collective-permute-done.12 = bf16[64,5632]{1,0:T(8,128)(2,1)} collective-permute-done((bf16[64,5632]{1,0:T(8,128)(2,1)S(1)}, bf16[64,5632]{1,0:T(8,128)(2,1)}, u32[]{:S(2)}, u32[]{:S(2)}) %collective-permute-start.12) | collective-permute-done | bytes 720928 | tf_op jit(solution)/shard_map/ppermute | solution.py:83
  161.1 15.5 %collective-permute-done.18 = bf16[64,5632]{1,0:T(8,128)(2,1)S(1)} collective-permute-done((bf16[64,5632]{1,0:T(8,128)(2,1)S(1)}, bf16[64,5632]{1,0:T(8,128)(2,1)S(1)}, u32[]{:S(2)}, u32[]{:S(2)}) %collective-permute-start.18) | collective-permute-done | bytes 720928 | tf_op jit(solution)/shard_map/ppermute | solution.py:83
  181.2 25.2 %collective-permute-done.19 = bf16[64,5632]{1,0:T(8,128)(2,1)S(1)} collective-permute-done((bf16[64,5632]{1,0:T(8,128)(2,1)S(1)}, bf16[64,5632]{1,0:T(8,128)(2,1)S(1)}, u32[]{:S(2)}, u32[]{:S(2)}) %collective-permute-start.19) | collective-permute-done | bytes 720928 | tf_op jit(solution)/shard_map/ppermute | solution.py:83
  209.7 15.9 %collective-permute-done.20 = bf16[64,5632]{1,0:T(8,128)(2,1)S(1)} collective-permute-done((bf16[64,5632]{1,0:T(8,128)(2,1)S(1)}, bf16[64,5632]{1,0:T(8,128)(2,1)S(1)}, u32[]{:S(2)}, u32[]{:S(2)}) %collective-permute-start.20) | collective-permute-done | bytes 720928 | tf_op jit(solution)/shard_map/ppermute | solution.py:83
  253.0 30.2 %collective-permute-done.26 = bf16[176,2048]{1,0:T(8,128)(2,1)} collective-permute-done((bf16[176,2048]{1,0:T(8,128)(2,1)}, bf16[176,2048]{1,0:T(8,128)(2,1)}, u32[]{:S(2)}, u32[]{:S(2)}) %collective-permute-start.26) | collective-permute-done | bytes 720928 | tf_op jit(solution)/shard_map/ppermute | solution.py:83
  290.1 12.9 collective-permute-done.27
  326.4 43.0 %collective-permute-done.32 = bf16[256,512]{1,0:T(8,128)(2,1)S(1)} collective-permute-done((bf16[256,512]{1,0:T(8,128)(2,1)S(1)}, bf16[256,512]{1,0:T(8,128)(2,1)S(1)}, u32[]{:S(2)}, u32[]{:S(2)}) %collective-permute-start.32) | collective-permute-done | bytes 262176 | tf_op jit(solution)/shard_map/ppermute | solution.py:83
  369.4 19.7 %collective-permute-done.29 = bf16[3,64,5632]{2,1,0:T(8,128)(2,1)S(1)} collective-permute-done((bf16[3,64,5632]{2,1,0:T(8,128)(2,1)}, bf16[3,64,5632]{2,1,0:T(8,128)(2,1)S(1)}, u32[]{:S(2)}, u32[]{:S(2)}) %collective-permute-start.29) | collective-permute-done | bytes 2162720 | tf_op jit(solution)/shard_map/ppermute | solution.py:83
  408.9 9.7 fusion.53
  418.6 15.3 %fusion.50 = (bf16[4,8,256,512]{2,3,1,0:T(8,128)(2,1)}, f32[4,8,256,512]{2,3,1,0:T(8,128)}) fusion(f32[4,8,256,512]{2,3,1,0:T(8,128)} %get-tuple-element.496, f32[4,8,256]{2,1,0:T(8,128)S(1)} %get-tuple-element.495), kind=kLoop, calls=%fused_computation.265 | loop fusion | flops 8388608 | bytes 41975808 | tf_op jit(solution)/shard_map/convert_element_type | solution.py:309
  461.2 9.7 fusion.37
  483.0 8.7 broadcast_select_fusion.3
  506.9 11.6 multiply_convert_fusion.2
  529.0 9.9 multiply_convert_fusion
  559.2 8.8 broadcast_select_fusion.9
  625.7 9.3 convolution_convert_fusion.2
  635.1 13.3 fusion.1
  651.8 10.4 fusion.3
  676.4 13.2 add_convert_fusion.4
  697.7 9.7 convolution_convert_fusion.1
  709.1 11.1 add_convert_fusion.2
  720.2 43.6 %collective-permute-done.38 = bf16[256,512]{0,1:T(8,128)(2,1)} collective-permute-done((bf16[256,512]{0,1:T(8,128)(2,1)S(1)}, bf16[256,512]{0,1:T(8,128)(2,1)}, u32[]{:S(2)}, u32[]{:S(2)}) %collective-permute-start.38) | collective-permute-done | bytes 262176 | tf_op jit(solution)/shard_map/ppermute | solution.py:83
  764.2 8.9 fusion.63
  782.7 9.2 fusion.12
  802.5 27.0 %collective-permute-done.40 = bf16[4,128,5632]{2,1,0:T(8,128)(2,1)} collective-permute-done((bf16[4,128,5632]{2,1,0:T(8,128)(2,1)}, bf16[4,128,5632]{2,1,0:T(8,128)(2,1)}, u32[]{:S(2)}, u32[]{:S(2)}) %collective-permute-start.40) | collective-permute-done | bytes 5767200 | tf_op jit(solution)/shard_map/ppermute | solution.py:83
  861.1 8.5 add_convert_fusion.11
  869.7 9.2 add_convert_fusion
  878.9 8.7 collective-permute-done.43
  898.2 106.2 %collective-permute-done.51 = bf16[4,128,2048]{2,1,0:T(8,128)(2,1)S(1)} collective-permute-done((bf16[4,128,2048]{2,1,0:T(8,128)(2,1)}, bf16[4,128,2048]{2,1,0:T(8,128)(2,1)S(1)}, u32[]{:S(2)}, u32[]{:S(2)}) %collective-permute-start.51) | collective-permute-done | bytes 2097184 | tf_op jit(solution)/shard_map/ppermute | solution.py:83
  1029.8 29.9 %collective-permute-done.53 = bf16[176,2048]{1,0:T(8,128)(2,1)} collective-permute-done((bf16[176,2048]{1,0:T(8,128)(2,1)}, bf16[176,2048]{1,0:T(8,128)(2,1)}, u32[]{:S(2)}, u32[]{:S(2)}) %collective-permute-start.53) | collective-permute-done | bytes 720928 | tf_op jit(solution)/shard_map/ppermute | solution.py:83
  1066.8 27.9 %collective-permute-done.46 = f32[32,128]{1,0:T(8,128)S(1)} collective-permute-done((f32[32,128]{1,0:T(8,128)S(1)}, f32[32,128]{1,0:T(8,128)S(1)}, u32[]{:S(2)}, u32[]{:S(2)}) %collective-permute-start.46) | collective-permute-done | bytes 16416 | tf_op jit(solution)/shard_map/ppermute | solution.py:83
  1094.7 15.4 %collective-permute-start.47 = (f32[32,128]{1,0:T(8,128)S(1)}, f32[32,128]{1,0:T(8,128)S(1)}, u32[]{:S(2)}, u32[]{:S(2)}) collective-permute-start(f32[32,128]{1,0:T(8,128)S(1)} %add.455), channel_id=1, source_target_pairs={{0,2},{8,10},{16,18},{24,26},{1,3},{9,11},{17,19},{25,27},{2,0},{1... | collective-permute-start | bytes 49160 | tf_op jit(solution)/shard_map/ppermute | solution.py:83
  1131.0 8.9 collective-permute-done.56
  1139.8 25.5 %collective-permute-done.57 = bf16[64,5632]{1,0:T(8,128)(2,1)} collective-permute-done((bf16[64,5632]{1,0:T(8,128)(2,1)}, bf16[64,5632]{1,0:T(8,128)(2,1)}, u32[]{:S(2)}, u32[]{:S(2)}) %collective-permute-start.57) | collective-permute-done | bytes 720928 | tf_op jit(solution)/shard_map/ppermute | solution.py:83
  1174.6 9.8 collective-permute-done.61
  1185.6 26.8 %collective-permute-done.63 = bf16[4,128,2560]{2,1,0:T(8,128)(2,1)S(1)} collective-permute-done((bf16[4,128,2560]{2,1,0:T(8,128)(2,1)S(1)}, bf16[4,128,2560]{2,1,0:T(8,128)(2,1)S(1)}, u32[]{:S(2)}, u32[]{:S(2)}) %collective-permute-start.63) | collective-permute-done | bytes 2621472 | tf_op jit(solution)/shard_map/ppermute | solution.py:83
  1214.5 16.0 %collective-permute-start.70 = (bf16[64,2048]{1,0:T(8,128)(2,1)S(1)}, bf16[64,2048]{1,0:T(8,128)(2,1)S(1)}, u32[]{:S(2)}, u32[]{:S(2)}) collective-permute-start(bf16[64,2048]{1,0:T(8,128)(2,1)S(1)} %get-tuple-element.364), channel_id=1, source_target_pairs={{0,2},{8,10},{16,18},{24,26},{1,3},{9,11},{17,19},{25,27},{2,4},{1... | collective-permute-start | bytes 786440 | tf_op jit(solution)/shard_map/ppermute | solution.py:83
  1244.3 9.3 collective-permute-start.67
  1257.8 15.6 %collective-permute-done.67 = bf16[64,5632]{1,0:T(8,128)(2,1)S(1)} collective-permute-done((bf16[64,5632]{1,0:T(8,128)(2,1)S(1)}, bf16[64,5632]{1,0:T(8,128)(2,1)S(1)}, u32[]{:S(2)}, u32[]{:S(2)}) %collective-permute-start.67) | collective-permute-done | bytes 720928 | tf_op jit(solution)/shard_map/ppermute | solution.py:83
  1273.5 28.4 %collective-permute-done.68 = bf16[64,5632]{1,0:T(8,128)(2,1)S(1)} collective-permute-done((bf16[64,5632]{1,0:T(8,128)(2,1)S(1)}, bf16[64,5632]{1,0:T(8,128)(2,1)S(1)}, u32[]{:S(2)}, u32[]{:S(2)}) %collective-permute-start.68) | collective-permute-done | bytes 720928 | tf_op jit(solution)/shard_map/ppermute | solution.py:83
  1313.2 14.0 collective-permute-done.74
  1336.6 13.4 collective-permute-done.77
  1352.1 16.0 %collective-permute-start.81 = (bf16[64,2560]{1,0:T(8,128)(2,1)S(1)}, bf16[64,2560]{1,0:T(8,128)(2,1)S(1)}, u32[]{:S(2)}, u32[]{:S(2)}) collective-permute-start(bf16[64,2560]{1,0:T(8,128)(2,1)S(1)} %get-tuple-element.386), channel_id=1, source_target_pairs={{0,2},{8,10},{16,18},{24,26},{1,3},{9,11},{17,19},{25,27},{2,4},{1... | collective-permute-start | bytes 983048 | tf_op jit(solution)/shard_map/ppermute | solution.py:83
  1376.2 9.8 collective-permute-done.82
  1392.6 9.9 pad_maximum_fusion
  (552 shorter events, 518.2 us)
Async XLA Ops:
  42.9 28.8 %collective-permute-start.3 = (bf16[3,64,2560]{2,1,0:T(8,128)(2,1)S(1)}, bf16[3,64,2560]{2,1,0:T(8,128)(2,1)S(1)}, u32[]{:S(2)}, u32[]{:S(2)}) collective-permute-start(bf16[3,64,2560]{2,1,0:T(8,128)(2,1)S(1)} %pad_maximum_fusion.12), channel_id=1, source_target_pairs={{0,8},{8,0},{16,24},{24,16},{1,17},{9,25},{17,1},{25,9},{2,10},{10... | collective-permute-start | bytes 2949128 | tf_op jit(solution)/shard_map/ppermute | solution.py:83
  71.8 63.1 %collective-permute-start.9 = (bf16[3,64,2048]{2,1,0:T(8,128)(2,1)S(1)}, bf16[3,64,2048]{2,1,0:T(8,128)(2,1)S(1)}, u32[]{:S(2)}, u32[]{:S(2)}) collective-permute-start(bf16[3,64,2048]{2,1,0:T(8,128)(2,1)S(1)} %pad_maximum_fusion.13), channel_id=1, source_target_pairs={{0,8},{8,0},{16,24},{24,16},{1,17},{9,25},{17,1},{25,9},{2,10},{10... | collective-permute-start | bytes 2359304 | tf_op jit(solution)/shard_map/ppermute | solution.py:83
  72.4 62.5 %collective-permute-start.10 = (bf16[3,64,2048]{2,1,0:T(8,128)(2,1)S(1)}, bf16[3,64,2048]{2,1,0:T(8,128)(2,1)S(1)}, u32[]{:S(2)}, u32[]{:S(2)}) collective-permute-start(bf16[3,64,2048]{2,1,0:T(8,128)(2,1)S(1)} %pad_maximum_fusion.13), channel_id=1, source_target_pairs={{0,16},{8,24},{16,0},{24,8},{1,9},{9,1},{17,25},{25,17},{2,18},{10... | collective-permute-start | bytes 2359304 | tf_op jit(solution)/shard_map/ppermute | solution.py:83
  72.9 62.0 %collective-permute-start.12 = (bf16[64,5632]{1,0:T(8,128)(2,1)S(1)}, bf16[64,5632]{1,0:T(8,128)(2,1)}, u32[]{:S(2)}, u32[]{:S(2)}) collective-permute-start(bf16[64,5632]{1,0:T(8,128)(2,1)S(1)} %copy-done.73), channel_id=1, source_target_pairs={{0,4},{8,12},{16,20},{24,28},{1,5},{9,13},{17,21},{25,29},{2,6},{1... | collective-permute-start | bytes 2162696 | tf_op jit(solution)/shard_map/ppermute | solution.py:83
  72.9 62.0 %collective-permute-start.8 = (bf16[3,64,2560]{2,1,0:T(8,128)(2,1)S(1)}, bf16[3,64,2560]{2,1,0:T(8,128)(2,1)S(1)}, u32[]{:S(2)}, u32[]{:S(2)}) collective-permute-start(bf16[3,64,2560]{2,1,0:T(8,128)(2,1)S(1)} %collective-permute-done.3), channel_id=1, source_target_pairs={{0,16},{8,24},{16,0},{24,8},{1,9},{9,1},{17,25},{25,17},{2,18},{10... | collective-permute-start | bytes 2949128 | tf_op jit(solution)/shard_map/ppermute | solution.py:83
  89.5 45.4 %collective-permute-start.13 = (bf16[64,5632]{1,0:T(8,128)(2,1)S(1)}, bf16[64,5632]{1,0:T(8,128)(2,1)}, u32[]{:S(2)}, u32[]{:S(2)}) collective-permute-start(bf16[64,5632]{1,0:T(8,128)(2,1)S(1)} %copy-done.73), channel_id=1, source_target_pairs={{0,2},{8,10},{16,18},{24,26},{1,3},{9,11},{17,19},{25,27},{2,4},{1... | collective-permute-start | bytes 2162696 | tf_op jit(solution)/shard_map/ppermute | solution.py:83
  136.4 89.2 %collective-permute-start.14 = (bf16[1024,2560]{1,0:T(8,128)(2,1)}, bf16[1024,2560]{1,0:T(8,128)(2,1)}, u32[]{:S(2)}, u32[]{:S(2)}) collective-permute-start(bf16[1024,2560]{1,0:T(8,128)(2,1)} %bitcast.29), channel_id=1, source_target_pairs={{0,1},{8,9},{16,17},{24,25},{1,0},{9,8},{17,16},{25,24},{2,3},{10,... | collective-permute-start | bytes 15728648 | tf_op jit(solution)/shard_map/ppermute | solution.py:83
  154.9 70.7 %collective-permute-start.16 = (bf16[3,64,5632]{2,1,0:T(8,128)(2,1)S(1)}, bf16[3,64,5632]{2,1,0:T(8,128)(2,1)}, u32[]{:S(2)}, u32[]{:S(2)}) collective-permute-start(bf16[3,64,5632]{2,1,0:T(8,128)(2,1)S(1)} %pad_maximum_fusion.2), channel_id=1, source_target_pairs={{0,8},{8,0},{16,24},{24,16},{1,17},{9,25},{17,1},{25,9},{2,10},{10... | collective-permute-start | bytes 6488072 | tf_op jit(solution)/shard_map/ppermute | solution.py:83
  156.4 69.2 %collective-permute-start.17 = (bf16[3,64,5632]{2,1,0:T(8,128)(2,1)S(1)}, bf16[3,64,5632]{2,1,0:T(8,128)(2,1)S(1)}, u32[]{:S(2)}, u32[]{:S(2)}) collective-permute-start(bf16[3,64,5632]{2,1,0:T(8,128)(2,1)S(1)} %pad_maximum_fusion.2), channel_id=1, source_target_pairs={{0,16},{8,24},{16,0},{24,8},{1,9},{9,1},{17,25},{25,17},{2,18},{10... | collective-permute-start | bytes 6488072 | tf_op jit(solution)/shard_map/ppermute | solution.py:83
  158.0 48.4 %collective-permute-start.19 = (bf16[64,5632]{1,0:T(8,128)(2,1)S(1)}, bf16[64,5632]{1,0:T(8,128)(2,1)S(1)}, u32[]{:S(2)}, u32[]{:S(2)}) collective-permute-start(bf16[64,5632]{1,0:T(8,128)(2,1)S(1)} %copy-done.72), channel_id=1, source_target_pairs={{0,4},{8,12},{16,20},{24,28},{1,5},{9,13},{17,21},{25,29},{2,6},{1... | collective-permute-start | bytes 2162696 | tf_op jit(solution)/shard_map/ppermute | solution.py:83
  176.7 49.0 %collective-permute-start.15 = (bf16[3,64,2048]{2,1,0:T(8,128)(2,1)S(1)}, bf16[3,64,2048]{2,1,0:T(8,128)(2,1)S(1)}, u32[]{:S(2)}, u32[]{:S(2)}) collective-permute-start(bf16[3,64,2048]{2,1,0:T(8,128)(2,1)S(1)} %copy-done.67), channel_id=1, source_target_pairs={{0,16},{8,24},{16,0},{24,8},{1,9},{9,1},{17,25},{25,17},{2,18},{10... | collective-permute-start | bytes 2359304 | tf_op jit(solution)/shard_map/ppermute | solution.py:83
  227.2 75.8 %collective-permute-start.23 = (bf16[3,64,5632]{2,1,0:T(8,128)(2,1)}, bf16[3,64,5632]{2,1,0:T(8,128)(2,1)}, u32[]{:S(2)}, u32[]{:S(2)}) collective-permute-start(bf16[3,64,5632]{2,1,0:T(8,128)(2,1)} %pad_maximum_fusion.3), channel_id=1, source_target_pairs={{0,8},{8,0},{16,24},{24,16},{1,17},{9,25},{17,1},{25,9},{2,10},{10... | collective-permute-start | bytes 6488072 | tf_op jit(solution)/shard_map/ppermute | solution.py:83
  227.8 75.2 %collective-permute-start.24 = (bf16[3,64,5632]{2,1,0:T(8,128)(2,1)}, bf16[3,64,5632]{2,1,0:T(8,128)(2,1)}, u32[]{:S(2)}, u32[]{:S(2)}) collective-permute-start(bf16[3,64,5632]{2,1,0:T(8,128)(2,1)} %pad_maximum_fusion.3), channel_id=1, source_target_pairs={{0,16},{8,24},{16,0},{24,8},{1,9},{9,1},{17,25},{25,17},{2,18},{10... | collective-permute-start | bytes 6488072 | tf_op jit(solution)/shard_map/ppermute | solution.py:83
  229.2 73.8 %collective-permute-start.21 = (bf16[1024,2048]{1,0:T(8,128)(2,1)}, bf16[1024,2048]{1,0:T(8,128)(2,1)}, u32[]{:S(2)}, u32[]{:S(2)}) collective-permute-start(bf16[1024,2048]{1,0:T(8,128)(2,1)} %bitcast.34), channel_id=1, source_target_pairs={{0,1},{8,9},{16,17},{24,25},{1,0},{9,8},{17,16},{25,24},{2,3},{10,... | collective-permute-start | bytes 12582920 | tf_op jit(solution)/shard_map/ppermute | solution.py:83
  229.2 73.7 %collective-permute-start.22 = (bf16[3,64,5632]{2,1,0:T(8,128)(2,1)}, bf16[3,64,5632]{2,1,0:T(8,128)(2,1)}, u32[]{:S(2)}, u32[]{:S(2)}) collective-permute-start(bf16[3,64,5632]{2,1,0:T(8,128)(2,1)} %collective-permute-done.16), channel_id=1, source_target_pairs={{0,16},{8,24},{16,0},{24,8},{1,9},{9,1},{17,25},{25,17},{2,18},{10... | collective-permute-start | bytes 6488072 | tf_op jit(solution)/shard_map/ppermute | solution.py:83
  249.1 34.1 %collective-permute-start.26 = (bf16[176,2048]{1,0:T(8,128)(2,1)}, bf16[176,2048]{1,0:T(8,128)(2,1)}, u32[]{:S(2)}, u32[]{:S(2)}) collective-permute-start(bf16[176,2048]{1,0:T(8,128)(2,1)} %constant_dynamic-slice_fusion.3), channel_id=1, source_target_pairs={{0,4},{8,12},{16,20},{24,28},{1,5},{9,13},{17,21},{25,29},{2,6},{1... | collective-permute-start | bytes 2162696 | tf_op jit(solution)/shard_map/ppermute | solution.py:83
  306.1 83.0 %collective-permute-start.28 = (bf16[1024,5632]{1,0:T(8,128)(2,1)}, bf16[1024,5632]{1,0:T(8,128)(2,1)}, u32[]{:S(2)}, u32[]{:S(2)}) collective-permute-start(bf16[1024,5632]{1,0:T(8,128)(2,1)} %bitcast.416), channel_id=1, source_target_pairs={{0,1},{8,9},{16,17},{24,25},{1,0},{9,8},{17,16},{25,24},{2,3},{10,... | collective-permute-start | bytes 34603016 | tf_op jit(solution)/shard_map/ppermute | solution.py:83
  315.6 73.5 %collective-permute-start.30 = (bf16[3,176,2048]{2,1,0:T(8,128)(2,1)S(1)}, bf16[3,176,2048]{2,1,0:T(8,128)(2,1)}, u32[]{:S(2)}, u32[]{:S(2)}) collective-permute-start(bf16[3,176,2048]{2,1,0:T(8,128)(2,1)S(1)} %pad_maximum_fusion.4), channel_id=1, source_target_pairs={{0,8},{8,0},{16,24},{24,16},{1,17},{9,25},{17,1},{25,9},{2,10},{10... | collective-permute-start | bytes 6488072 | tf_op jit(solution)/shard_map/ppermute | solution.py:83
  315.6 73.4 %collective-permute-start.31 = (bf16[3,176,2048]{2,1,0:T(8,128)(2,1)S(1)}, bf16[3,176,2048]{2,1,0:T(8,128)(2,1)}, u32[]{:S(2)}, u32[]{:S(2)}) collective-permute-start(bf16[3,176,2048]{2,1,0:T(8,128)(2,1)S(1)} %pad_maximum_fusion.4), channel_id=1, source_target_pairs={{0,16},{8,24},{16,0},{24,8},{1,9},{9,1},{17,25},{25,17},{2,18},{10... | collective-permute-start | bytes 6488072 | tf_op jit(solution)/shard_map/ppermute | solution.py:83
  318.3 70.8 %collective-permute-start.29 = (bf16[3,64,5632]{2,1,0:T(8,128)(2,1)}, bf16[3,64,5632]{2,1,0:T(8,128)(2,1)S(1)}, u32[]{:S(2)}, u32[]{:S(2)}) collective-permute-start(bf16[3,64,5632]{2,1,0:T(8,128)(2,1)} %collective-permute-done.23), channel_id=1, source_target_pairs={{0,16},{8,24},{16,0},{24,8},{1,9},{9,1},{17,25},{25,17},{2,18},{10... | collective-permute-start | bytes 6488072 | tf_op jit(solution)/shard_map/ppermute | solution.py:83
  318.3 51.0 %collective-permute-start.32 = (bf16[256,512]{1,0:T(8,128)(2,1)S(1)}, bf16[256,512]{1,0:T(8,128)(2,1)S(1)}, u32[]{:S(2)}, u32[]{:S(2)}) collective-permute-start(bf16[256,512]{1,0:T(8,128)(2,1)S(1)} %pad_maximum_fusion.14), channel_id=1, source_target_pairs={{0,8},{8,0},{16,24},{24,16},{1,9},{9,1},{17,25},{25,17},{2,10},{10... | collective-permute-start | bytes 786440 | tf_op jit(solution)/shard_map/ppermute | solution.py:83
  390.5 55.1 %collective-permute-start.33 = (bf16[1024,5632]{1,0:T(8,128)(2,1)}, bf16[1024,5632]{1,0:T(8,128)(2,1)}, u32[]{:S(2)}, u32[]{:S(2)}) collective-permute-start(bf16[1024,5632]{1,0:T(8,128)(2,1)} %bitcast.447), channel_id=1, source_target_pairs={{0,1},{8,9},{16,17},{24,25},{1,0},{9,8},{17,16},{25,24},{2,3},{10,... | collective-permute-start | bytes 34603016 | tf_op jit(solution)/shard_map/ppermute | solution.py:83
  405.0 40.6 %collective-permute-start.34 = (bf16[3,176,2048]{2,1,0:T(8,128)(2,1)}, bf16[3,176,2048]{2,1,0:T(8,128)(2,1)S(1)}, u32[]{:S(2)}, u32[]{:S(2)}) collective-permute-start(bf16[3,176,2048]{2,1,0:T(8,128)(2,1)} %collective-permute-done.30), channel_id=1, source_target_pairs={{0,16},{8,24},{16,0},{24,8},{1,9},{9,1},{17,25},{25,17},{2,18},{10... | collective-permute-start | bytes 6488072 | tf_op jit(solution)/shard_map/ppermute | solution.py:83
  595.0 30.2 %collective-permute-start.36 = (bf16[2816,2048]{1,0:T(8,128)(2,1)}, bf16[2816,2048]{1,0:T(8,128)(2,1)}, u32[]{:S(2)}, u32[]{:S(2)}) collective-permute-start(bf16[2816,2048]{1,0:T(8,128)(2,1)} %convolution_convert_fusion.5), channel_id=1, source_target_pairs={{0,1},{8,9},{16,17},{24,25},{1,0},{9,8},{17,16},{25,24},{2,3},{10,... | collective-permute-start | bytes 34603016 | tf_op jit(solution)/shard_map/ppermute | solution.py:83
  625.2 67.3 %collective-permute-start.37 = (bf16[1024,5632]{1,0:T(8,128)(2,1)}, bf16[1024,5632]{1,0:T(8,128)(2,1)}, u32[]{:S(2)}, u32[]{:S(2)}) collective-permute-start(bf16[1024,5632]{1,0:T(8,128)(2,1)} %convolution_convert_fusion.3), channel_id=1, source_target_pairs={{0,1},{8,9},{16,17},{24,25},{1,0},{9,8},{17,16},{25,24},{2,3},{10,... | collective-permute-start | bytes 34603016 | tf_op jit(solution)/shard_map/ppermute | solution.py:83
  692.5 71.3 %collective-permute-start.39 = (bf16[4,352,2048]{2,1,0:T(8,128)(2,1)}, bf16[4,352,2048]{2,1,0:T(8,128)(2,1)}, u32[]{:S(2)}, u32[]{:S(2)}) collective-permute-start(bf16[4,352,2048]{2,1,0:T(8,128)(2,1)} %get-tuple-element.302), channel_id=1, source_target_pairs={{0,8},{8,0},{16,24},{24,16},{1,17},{9,25},{17,1},{25,9},{2,10},{10... | collective-permute-start | bytes 17301512 | tf_op jit(solution)/shard_map/ppermute | solution.py:83
  707.4 56.5 %collective-permute-start.38 = (bf16[256,512]{0,1:T(8,128)(2,1)S(1)}, bf16[256,512]{0,1:T(8,128)(2,1)}, u32[]{:S(2)}, u32[]{:S(2)}) collective-permute-start(bf16[256,512]{0,1:T(8,128)(2,1)S(1)} %copy-done.77), channel_id=1, source_target_pairs={{0,8},{8,0},{16,24},{24,16},{1,9},{9,1},{17,25},{25,17},{2,10},{10... | collective-permute-start | bytes 786440 | tf_op jit(solution)/shard_map/ppermute | solution.py:83
  763.8 65.7 %collective-permute-start.41 = (bf16[1024,5632]{1,0:T(8,128)(2,1)}, bf16[1024,5632]{1,0:T(8,128)(2,1)}, u32[]{:S(2)}, u32[]{:S(2)}) collective-permute-start(bf16[1024,5632]{1,0:T(8,128)(2,1)} %convolution_convert_fusion.1), channel_id=1, source_target_pairs={{0,1},{8,9},{16,17},{24,25},{1,0},{9,8},{17,16},{25,24},{2,3},{10,... | collective-permute-start | bytes 34603016 | tf_op jit(solution)/shard_map/ppermute | solution.py:83
  763.8 65.7 %collective-permute-start.40 = (bf16[4,128,5632]{2,1,0:T(8,128)(2,1)}, bf16[4,128,5632]{2,1,0:T(8,128)(2,1)}, u32[]{:S(2)}, u32[]{:S(2)}) collective-permute-start(bf16[4,128,5632]{2,1,0:T(8,128)(2,1)} %get-tuple-element.308), channel_id=1, source_target_pairs={{0,8},{8,0},{16,24},{24,16},{1,17},{9,25},{17,1},{25,9},{2,10},{10... | collective-permute-start | bytes 17301512 | tf_op jit(solution)/shard_map/ppermute | solution.py:83
  773.1 29.4 %collective-permute-start.42 = (bf16[1024,2048]{1,0:T(8,128)(2,1)S(1)}, bf16[1024,2048]{1,0:T(8,128)(2,1)}, u32[]{:S(2)}, u32[]{:S(2)}) collective-permute-start(bf16[1024,2048]{1,0:T(8,128)(2,1)S(1)} %copy-done.21), channel_id=1, source_target_pairs={{0,1},{8,9},{16,17},{24,25},{1,0},{9,8},{17,16},{25,24},{2,3},{10,... | collective-permute-start | bytes 12582920 | tf_op jit(solution)/shard_map/ppermute | solution.py:83
  852.7 34.8 %collective-permute-start.43 = (bf16[4,176,2048]{2,1,0:T(8,128)(2,1)}, bf16[4,176,2048]{2,1,0:T(8,128)(2,1)}, u32[]{:S(2)}, u32[]{:S(2)}) collective-permute-start(bf16[4,176,2048]{2,1,0:T(8,128)(2,1)} %get-tuple-element.312), channel_id=1, source_target_pairs={{0,16},{8,24},{16,0},{24,8},{1,9},{9,1},{17,25},{25,17},{2,18},{10... | collective-permute-start | bytes 8650760 | tf_op jit(solution)/shard_map/ppermute | solution.py:83
  887.5 116.8 %collective-permute-start.50 = (bf16[4,128,5632]{2,1,0:T(8,128)(2,1)S(1)}, bf16[4,128,5632]{2,1,0:T(8,128)(2,1)S(1)}, u32[]{:S(2)}, u32[]{:S(2)}) collective-permute-start(bf16[4,128,5632]{2,1,0:T(8,128)(2,1)S(1)} %get-tuple-element.326), channel_id=1, source_target_pairs={{0,8},{8,0},{16,24},{24,16},{1,17},{9,25},{17,1},{25,9},{2,10},{10... | collective-permute-start | bytes 17301512 | tf_op jit(solution)/shard_map/ppermute | solution.py:83
  887.9 116.4 %collective-permute-start.49 = (bf16[4,64,5632]{2,1,0:T(8,128)(2,1)}, bf16[4,64,5632]{2,1,0:T(8,128)(2,1)S(1)}, u32[]{:S(2)}, u32[]{:S(2)}) collective-permute-start(bf16[4,64,5632]{2,1,0:T(8,128)(2,1)} %get-tuple-element.325), channel_id=1, source_target_pairs={{0,16},{8,24},{16,0},{24,8},{1,9},{9,1},{17,25},{25,17},{2,18},{10... | collective-permute-start | bytes 8650760 | tf_op jit(solution)/shard_map/ppermute | solution.py:83
  888.7 115.6 %collective-permute-start.51 = (bf16[4,128,2048]{2,1,0:T(8,128)(2,1)}, bf16[4,128,2048]{2,1,0:T(8,128)(2,1)S(1)}, u32[]{:S(2)}, u32[]{:S(2)}) collective-permute-start(bf16[4,128,2048]{2,1,0:T(8,128)(2,1)} %get-tuple-element.327), channel_id=1, source_target_pairs={{0,8},{8,0},{16,24},{24,16},{1,17},{9,25},{17,1},{25,9},{2,10},{10... | collective-permute-start | bytes 6291464 | tf_op jit(solution)/shard_map/ppermute | solution.py:83
  1006.6 53.1 %collective-permute-start.55 = (bf16[1024,2560]{1,0:T(8,128)(2,1)}, bf16[1024,2560]{1,0:T(8,128)(2,1)}, u32[]{:S(2)}, u32[]{:S(2)}) collective-permute-start(bf16[1024,2560]{1,0:T(8,128)(2,1)} %convolution_convert_fusion.7), channel_id=1, source_target_pairs={{0,1},{8,9},{16,17},{24,25},{1,0},{9,8},{17,16},{25,24},{2,3},{10,... | collective-permute-start | bytes 15728648 | tf_op jit(solution)/shard_map/ppermute | solution.py:83
  1008.5 51.2 %collective-permute-start.53 = (bf16[176,2048]{1,0:T(8,128)(2,1)}, bf16[176,2048]{1,0:T(8,128)(2,1)}, u32[]{:S(2)}, u32[]{:S(2)}) collective-permute-start(bf16[176,2048]{1,0:T(8,128)(2,1)} %get-tuple-element.330), channel_id=1, source_target_pairs={{0,4},{8,12},{16,20},{24,28},{1,5},{9,13},{17,21},{25,29},{2,6},{1... | collective-permute-start | bytes 2162696 | tf_op jit(solution)/shard_map/ppermute | solution.py:83
  1008.5 51.2 %collective-permute-start.54 = (bf16[176,2048]{1,0:T(8,128)(2,1)}, bf16[176,2048]{1,0:T(8,128)(2,1)}, u32[]{:S(2)}, u32[]{:S(2)}) collective-permute-start(bf16[176,2048]{1,0:T(8,128)(2,1)} %get-tuple-element.331), channel_id=1, source_target_pairs={{0,6},{8,14},{16,22},{24,30},{1,7},{9,15},{17,23},{25,31},{2,0},{1... | collective-permute-start | bytes 2162696 | tf_op jit(solution)/shard_map/ppermute | solution.py:83
  1059.7 105.7 %collective-permute-start.59 = (bf16[4,64,5632]{2,1,0:T(8,128)(2,1)}, bf16[4,64,5632]{2,1,0:T(8,128)(2,1)S(1)}, u32[]{:S(2)}, u32[]{:S(2)}) collective-permute-start(bf16[4,64,5632]{2,1,0:T(8,128)(2,1)} %get-tuple-element.345), channel_id=1, source_target_pairs={{0,16},{8,24},{16,0},{24,8},{1,9},{9,1},{17,25},{25,17},{2,18},{10... | collective-permute-start | bytes 8650760 | tf_op jit(solution)/shard_map/ppermute | solution.py:83
  1116.4 49.0 %collective-permute-start.60 = (bf16[4,64,2048]{2,1,0:T(8,128)(2,1)}, bf16[4,64,2048]{2,1,0:T(8,128)(2,1)S(1)}, u32[]{:S(2)}, u32[]{:S(2)}) collective-permute-start(bf16[4,64,2048]{2,1,0:T(8,128)(2,1)} %get-tuple-element.346), channel_id=1, source_target_pairs={{0,16},{8,24},{16,0},{24,8},{1,9},{9,1},{17,25},{25,17},{2,18},{10... | collective-permute-start | bytes 3145736 | tf_op jit(solution)/shard_map/ppermute | solution.py:83
  1120.8 44.6 %collective-permute-start.57 = (bf16[64,5632]{1,0:T(8,128)(2,1)}, bf16[64,5632]{1,0:T(8,128)(2,1)}, u32[]{:S(2)}, u32[]{:S(2)}) collective-permute-start(bf16[64,5632]{1,0:T(8,128)(2,1)} %get-tuple-element.343), channel_id=1, source_target_pairs={{0,4},{8,12},{16,20},{24,28},{1,5},{9,13},{17,21},{25,29},{2,6},{1... | collective-permute-start | bytes 2162696 | tf_op jit(solution)/shard_map/ppermute | solution.py:83
  1120.8 44.6 %collective-permute-start.58 = (bf16[64,5632]{1,0:T(8,128)(2,1)}, bf16[64,5632]{1,0:T(8,128)(2,1)}, u32[]{:S(2)}, u32[]{:S(2)}) collective-permute-start(bf16[64,5632]{1,0:T(8,128)(2,1)} %get-tuple-element.344), channel_id=1, source_target_pairs={{0,6},{8,14},{16,22},{24,30},{1,7},{9,15},{17,23},{25,31},{2,0},{1... | collective-permute-start | bytes 2162696 | tf_op jit(solution)/shard_map/ppermute | solution.py:83
  1170.8 41.6 %collective-permute-start.63 = (bf16[4,128,2560]{2,1,0:T(8,128)(2,1)S(1)}, bf16[4,128,2560]{2,1,0:T(8,128)(2,1)S(1)}, u32[]{:S(2)}, u32[]{:S(2)}) collective-permute-start(bf16[4,128,2560]{2,1,0:T(8,128)(2,1)S(1)} %copy-done.54), channel_id=1, source_target_pairs={{0,8},{8,0},{16,24},{24,16},{1,17},{9,25},{17,1},{25,9},{2,10},{10... | collective-permute-start | bytes 7864328 | tf_op jit(solution)/shard_map/ppermute | solution.py:83
  1212.5 44.5 %collective-permute-start.64 = (bf16[176,2048]{1,0:T(8,128)(2,1)S(1)}, bf16[176,2048]{1,0:T(8,128)(2,1)S(1)}, u32[]{:S(2)}, u32[]{:S(2)}) collective-permute-start(bf16[176,2048]{1,0:T(8,128)(2,1)S(1)} %collective-permute-done.61), channel_id=1, source_target_pairs={{0,16},{8,24},{16,0},{24,8},{1,9},{9,1},{17,25},{25,17},{2,18},{10... | collective-permute-start | bytes 2162696 | tf_op jit(solution)/shard_map/ppermute | solution.py:83
  1213.3 44.6 %collective-permute-start.65 = (bf16[64,5632]{1,0:T(8,128)(2,1)S(1)}, bf16[64,5632]{1,0:T(8,128)(2,1)S(1)}, u32[]{:S(2)}, u32[]{:S(2)}) collective-permute-start(bf16[64,5632]{1,0:T(8,128)(2,1)S(1)} %add_convert_fusion.26), channel_id=1, source_target_pairs={{0,8},{8,0},{16,24},{24,16},{1,17},{9,25},{17,1},{25,9},{2,10},{10... | collective-permute-start | bytes 2162696 | tf_op jit(solution)/shard_map/ppermute | solution.py:83
  1244.3 29.2 %collective-permute-start.67 = (bf16[64,5632]{1,0:T(8,128)(2,1)S(1)}, bf16[64,5632]{1,0:T(8,128)(2,1)S(1)}, u32[]{:S(2)}, u32[]{:S(2)}) collective-permute-start(bf16[64,5632]{1,0:T(8,128)(2,1)S(1)} %get-tuple-element.361), channel_id=1, source_target_pairs={{0,2},{8,10},{16,18},{24,26},{1,3},{9,11},{17,19},{25,27},{2,4},{1... | collective-permute-start | bytes 2162696 | tf_op jit(solution)/shard_map/ppermute | solution.py:83
  1253.6 48.3 %collective-permute-start.68 = (bf16[64,5632]{1,0:T(8,128)(2,1)S(1)}, bf16[64,5632]{1,0:T(8,128)(2,1)S(1)}, u32[]{:S(2)}, u32[]{:S(2)}) collective-permute-start(bf16[64,5632]{1,0:T(8,128)(2,1)S(1)} %get-tuple-element.362), channel_id=1, source_target_pairs={{0,4},{8,12},{16,20},{24,28},{1,5},{9,13},{17,21},{25,29},{2,6},{1... | collective-permute-start | bytes 2162696 | tf_op jit(solution)/shard_map/ppermute | solution.py:83
  1256.9 45.0 %collective-permute-start.69 = (bf16[64,5632]{1,0:T(8,128)(2,1)S(1)}, bf16[64,5632]{1,0:T(8,128)(2,1)S(1)}, u32[]{:S(2)}, u32[]{:S(2)}) collective-permute-start(bf16[64,5632]{1,0:T(8,128)(2,1)S(1)} %get-tuple-element.363), channel_id=1, source_target_pairs={{0,6},{8,14},{16,22},{24,30},{1,7},{9,15},{17,23},{25,31},{2,0},{1... | collective-permute-start | bytes 2162696 | tf_op jit(solution)/shard_map/ppermute | solution.py:83
  1350.0 37.1 %collective-permute-start.79 = (bf16[64,5632]{1,0:T(8,128)(2,1)S(1)}, bf16[64,5632]{1,0:T(8,128)(2,1)S(1)}, u32[]{:S(2)}, u32[]{:S(2)}) collective-permute-start(bf16[64,5632]{1,0:T(8,128)(2,1)S(1)} %collective-permute-done.75), channel_id=1, source_target_pairs={{0,16},{8,24},{16,0},{24,8},{1,9},{9,1},{17,25},{25,17},{2,18},{10... | collective-permute-start | bytes 2162696 | tf_op jit(solution)/shard_map/ppermute | solution.py:83
  (148 other events, 2500.0 us)

commit v2 on v0

v2 whole, which is shorter than its diff:
```python
import functools

import jax
import jax.numpy as jnp
from jax import lax
from jax.experimental import pallas as pl
from jax.experimental.pallas import tpu as pltpu
from jax.sharding import PartitionSpec as P

H = 32
KV = 4
HD = 64
DOC_MAX = 512
F32 = jnp.float32
BF16 = jnp.bfloat16


def rms_parts(values, gain_vector):
    inv_rms = lax.rsqrt(jnp.mean(values * values, axis=-1, keepdims=True) + 1e-05)
    return (values * inv_rms * gain_vector, inv_rms)


def norm_back(grad_normed, values, inv_rms, gain_vector):
    weighted = grad_normed * gain_vector
    inner_sum = jnp.mean(weighted * values, axis=-1, keepdims=True)
    return inv_rms * weighted - values * (inv_rms * inv_rms * inv_rms) * inner_sum


def rotary_tables(seq_positions, head_dim):
    half_dim = head_dim // 2
    frequency = 10000.0 ** (-jnp.arange(half_dim, dtype=F32) * 2.0 / head_dim)
    angles = seq_positions.astype(F32)[:, None] * frequency[None, :]
    return (jnp.cos(angles)[:, None, :], jnp.sin(angles)[:, None, :])


def rotate(values, cosine, sine_part):
    half_dim = values.shape[-1] // 2
    first_half = values[..., :half_dim]
    second_half = values[..., half_dim:]
    return jnp.concatenate(
        [
            first_half * cosine - second_half * sine_part,
            second_half * cosine + first_half * sine_part,
        ],
        axis=-1,
    )


def dot(left, right):
    return jnp.dot(left, right, preferred_element_type=F32)


def dot_nt(left, right):
    return lax.dot_general(left, right, (((1,), (1,)), ((), ())), preferred_element_type=F32)


def dot_tn(left, right):
    return lax.dot_general(left, right, (((0,), (0,)), ((), ())), preferred_element_type=F32)


class Place:
    def __init__(self, chips, bits):
        self.chips, self.bits = chips, bits
        self.s = lax.axis_index("seq")
        place = lax.axis_index("batch")
        self.z, self.core = place // 2, place % 2
        reverse = 0
        for bit in range(bits):
            reverse = reverse + ((self.s // (1 << bit)) % 2) * (1 << (bits - 1 - bit))
        self.part = reverse + self.core * (self.s - reverse)

    def sibling(self):
        return {"batch": self.z * 2 + 1 - self.core}

    def chip(self, shift):
        return {"batch": ((self.z + shift) % self.chips) * 2 + self.core}

    def partner(self, step):
        first, second = 1 << step, 1 << (self.bits - 1 - step)
        mask = first + self.core * (second - first)
        return {"seq": self.s + mask * (1 - 2 * ((self.s // mask) % 2))}

    def fellows(self):
        found = [self.sibling()] + [self.partner(step) for step in range(self.bits)]
        step = 1
        while step < self.chips:
            found.append({"batch": (self.z + step * (1 - 2 * ((self.z // step) % 2))) * 2 + self.core})
            step *= 2
        return found

    def bit(self, step):
        return (self.part // (1 << (self.bits - 1 - step))) % 2

    def part_of(self, subset):
        part = self.part
        for step in range(self.bits):
            if subset >> step & 1:
                weight = 1 << (self.bits - 1 - step)
                part = part + weight * (1 - 2 * self.bit(step))
        return part


def reduce_kernel(chips, bits, count, terms, small, out, arrived, small_out, *scratch):
    halves = scratch[:bits]
    own, got, along, final = scratch[bits : bits + 4]
    (own_sem, got_sem, core_out, core_in, half_out, half_in, along_out, along_in, spread_out, spread_in, local_sem) = (
        scratch[bits + 4 : -4]
    )
    small_sum, small_got, small_send, small_recv = scratch[-4:]
    here = Place(chips, bits)
    rows, width = own.shape[2], own.shape[3]
    piece = rows >> bits
    slots = own.shape[0]
    seq = 1 << bits

    barrier = pltpu.get_barrier_semaphore()
    peers = [here.sibling()] + [here.partner(i) for i in range(bits)] + [here.chip(k) for k in range(1, chips)]
    fellows = here.fellows()
    for peer in peers:
        pl.semaphore_signal(barrier, inc=1, device_id=peer, device_id_type=pl.DeviceIdType.MESH)
    pl.semaphore_wait(barrier, len(peers))

    def columns(j):
        return pl.ds(pl.multiple_of(j * width, 128), width)

    def core_copy(j):
        return pltpu.make_async_remote_copy(
            src_ref=terms.at[:, 1 - here.core, :, columns(j)],
            dst_ref=arrived.at[j],
            send_sem=core_out.at[j],
            recv_sem=core_in.at[j],
            device_id=here.sibling(),
            device_id_type=pl.DeviceIdType.MESH,
        )

    def own_load(j):
        return pltpu.make_async_copy(terms.at[:, here.core, :, columns(j)], own.at[j % slots], own_sem.at[j])

    def got_load(j):
        return pltpu.make_async_copy(arrived.at[j], got.at[j % 2], got_sem.at[j])

    def offset(step):
        total = 0
        for i in range(step):
            total = total + here.bit(i) * (rows >> (i + 1))
        return total

    def half_copy(j, step):
        half = rows >> (step + 1)
        first = pl.multiple_of(offset(step) + (1 - here.bit(step)) * half, piece)
        return pltpu.make_async_remote_copy(
            src_ref=own.at[j % slots, :, pl.ds(first, half), :],
            dst_ref=halves[step].at[j],
            send_sem=half_out.at[j, step],
            recv_sem=half_in.at[j, step],
            device_id=here.partner(step),
            device_id_type=pl.DeviceIdType.MESH,
        )

    def along_copy(j, k):
        first = pl.multiple_of(offset(bits), piece)
        return pltpu.make_async_remote_copy(
            src_ref=own.at[j % slots, (here.z + k) % chips, pl.ds(first, piece), :],
            dst_ref=along.at[j, k - 1],
            send_sem=along_out.at[j, k - 1],
            recv_sem=along_in.at[j, k - 1],
            device_id=here.chip(k),
            device_id_type=pl.DeviceIdType.MESH,
        )

    def place_of(j, subset):
        return out.at[pl.ds(pl.multiple_of(here.part_of(subset) * piece, piece), piece), columns(j)]

    def spread_copy(j, subset):
        last = subset.bit_length() - 1
        parent = subset ^ (1 << last)
        return pltpu.make_async_remote_copy(
            src_ref=final.at[j] if parent == 0 else place_of(j, parent),
            dst_ref=place_of(j, parent),
            send_sem=spread_out.at[j, subset - 1],
            recv_sem=spread_in.at[j, subset - 1],
            device_id=here.partner(last),
            device_id_type=pl.DeviceIdType.MESH,
        )

    def local_copy(j):
        return pltpu.make_async_copy(final.at[j], place_of(j, 0), local_sem.at[j])

    def level(size):
        return [subset for subset in range(1, seq) if bin(subset).count("1") == size]

    def fresh(j):
        core_copy(j).start()

    def loads(j):
        core_copy(j).wait()
        own_load(j).start()
        got_load(j).start()

    def first_sum(j):
        own_load(j).wait()
        got_load(j).wait()
        block = 32 if rows % 32 == 0 else 16
        blocks = rows // block
        slot = j % slots

        def body(index, carry):
            z = index // blocks
            span = pl.ds(pl.multiple_of((index % blocks) * block, block), block)
            own[slot, z, span, :] = (
                own[slot, z, span, :].astype(F32) + got[j % 2, z, span, :].astype(F32)
            ).astype(BF16)
            return carry

        lax.fori_loop(0, chips * blocks, body, 0)

    def half_sum(j, step):
        half_copy(j, step).wait()
        half = rows >> (step + 1)
        block = 32 if half % 32 == 0 else 16
        blocks = half // block
        slot = j % slots
        start = offset(step + 1)

        def body(index, carry):
            z = index // blocks
            first = (index % blocks) * block
            there = pl.ds(pl.multiple_of(first, block), block)
            span = pl.ds(pl.multiple_of(start + first, block), block)
            own[slot, z, span, :] = (
                own[slot, z, span, :].astype(F32) + halves[step][j, z, there, :].astype(F32)
            ).astype(BF16)
            return carry

        lax.fori_loop(0, chips * blocks, body, 0)

    def send_along(j):
        for k in range(1, chips):
            along_copy(j, k).start()

    def last_sum(j):
        for k in range(1, chips):
            along_copy(j, k).wait()
        block = 16
        slot = j % slots
        start = offset(bits)

        def body(index, carry):
            first = index * block
            there = pl.ds(pl.multiple_of(first, block), block)
            total = own[slot, here.z, pl.ds(pl.multiple_of(start + first, block), block), :].astype(F32)
            for k in range(chips - 1):
                total = total + along[j, k, there, :].astype(F32)
            final[j, there, :] = total.astype(BF16)
            return carry

        lax.fori_loop(0, piece // block, body, 0)
        local_copy(j).start()
        for subset in level(1):
            spread_copy(j, subset).start()

    def pass_on(j, size):
        for subset in level(size):
            spread_copy(j, subset).wait()
        for subset in level(size + 1):
            spread_copy(j, subset).start()

    def small_copy(step):
        return pltpu.make_async_remote_copy(
            src_ref=small_sum.at[step],
            dst_ref=small_got.at[step],
            send_sem=small_send.at[step],
            recv_sem=small_recv.at[step],
            device_id=fellows[step],
            device_id_type=pl.DeviceIdType.MESH,
        )

    def small_step(step):
        if step:
            small_copy(step - 1).wait()
            small_sum[step] = small_sum[step - 1] + small_got[step - 1]
        if step < len(fellows):
            small_copy(step).start()
        else:
            small_out[...] = small_sum[step]

    stages = [fresh, loads, first_sum, lambda j: half_copy(j, 0).start()]
    for step in range(bits):

        def stage(j, step=step):
            half_sum(j, step)
            if step + 1 < bits:
                half_copy(j, step + 1).start()
            else:
                send_along(j)

        stages.append(stage)
    stages.append(last_sum)
    for size in range(1, bits + 1):
        stages.append(lambda j, size=size: pass_on(j, size))
    stages.append(lambda j: local_copy(j).wait())
    order = list(range(3, len(stages))) + [2, 1, 0]

    def round_of(now, carry):
        for step in range(len(fellows) + 1):

            @pl.when(now == step)
            def _(step=step):
                small_step(step)

        for number in order:
            chunk = now - number

            @pl.when((chunk >= 0) & (chunk < count))
            def _(number=number, chunk=chunk):
                stages[number](chunk)

        return carry

    small_sum[0] = small[...]
    lax.fori_loop(0, count + len(stages) - 1, round_of, 0)


def reduced(terms, small, chips, bits, count, number):
    rows, width = terms.shape[0] // (2 * chips), terms.shape[1]
    seq, wide = 1 << bits, width // count
    piece = rows // seq
    slots = bits + 5
    dma = pltpu.SemaphoreType.DMA
    steps = 1 + bits + (chips - 1).bit_length()
    out, _, small_out = pl.pallas_call(
        functools.partial(reduce_kernel, chips, bits, count),
        out_shape=(
            jax.ShapeDtypeStruct((rows, width), BF16),
            jax.ShapeDtypeStruct((count, chips, rows, wide), BF16),
            jax.ShapeDtypeStruct(small.shape, F32),
        ),
        in_specs=[pl.BlockSpec(memory_space=pl.ANY), pl.BlockSpec(memory_space=pltpu.VMEM)],
        out_specs=(
            pl.BlockSpec(memory_space=pl.ANY),
            pl.BlockSpec(memory_space=pl.ANY),
            pl.BlockSpec(memory_space=pltpu.VMEM),
        ),
        scratch_shapes=[pltpu.VMEM((count, chips, rows >> (step + 1), wide), BF16) for step in range(bits)]
        + [
            pltpu.VMEM((slots, chips, rows, wide), BF16),
            pltpu.VMEM((2, chips, rows, wide), BF16),
            pltpu.VMEM((count, chips - 1, piece, wide), BF16),
            pltpu.VMEM((count, piece, wide), BF16),
            dma((count,)),
            dma((count,)),
            dma((count,)),
            dma((count,)),
            dma((count, bits)),
            dma((count, bits)),
            dma((count, chips - 1)),
            dma((count, chips - 1)),
            dma((count, seq - 1)),
            dma((count, seq - 1)),
            dma((count,)),
            pltpu.VMEM((steps + 1,) + small.shape, F32),
            pltpu.VMEM((steps,) + small.shape, F32),
            dma((steps,)),
            dma((steps,)),
        ],
        compiler_params=pltpu.CompilerParams(
            collective_id=number, has_side_effects=True, vmem_limit_bytes=62 * 1024 * 1024
        ),
        cost_estimate=pl.CostEstimate(flops=0, bytes_accessed=800_000_000, transcendentals=0),
    )(terms.reshape(chips, 2, rows, width), small)
    return out, small_out


def gather_kernel(chips, bits, units, weights, *refs):
    shards, wholes = refs[:weights], refs[weights : 2 * weights]
    held = refs[2 * weights : 3 * weights]
    (in_sem, own_sem, along_out, along_in, spread_out, spread_in, turn_out, turn_in) = refs[3 * weights :]
    here = Place(chips, bits)
    seq = 1 << bits

    barrier = pltpu.get_barrier_semaphore()
    peers = [here.sibling()] + [here.partner(i) for i in range(bits)] + [here.chip(k) for k in range(1, chips)]
    for peer in peers:
        pl.semaphore_signal(barrier, inc=1, device_id=peer, device_id_type=pl.DeviceIdType.MESH)
    pl.semaphore_wait(barrier, len(peers))

    def rows_of(unit, shift):
        which, first, width = units[unit]
        count = shards[which].shape[0]
        row = (((here.z - shift) % chips) * 2 + here.core) * count
        return which, row, count, first, width

    def piece_of(unit, shift, subset):
        which, row, count, first, width = rows_of(unit, shift)
        part = here.part_of(subset)
        if (count // seq) % 16 == 0:
            size = count // seq
            return which, pl.ds(pl.multiple_of(row + part * size, 16), size), pl.ds(first, width)
        size = width // seq
        return which, pl.ds(pl.multiple_of(row, 16), count), pl.ds(pl.multiple_of(first + part * size, 128), size)

    def remote(source, target, sems, index, device):
        return pltpu.make_async_remote_copy(
            src_ref=source,
            dst_ref=target,
            send_sem=sems[0].at[index],
            recv_sem=sems[1].at[index],
            device_id=device,
            device_id_type=pl.DeviceIdType.MESH,
        )

    def along(unit, k):
        which, row, count, first, width = rows_of(unit, 0)
        _, there, columns = piece_of(unit, 0, 0)
        part = here.part
        if (count // seq) % 16 == 0:
            size = count // seq
            source = shards[which].at[pl.ds(pl.multiple_of(part * size, 16), size), columns]
        else:
            source = shards[which].at[:, columns]
        return remote(source, wholes[which].at[there, columns], (along_out, along_in), (unit, k - 1), here.chip(k))

    def spread(unit, k, subset):
        last = subset.bit_length() - 1
        which, there, columns = piece_of(unit, k, subset ^ (1 << last))
        region = wholes[which].at[there, columns]
        return remote(region, region, (spread_out, spread_in), (unit, k - 1, subset - 1), here.partner(last))

    def turn(unit, k):
        which, row, count, first, width = rows_of(unit, k)
        there = pl.ds(pl.multiple_of(row, 16), count)
        region = wholes[which].at[there, pl.ds(first, width)]
        source = region if k else shards[which].at[:, pl.ds(first, width)]
        return remote(source, region, (turn_out, turn_in), (unit, k), here.sibling())

    def load(which):
        return pltpu.make_async_copy(shards[which], held[which], in_sem.at[which])

    def store(which):
        count = shards[which].shape[0]
        row = (here.z * 2 + here.core) * count
        there = pl.ds(pl.multiple_of(row, 16), count)
        return pltpu.make_async_copy(held[which], wholes[which].at[there], own_sem.at[which])

    def level(size):
        return [subset for subset in range(1, seq) if bin(subset).count("1") == size]

    shifts = range(1, chips)

    def begin(unit):
        for k in shifts:
            along(unit, k).start()
        turn(unit, 0).start()

    def arrive(unit):
        for k in shifts:
            along(unit, k).wait()
            for subset in level(1):
                spread(unit, k, subset).start()

    def pass_on(unit, size):
        for k in shifts:
            for subset in level(size):
                spread(unit, k, subset).wait()
            for subset in level(size + 1):
                spread(unit, k, subset).start()
            if size == bits:
                turn(unit, k).start()

    def finish(unit):
        for k in range(chips):
            turn(unit, k).wait()

    for which in range(weights):
        load(which).start()
    stages = [begin, arrive]
    for size in range(1, bits + 1):
        stages.append(lambda unit, size=size: pass_on(unit, size))
    stages.append(finish)
    begin(0)
    for now in range(len(units) + len(stages) - 2):
        for number, stage in enumerate(stages):
            unit = now - number + 1
            if 0 <= unit < len(units) and not (number == 0 and unit == 0):
                stage(unit)
        if now < weights:
            load(now).wait()
            store(now).start()
    for which in range(weights):
        if which >= len(units) + len(stages) - 2:
            load(which).wait()
            store(which).start()
    for which in range(weights):
        store(which).wait()


def gathered(shards, chips, bits, units):
    weights, seq, count = len(shards), 1 << bits, len(units)
    dma = pltpu.SemaphoreType.DMA
    return pl.pallas_call(
        functools.partial(gather_kernel, chips, bits, units, weights),
        out_shape=tuple(jax.ShapeDtypeStruct((2 * chips * one.shape[0], one.shape[1]), one.dtype) for one in shards),
        in_specs=[pl.BlockSpec(memory_space=pl.ANY)] * weights,
        out_specs=tuple(pl.BlockSpec(memory_space=pl.ANY) for _ in shards),
        scratch_shapes=[pltpu.VMEM(one.shape, one.dtype) for one in shards]
        + [
            dma((weights,)),
            dma((weights,)),
            dma((count, chips - 1)),
            dma((count, chips - 1)),
            dma((count, chips - 1, seq - 1)),
            dma((count, chips - 1, seq - 1)),
            dma((count, chips)),
            dma((count, chips)),
        ],
        compiler_params=pltpu.CompilerParams(
            collective_id=1, has_side_effects=True, vmem_limit_bytes=62 * 1024 * 1024
        ),
        cost_estimate=pl.CostEstimate(flops=0, bytes_accessed=900_000_000, transcendentals=0),
    )(*shards)


def parts_of(which, width, count):
    return tuple((which, i * (width // count), width // count) for i in range(count))


def sum_rows(terms):
    mine = lax.psum_scatter(terms, "batch", scatter_dimension=0, tiled=True)
    return lax.psum(mine, "seq").astype(F32)


def local(
    tokens,
    cotangent,
    segment_ids,
    positions,
    attn_gain,
    qkv_weight,
    out_weight,
    mlp_gain,
    gate_up_weight,
    down_weight,
):
    seq = lax.axis_size("seq")
    chips = lax.axis_size("batch") // 2
    bits = seq.bit_length() - 1
    s = lax.axis_index("seq")
    swap = [(i, i ^ 1) for i in range(seq)]
    model_width = tokens.shape[2]
    rows = tokens.shape[1]
    if rows * 2 != DOC_MAX:
        raise ValueError("token shard")
    share = H // KV
    kv_width = KV * HD
    scale_factor = HD ** (-0.5)
    ff_width = gate_up_weight.shape[1] // 2

    shards = (qkv_weight, out_weight, gate_up_weight, down_weight)
    cuts = (1, 1, 8, max(1, min(4, model_width // (seq * 128))))
    units = sum((parts_of(i, one.shape[1], n) for i, (one, n) in enumerate(zip(shards, cuts))), ())
    qkv_whole, out_whole, gate_up_whole, down_whole = gathered(shards, chips, bits, units)

    inputs = tokens[0].astype(F32)
    normed, inv_first = rms_parts(inputs, attn_gain)
    normed_low = normed.astype(BF16)
    projected = dot(normed_low, qkv_whole)

    row_start = s * rows
    own_segments = lax.dynamic_slice_in_dim(segment_ids[0], row_start, rows, 0)
    other = s ^ 1
    other_segments = lax.dynamic_slice_in_dim(segment_ids[0], other * rows, rows, 0)
    own_positions = lax.dynamic_slice_in_dim(positions[0], row_start, rows, 0)
    cosine, sine_part = rotary_tables(own_positions, HD)
    queries = projected[:, :model_width].astype(BF16).reshape(rows, H, HD)
    queries_rot = rotate(queries.astype(F32), cosine, sine_part).astype(BF16)
    queries_rot = queries_rot.reshape(rows, KV, share, HD)
    keys = projected[:, model_width : model_width + kv_width].astype(BF16).reshape(rows, KV, HD)
    keys_rot = rotate(keys.astype(F32), cosine, sine_part).astype(BF16).reshape(rows, kv_width)
    values = projected[:, model_width + kv_width :].astype(BF16)
    own_kv = jnp.concatenate([keys_rot, values], axis=1)
    other_kv = lax.ppermute(own_kv, "seq", swap)
    both_kv = jnp.concatenate([own_kv, other_kv], axis=0)
    all_keys = both_kv[:, :kv_width].reshape(2 * rows, KV, HD)
    all_values = both_kv[:, kv_width:].reshape(2 * rows, KV, HD)
    index = jnp.arange(rows, dtype=jnp.int32)
    allowed = jnp.concatenate(
        [
            (index[None, :] <= index[:, None]) & (own_segments[None, :] == own_segments[:, None]),
            (other < s) & (other_segments[None, :] == own_segments[:, None]),
        ],
        axis=1,
    )
    scores = (
        jnp.einsum("qgsd,kgd->gsqk", queries_rot, all_keys, preferred_element_type=F32)
        * scale_factor
    )
    masked = jnp.where(allowed[None, None], scores, -1e30)
    row_max = jnp.max(masked, axis=-1, keepdims=True)
    exps = jnp.exp(masked - row_max)
    probs = exps / jnp.sum(exps, axis=-1, keepdims=True)
    probs_low = probs.astype(BF16)
    attended = jnp.einsum("gsqk,kgd->qgsd", probs_low, all_values, preferred_element_type=F32)
    attended = attended.astype(BF16).reshape(rows, model_width)
    residual = inputs + dot(attended, out_whole)
    normed_mlp, inv_second = rms_parts(residual, mlp_gain)
    normed_mlp_low = normed_mlp.astype(BF16)
    gate_up = dot(normed_mlp_low, gate_up_whole)
    gate_part = gate_up[:, :ff_width]
    up_part = gate_up[:, ff_width:]
    sigmoid_gate = jax.nn.sigmoid(gate_part)
    hidden_low = (gate_part * sigmoid_gate * up_part).astype(BF16)
    output = (residual + dot(hidden_low, down_whole)).astype(BF16)

    grad_out = cotangent[0].astype(F32)
    grad_down = cotangent[0]
    down_terms = dot_tn(hidden_low, grad_down).astype(BF16)
    grad_hidden = dot_nt(grad_down, down_whole)
    grad_gate = grad_hidden * up_part * sigmoid_gate * (1.0 + gate_part * (1.0 - sigmoid_gate))
    grad_up = grad_hidden * gate_part * sigmoid_gate
    grad_gate_up = jnp.concatenate([grad_gate, grad_up], axis=1).astype(BF16)
    gate_up_terms = dot_tn(normed_mlp_low, grad_gate_up).astype(BF16)
    grad_normed_mlp = dot_nt(grad_gate_up, gate_up_whole)
    mlp_term = jnp.sum(grad_normed_mlp * residual * inv_second, axis=0)
    grad_resid = grad_out + norm_back(grad_normed_mlp, residual, inv_second, mlp_gain)
    grad_proj = grad_resid.astype(BF16)
    out_grad = sum_rows(dot_tn(attended, grad_proj).astype(BF16))
    grad_heads = dot_nt(grad_proj, out_whole)
    grad_heads = grad_heads.astype(BF16).reshape(rows, KV, share, HD)

    grad_probs = jnp.einsum("qgsd,kgd->gsqk", grad_heads, all_values, preferred_element_type=F32)
    inner_sum = jnp.sum(probs * grad_probs, axis=-1, keepdims=True)
    grad_scores = (probs * (grad_probs - inner_sum)).astype(BF16)
    grad_queries = (
        jnp.einsum("gsqk,kgd->qgsd", grad_scores, all_keys, preferred_element_type=F32)
        * scale_factor
    )
    grad_keys = (
        jnp.einsum("gsqk,qgsd->kgd", grad_scores, queries_rot, preferred_element_type=F32)
        * scale_factor
    )
    grad_values = jnp.einsum("gsqk,qgsd->kgd", probs_low, grad_heads, preferred_element_type=F32)
    grad_kv = jnp.concatenate(
        [grad_keys.reshape(2 * rows, kv_width), grad_values.reshape(2 * rows, kv_width)], axis=1
    )
    away = grad_kv[rows:].astype(BF16)
    arrived = lax.ppermute(away, "seq", swap)
    own_grad_kv = grad_kv[:rows] + arrived.astype(F32)
    back_queries = rotate(grad_queries.reshape(rows, H, HD), cosine, -sine_part)
    back_keys = rotate(own_grad_kv[:, :kv_width].reshape(rows, KV, HD), cosine, -sine_part)
    grad_qkv = jnp.concatenate(
        [
            back_queries.reshape(rows, model_width),
            back_keys.reshape(rows, kv_width),
            own_grad_kv[:, kv_width:],
        ],
        axis=1,
    ).astype(BF16)
    qkv_grad = sum_rows(dot_tn(normed_low, grad_qkv).astype(BF16))
    grad_normed = dot_nt(grad_qkv, qkv_whole)
    attn_term = jnp.sum(grad_normed * inputs * inv_first, axis=0)
    tokens_grad = (grad_resid + norm_back(grad_normed, inputs, inv_first, attn_gain)).astype(BF16)
    gains = jnp.concatenate([attn_term, mlp_term]).reshape(-1, 128)
    gate_up_grad, gains = reduced(gate_up_terms, gains, chips, bits, 11, 0)
    gains = gains.reshape(-1)
    if down_weight.shape[0] // seq % 16 == 0:
        down_grad, _ = reduced(down_terms, jnp.zeros((8, 128), F32), chips, bits, 8, 2)
    else:
        down_grad = sum_rows(down_terms)
    return (
        output[None],
        tokens_grad[None],
        gains[:model_width],
        qkv_grad,
        out_grad,
        gains[model_width:],
        gate_up_grad.astype(F32),
        down_grad.astype(F32),
    )


def solution(mesh):
    return jax.shard_map(
        local,
        mesh=mesh,
        in_specs=(
            P("batch", "seq", None),
            P("batch", "seq", None),
            P("batch", None),
            P("batch", None),
            P(),
            P("batch", None),
            P("batch", None),
            P(),
            P("batch", None),
            P("batch", None),
        ),
        out_specs=(
            P("batch", "seq", None),
            P("batch", "seq", None),
            P(),
            P("batch", None),
            P("batch", None),
            P(),
            P("batch", None),
            P("batch", None),
        ),
        check_vma=False,
    )
```

time: 2070 us -> 1130 us (0.55)
  waiting for transfers between devices: 1590 us -> 123 us
  Pallas kernels: 0 us -> 733 us
  local copies, waits for them, and re-layouts: 77 us -> 6.1 us
  blocking collectives: 53.5 us -> 0 us
  matrix products: 236 us -> 199 us
  starting transfers between devices: 28 us -> 4.05 us
    pallas_call x0 -> x3, Pallas kernels: none -> 733 us  [the longest x2 427 us: reduced(): pl.pallas_call(functools.partial(reduce_kernel, chips, bits, count), out_...]
    all_gather x4 -> x0, waiting for transfers between devices: 643 us -> none  [fold_product(): lax.all_gather(weight, 'batch', axis=0, tiled=True)]
    unnamed x10 -> x3, waiting for transfers between devices: 447 us -> 0.05 us
    reduce_scatter x3 -> x2, waiting for transfers between devices: 297 us -> 117 us  [sum_rows(): mine = lax.psum_scatter(terms, 'batch', scatter_dimension=0, tiled=True)]
    psum x1, waiting for transfers between devices: 153 us -> 0.01 us  [sum_rows(): return lax.psum(mine, 'seq').astype(F32)]
    all_to_all x7 -> x0, waiting for transfers between devices: 47.3 us -> none  [the longest x1 14.2 us: column_heads(): lax.all_to_all(values, 'seq', split_axis=1, concat_axis=0, tiled=True)]
    dot_general x26 -> x17, matrix products: 236 us -> 190 us  [the longest x4 64.2 us: dot_nt(): lax.dot_general(left, right, (((1,), (1,)), ((), ())), preferred_element_...]
    dynamic_update_slice x4 -> x0, local copies, waits for them, and re-layouts: 41.2 us -> none  [local(): lax.scan(attend_back, (empty_heads, empty_heads), (jnp.arange(block_total...]
  transfers between devices with their start and end apart: 16 -> 5, of which waited for: 13 -> 4; matrix products, arithmetic and copies ran while one was open for 15% -> 11% of each run, Pallas kernels for 0% -> 38%
where the time goes in v2:
time: 1130 us
  Pallas kernels  733 us (65%)
  matrix products  199 us (18%)
  waiting for transfers between devices  123 us (11%)
  other arithmetic  45.7 us (4%)
  between operations  14.8 us (1%)
    pallas_call x2, Pallas kernels, reduced(): pl.pallas_call(functools.partial(reduce_kernel, chips, bits, count), out_...  427 us
    pallas_call x1, Pallas kernels, gathered(): pl.pallas_call(functools.partial(gather_kernel, chips, bits, units, weigh...  306 us
    reduce_scatter x2, waiting for transfers between devices, sum_rows(): mine = lax.psum_scatter(terms, 'batch', scatter_dimension=0, tiled=True)  117 us
    dot_general x4, matrix products, dot_nt(): lax.dot_general(left, right, (((1,), (1,)), ((), ())), preferred_element_...  64.2 us
    dot_general x4, matrix products, dot(): return jnp.dot(left, right, preferred_element_type=F32)  49.8 us
    dot_general x4, matrix products, dot_tn(): lax.dot_general(left, right, (((0,), (0,)), ((), ())), preferred_element_...  46.6 us
  transfers between devices with their start and end apart: 5, of which 4 were waited for; matrix products, arithmetic and copies ran while one was open for 11% of the time, Pallas kernels for 38%

profile of v2, /device:TPU:0, one launch (start us, length us, event | category | flops | bytes accessed | tf_op | source)
XLA Modules:
  0.0 1126.2 jit_solution(12037025281818422851)
XLA Ops:
  7.2 1.5 fusion.15
  8.7 0.6 multiply_multiply_fusion
  9.4 306.0 %shard_map.161 = (bf16[2048,2560]{1,0:T(8,128)(2,1)}, bf16[2048,2048]{1,0:T(8,128)(2,1)}, bf16[2048,11264]{1,0:T(8,128)(2,1)}, bf16[5632,2048]{1,0:T(8,128)(2,1)}) custom-call(bf16[256,2560]{1,0:T(8,128)(2,1)} %refs_0_.1, bf16[256,2048]{1,0:T(8,128)(2,1)} %refs_1_.1, bf16[256,11264]{1,0:T(8,128)(2,1)} %refs_2_.1, bf16[704,2048]{1,0:T(8,128)(2,1)} %refs_3_.1), custom_call_target="tpu_custom_call" | custom-call | bytes 900000000 | tf_op jit(solution)/shard_map/pallas_call | solution.py:500
  315.4 6.9 convolution_convert_fusion.4
  322.5 0.7 constant_dynamic-slice_fusion
  323.2 0.8 fusion.44
  324.2 0.7 pad_maximum_fusion.17
  324.9 2.1 collective-permute-start
  327.0 1.6 slice_convert_fusion
  328.6 2.1 copy.39
  330.9 0.7 pad_add_fusion
  331.5 1.3 subtract_convert_fusion.1
  332.8 1.3 collective-permute-done
  334.2 1.0 pad_maximum_fusion.9
  335.6 8.8 fusion.58
  344.4 7.4 fusion.27
  351.7 6.2 multiply_reduce_fusion.2
  358.0 23.9 %fusion.56 = f32[256,11264]{1,0:T(8,128)} fusion(bf16[2048,11264]{1,0:T(8,128)(2,1)} %get-tuple-element.17, f32[256,2048]{1,0:T(8,128)S(1)} %get-tuple-element.59, f32[2048]{0:T(1024)S(1)} %copy-done.22, f32[256]{0:T(256)S(1)} %get-tuple-element.53), kind=kOutput, calls=%fused_computation.119 | convolution fusion | flops 11812732928 | bytes 59778048 | tf_op jit(solution)/shard_map/dot_general | solution.py:50
  381.9 28.4 %multiply_convert_fusion.1 = (bf16[256,5632]{1,0:T(8,128)(2,1)}, bf16[256,5632]{1,0:T(8,128)(2,1)}, bf16[256,5632]{1,0:T(8,128)(2,1)}) fusion(f32[256,11264]{1,0:T(8,128)} %fusion.56, bf16[5632,2048]{1,0:T(8,128)(2,1)} %get-tuple-element.18, bf16[1,256,2048]{2,1,0:T(8,128)(2,1)S(1)} %copy-done.8), kind=kOutput, calls=%fused_computation.20 | convolution fusion | flops 5928648704 | bytes 44302336 | tf_op jit(solution)/shard_map/dot_general | solution.py:54
  410.4 21.6 %multiply_reduce_fusion = (f32[2048]{0:T(1024)S(1)}, f32[256]{0:T(256)S(1)}, f32[256,2048]{1,0:T(8,128)}) fusion(f32[256,2048]{1,0:T(8,128)S(1)} %get-tuple-element.59, f32[256]{0:T(256)S(1)} %get-tuple-element.53, f32[2048]{0:T(1024)S(1)} %copy-done.22, bf16[2048,11264]{1,0:T(8,128)(2,1)} %get-tuple-element.17, bf16[256,5632]{1,0:T(8,128)(2,1)} %get-tuple-element.29, ...), kind=kOutput, calls=%fused_computation.49 | convolution fusion | flops 11825838080 | bytes 56117248 | tf_op jit(solution)/shard_map/dot_general | solution.py:54
  432.0 3.2 subtract_add_fusion
  435.2 5.6 convolution_convert_fusion.3
  440.9 5.7 convolution_convert_fusion.5
  447.2 10.9 fusion.1
  458.0 12.0 %fusion.3 = bf16[4,8,256,512]{2,3,1,0:T(8,128)(2,1)S(1)} fusion(f32[4,512,256,8]{2,1,3,0:T(8,128)} %get-tuple-element.62, f32[4,8,256]{2,1,0:T(8,128)S(1)} %get-tuple-element.61, f32[4,8,256,512]{2,3,1,0:T(8,128)} %get-tuple-element.57, f32[4,8,256]{2,1,0:T(8,128)S(1)} %get-tuple-element.56), kind=kLoop, calls=%fused_computation.7 | loop fusion | flops 16777216 | bytes 42008576 | tf_op jit(solution)/shard_map/convert_element_type | solution.py:632
  470.1 2.6 fusion.30
  472.7 7.3 fusion.8
  480.1 1.8 collective-permute-start.1
  481.9 1.6 convolution_multiply_fusion
  484.0 4.4 collective-permute-done.1
  488.6 6.7 convolution_convert_fusion.2
  495.4 1.5 copy-done.5
  496.9 12.8 %fusion.14 = bf16[1,256,2048]{2,1,0:T(8,128)(2,1)} fusion(f32[256,2048]{1,0:T(8,128)S(1)} %copy-done.5, bf16[256,5632]{1,0:T(8,128)(2,1)} %get-tuple-element.30, bf16[5632,2048]{1,0:T(8,128)(2,1)} %get-tuple-element.18), kind=kOutput, calls=%fused_computation.38 | convolution fusion | flops 5906628608 | bytes 29097984 | tf_op jit(solution)/shard_map/dot_general | solution.py:50
  509.7 21.2 %convolution_convert_fusion = bf16[2048,11264]{1,0:T(8,128)(2,1)} fusion(bf16[256,5632]{1,0:T(8,128)(2,1)} %get-tuple-element.29, bf16[256,5632]{1,0:T(8,128)(2,1)} %get-tuple-element.28, f32[256,2048]{1,0:T(8,128)S(1)} %copy-done.5, f32[2048]{0:T(1024)S(1)} %copy-done.22, f32[256]{0:T(256)S(1)} %get-tuple-element.53), kind=kOutput, calls=%fused_computation.1 | convolution fusion | flops 11847335936 | bytes 54010880 | tf_op jit(solution)/shard_map/dot_general | solution.py:58
  530.9 6.7 reduce-scatter.5.cloned.1.call-done
  537.6 110.7 %reduce-scatter.3.cloned.1.call-done = bf16[256,2560]{1,0:T(8,128)(2,1)} async-done(((bf16[2048,2560]{1,0:T(8,128)(2,1)}), bf16[256,2560]{1,0:T(8,128)(2,1)}) %reduce-scatter.3.cloned.1.call-update) | async-done | bytes 1310736 | tf_op jit(solution)/shard_map/reduce_scatter | solution.py:528
  648.3 13.1 %convolution_convert_fusion.1 = bf16[5632,2048]{1,0:T(8,128)(2,1)} fusion(bf16[256,5632]{1,0:T(8,128)(2,1)} %get-tuple-element.30, bf16[1,256,2048]{2,1,0:T(8,128)(2,1)S(1)} %copy-done.9), kind=kOutput, calls=%fused_computation.2 | convolution fusion | flops 5917114368 | bytes 27000832 | tf_op jit(solution)/shard_map/dot_general | solution.py:58
  661.4 0.6 broadcast_in_dim.22.small
  662.0 166.6 %shard_map.163 = (bf16[704,2048]{1,0:T(8,128)(2,1)}, bf16[8,4,704,256]{3,2,1,0:T(8,128)(2,1)}, f32[8,128]{1,0:T(8,128)}) custom-call(bf16[4,2,704,2048]{3,2,1,0:T(8,128)(2,1)} %bitcast.116, f32[8,128]{1,0:T(8,128)} %broadcast_in_dim.22.small), custom_call_target="tpu_custom_call" | custom-call | bytes 800000000 | tf_op jit(solution)/shard_map/pallas_call | solution.py:331
  828.6 5.2 convert_element_type.133
  833.8 8.4 fusion.24
  842.2 0.6 pad_maximum_fusion.20.small
  842.8 260.7 %shard_map.162 = (bf16[256,11264]{1,0:T(8,128)(2,1)}, bf16[11,4,256,1024]{3,2,1,0:T(8,128)(2,1)}, f32[32,128]{1,0:T(8,128)}) custom-call(bf16[4,2,256,11264]{3,2,1,0:T(8,128)(2,1)} %bitcast.115, f32[32,128]{1,0:T(8,128)} %pad_maximum_fusion.20.small), custom_call_target="tpu_custom_call" | custom-call | bytes 800000000 | tf_op jit(solution)/shard_map/pallas_call | solution.py:331
  1103.6 8.6 convert_element_type.131
  1112.2 0.6 slice_bitcast_fusion
  1112.8 1.6 fusion.31
  1114.5 3.2 convert_element_type.128
  1117.7 1.6 convert_element_type.130
  (92 shorter events, 2.3 us)
Async XLA Ops:
  7.2 530.4 %reduce-scatter.5.cloned.1.call-start = ((), (), s32[]{:S(2)}) async-start(), calls=%async_computation.3 | async-start | bytes 9437184 | tf_op jit(solution)/shard_map/reduce_scatter | solution.py:528
  9.4 306.0 %copy-start.27 = (f32[256]{0:T(256)}, f32[256]{0:T(256)S(1)}, u32[]{:S(2)}) copy-start(f32[256]{0:T(256)S(1)} %get-tuple-element.51) | copy-start | bytes 3076
  9.4 306.0 %copy-start = (bf16[1,256,2048]{2,1,0:T(8,128)(2,1)S(1)}, bf16[1,256,2048]{2,1,0:T(8,128)(2,1)}, u32[]{:S(2)}) copy-start(bf16[1,256,2048]{2,1,0:T(8,128)(2,1)} %param.10) | copy-start | bytes 3145732
  9.4 306.1 %copy-start.24 = (f32[2048]{0:T(1024)S(1)}, f32[2048]{0:T(1024)}, u32[]{:S(2)}) copy-start(f32[2048]{0:T(1024)} %param.14) | copy-start | bytes 24580
  315.4 7.1 copy-start.31
  324.0 7.5 copy-start.20
  324.9 9.3 collective-permute-start
  332.8 2.7 copy-start.13
  332.8 2.7 copy-start.15
  332.8 2.7 copy-start.26
  335.4 9.0 copy-start.18
  351.7 6.2 copy-start.6
  351.7 6.3 copy-start.22
  358.0 52.4 %copy-start.4 = (f32[256,2048]{1,0:T(8,128)}, f32[256,2048]{1,0:T(8,128)S(1)}, u32[]{:S(2)}) copy-start(f32[256,2048]{1,0:T(8,128)S(1)} %get-tuple-element.59) | copy-start | bytes 6291460
  358.0 23.9 %copy-start.8 = (bf16[1,256,2048]{2,1,0:T(8,128)(2,1)S(1)}, bf16[1,256,2048]{2,1,0:T(8,128)(2,1)}, u32[]{:S(2)}) copy-start(bf16[1,256,2048]{2,1,0:T(8,128)(2,1)} %param.11) | copy-start | bytes 3145732
  432.0 3.2 copy-start.7
  435.2 5.7 copy-start.2
  440.8 207.4 %reduce-scatter.3.cloned.1.call-start = ((), (), s32[]{:S(2)}) async-start(), calls=%async_computation.2 | async-start | bytes 11796480 | tf_op jit(solution)/shard_map/reduce_scatter | solution.py:528
  458.0 12.0 %copy-start.14 = (bf16[256,32,32]{0,2,1:T(8,128)(2,1)S(1)}, bf16[256,32,32]{0,2,1:T(8,128)(2,1)}, u32[]{:S(2)}) copy-start(bf16[256,32,32]{0,2,1:T(8,128)(2,1)} %get-tuple-element.33) | copy-start | bytes 1572868
  458.0 12.0 %copy-start.16 = (bf16[256,32,32]{0,2,1:T(8,128)(2,1)S(1)}, bf16[256,32,32]{0,2,1:T(8,128)(2,1)}, u32[]{:S(2)}) copy-start(bf16[256,32,32]{0,2,1:T(8,128)(2,1)} %get-tuple-element.34) | copy-start | bytes 1572868
  472.7 9.2 copy-start.19
  480.1 3.4 copy-start.21
  480.1 3.4 copy-start.23
  480.1 8.3 collective-permute-start.1
  483.9 4.7 copy-start.1
  483.9 4.7 copy-start.25
  483.9 4.7 copy-start.28
  484.0 4.6 copy-start.10
  495.3 1.6 copy-start.5
  495.3 619.1 %all-reduce.3.cloned.1.call-start = ((), (), s32[]{:S(2)}) async-start(), calls=%async_computation.4 | async-start | bytes 4718592 | tf_op jit(solution)/shard_map/psum | solution.py:529
  530.9 117.4 %copy-start.9 = (bf16[1,256,2048]{2,1,0:T(8,128)(2,1)S(1)}, bf16[1,256,2048]{2,1,0:T(8,128)(2,1)}, u32[]{:S(2)}) copy-start(bf16[1,256,2048]{2,1,0:T(8,128)(2,1)} %param.11) | copy-start | bytes 3145732
  828.6 5.2 copy-start.11
  1103.6 8.6 copy-start.29
  1103.6 9.2 copy-start.3
  1103.6 9.2 copy-start.12
  1103.6 9.2 copy-start.30
  1114.5 3.2 copy-start.17
Sparse Core Ops, SparseCore 0:
  440.9 96.5 reduce-scatter.4
  540.4 107.7 reduce-scatter.2
  651.5 94.8 all-reduce.2

commit v3 on v2

--- a/solution.py
+++ b/solution.py
@@ -371,7 +371,7 @@
     return out, small_out
 
 
-def gather_kernel(chips, bits, units, weights, *refs):
+def gather_kernel(chips, bits, units, weights, ahead, *refs):
     shards, wholes = refs[:weights], refs[weights : 2 * weights]
     held = refs[2 * weights : 3 * weights]
     (in_sem, own_sem, along_out, along_in, spread_out, spread_in, turn_out, turn_in) = refs[3 * weights :]
@@ -473,32 +473,35 @@
 
     for which in range(weights):
         load(which).start()
-    stages = [begin, arrive]
+    stages = [arrive]
     for size in range(1, bits + 1):
         stages.append(lambda unit, size=size: pass_on(unit, size))
     stages.append(finish)
-    begin(0)
-    for now in range(len(units) + len(stages) - 2):
+    for unit in range(min(ahead, len(units))):
+        begin(unit)
+    for now in range(len(units) + len(stages) - 1):
+        if now + ahead < len(units):
+            begin(now + ahead)
         for number, stage in enumerate(stages):
-            unit = now - number + 1
-            if 0 <= unit < len(units) and not (number == 0 and unit == 0):
+            unit = now - number
+            if 0 <= unit < len(units):
                 stage(unit)
         if now < weights:
             load(now).wait()
             store(now).start()
     for which in range(weights):
-        if which >= len(units) + len(stages) - 2:
+        if which >= len(units) + len(stages) - 1:
             load(which).wait()
             store(which).start()
     for which in range(weights):
         store(which).wait()
 
 
-def gathered(shards, chips, bits, units):
+def gathered(shards, chips, bits, units, ahead):
     weights, seq, count = len(shards), 1 << bits, len(units)
     dma = pltpu.SemaphoreType.DMA
     return pl.pallas_call(
-        functools.partial(gather_kernel, chips, bits, units, weights),
+        functools.partial(gather_kernel, chips, bits, units, weights, ahead),
         out_shape=tuple(jax.ShapeDtypeStruct((2 * chips * one.shape[0], one.shape[1]), one.dtype) for one in shards),
         in_specs=[pl.BlockSpec(memory_space=pl.ANY)] * weights,
         out_specs=tuple(pl.BlockSpec(memory_space=pl.ANY) for _ in shards),
@@ -524,9 +527,8 @@
     return tuple((which, i * (width // count), width // count) for i in range(count))
 
 
-def sum_rows(terms):
-    mine = lax.psum_scatter(terms, "batch", scatter_dimension=0, tiled=True)
-    return lax.psum(mine, "seq").astype(F32)
+def scatter_rows(terms):
+    return lax.psum_scatter(terms, "batch", scatter_dimension=0, tiled=True)
 
 
 def local(
@@ -556,9 +558,9 @@
     ff_width = gate_up_weight.shape[1] // 2
 
     shards = (qkv_weight, out_weight, gate_up_weight, down_weight)
-    cuts = (1, 1, 8, max(1, min(4, model_width // (seq * 128))))
+    cuts = (2, 2, 8, max(1, min(4, model_width // (seq * 128))))
     units = sum((parts_of(i, one.shape[1], n) for i, (one, n) in enumerate(zip(shards, cuts))), ())
-    qkv_whole, out_whole, gate_up_whole, down_whole = gathered(shards, chips, bits, units)
+    qkv_whole, out_whole, gate_up_whole, down_whole = gathered(shards, chips, bits, units, 3)
 
     inputs = tokens[0].astype(F32)
     normed, inv_first = rms_parts(inputs, attn_gain)
@@ -613,7 +615,11 @@
 
     grad_out = cotangent[0].astype(F32)
     grad_down = cotangent[0]
-    down_terms = dot_tn(hidden_low, grad_down).astype(BF16)
+    early = model_width * 4 // 8
+    early_terms = dot_tn(hidden_low, grad_down[:, :early]).astype(BF16)
+    early_terms, grad_down = lax.optimization_barrier((early_terms, grad_down))
+    down_early = scatter_rows(early_terms)
+    down_terms = dot_tn(hidden_low, grad_down[:, early:]).astype(BF16)
     grad_hidden = dot_nt(grad_down, down_whole)
     grad_gate = grad_hidden * up_part * sigmoid_gate * (1.0 + gate_part * (1.0 - sigmoid_gate))
     grad_up = grad_hidden * gate_part * sigmoid_gate
@@ -623,7 +629,7 @@
     mlp_term = jnp.sum(grad_normed_mlp * residual * inv_second, axis=0)
     grad_resid = grad_out + norm_back(grad_normed_mlp, residual, inv_second, mlp_gain)
     grad_proj = grad_resid.astype(BF16)
-    out_grad = sum_rows(dot_tn(attended, grad_proj).astype(BF16))
+    out_part = scatter_rows(dot_tn(attended, grad_proj).astype(BF16))
     grad_heads = dot_nt(grad_proj, out_whole)
     grad_heads = grad_heads.astype(BF16).reshape(rows, KV, share, HD)
 
@@ -655,23 +661,29 @@
         ],
         axis=1,
     ).astype(BF16)
-    qkv_grad = sum_rows(dot_tn(normed_low, grad_qkv).astype(BF16))
+    qkv_terms, down_early = lax.optimization_barrier((dot_tn(normed_low, grad_qkv).astype(BF16), down_early))
+    qkv_part = scatter_rows(qkv_terms)
     grad_normed = dot_nt(grad_qkv, qkv_whole)
     attn_term = jnp.sum(grad_normed * inputs * inv_first, axis=0)
     tokens_grad = (grad_resid + norm_back(grad_normed, inputs, inv_first, attn_gain)).astype(BF16)
     gains = jnp.concatenate([attn_term, mlp_term]).reshape(-1, 128)
     gate_up_grad, gains = reduced(gate_up_terms, gains, chips, bits, 11, 0)
     gains = gains.reshape(-1)
+    gate_up_grad, down_early, out_part, qkv_part, down_terms = lax.optimization_barrier(
+        (gate_up_grad, down_early, out_part, qkv_part, down_terms)
+    )
     if down_weight.shape[0] // seq % 16 == 0:
-        down_grad, _ = reduced(down_terms, jnp.zeros((8, 128), F32), chips, bits, 8, 2)
+        down_late, _ = reduced(down_terms, jnp.zeros((8, 128), F32), chips, bits, 4, 2)
     else:
-        down_grad = sum_rows(down_terms)
+        down_late = lax.psum(scatter_rows(down_terms), "seq")
+    down_early, out_grad, qkv_grad = lax.psum((down_early, out_part, qkv_part), "seq")
+    down_grad = jnp.concatenate([down_early, down_late], axis=1)
     return (
         output[None],
         tokens_grad[None],
         gains[:model_width],
-        qkv_grad,
-        out_grad,
+        qkv_grad.astype(F32),
+        out_grad.astype(F32),
         gains[model_width:],
         gate_up_grad.astype(F32),
         down_grad.astype(F32),

time: 1130 us -> 994 us (0.88)
  waiting for transfers between devices: 123 us -> 17.2 us
  Pallas kernels: 733 us -> 702 us
    reduce_scatter x2 -> x3, waiting for transfers between devices: 117 us -> 12.7 us  [scatter_rows(): return lax.psum_scatter(terms, 'batch', scatter_dimension=0, tiled=True)]
    pallas_call x2, Pallas kernels: 427 us -> 393 us  [reduced(): pl.pallas_call(functools.partial(reduce_kernel, chips, bits, count), out_...]
    dot_general x4 -> x5, matrix products: 46.6 us -> 47.1 us  [dot_tn(): lax.dot_general(left, right, (((0,), (0,)), ((), ())), preferred_element_...]
  transfers between devices with their start and end apart: 5 -> 6, of which waited for: 4 -> 2; matrix products, arithmetic and copies ran while one was open for 11% -> 17% of each run, Pallas kernels for 38% -> 40%
where the time goes in v3:
time: 994 us; the launch traced here: 988 us
  Pallas kernels  702 us (71%)
  matrix products  192 us (19%)
  other arithmetic  44.6 us (4%)
  waiting for transfers between devices  17.2 us (2%)
  between operations  14.9 us (1%)
  local copies, waits for them, and re-layouts  12.8 us (1%)
    pallas_call x2, Pallas kernels, reduced(): pl.pallas_call(functools.partial(reduce_kernel, chips, bits, count), out_...  393 us
    pallas_call x1, Pallas kernels, gathered(): pl.pallas_call(functools.partial(gather_kernel, chips, bits, units, weigh...  309 us
    dot_general x4, matrix products, dot_nt(): lax.dot_general(left, right, (((1,), (1,)), ((), ())), preferred_element_...  55.8 us
    dot_general x4, matrix products, dot(): return jnp.dot(left, right, preferred_element_type=F32)  50.2 us
    dot_general x5, matrix products, dot_tn(): lax.dot_general(left, right, (((0,), (0,)), ((), ())), preferred_element_...  47.1 us
  transfers between devices with their start and end apart: 6, of which 2 were waited for; matrix products, arithmetic and copies ran while one was open for 17% of the time, Pallas kernels for 40%

profile of v3, /device:TPU:0, one launch (start us, length us, event | category | flops | bytes accessed | tf_op | source)
XLA Modules:
  0.0 988.1 jit_solution(1019542354462680962)
XLA Ops:
  7.2 1.5 fusion.15
  8.7 0.6 multiply_multiply_fusion
  9.3 309.4 %shard_map.161 = (bf16[2048,2560]{1,0:T(8,128)(2,1)}, bf16[2048,2048]{1,0:T(8,128)(2,1)}, bf16[2048,11264]{1,0:T(8,128)(2,1)}, bf16[5632,2048]{1,0:T(8,128)(2,1)}) custom-call(bf16[256,2560]{1,0:T(8,128)(2,1)} %refs_0_.1, bf16[256,2048]{1,0:T(8,128)(2,1)} %refs_1_.1, bf16[256,11264]{1,0:T(8,128)(2,1)} %refs_2_.1, bf16[704,2048]{1,0:T(8,128)(2,1)} %refs_3_.1), custom_call_target="tpu_custom_call" | custom-call | bytes 900000000 | tf_op jit(solution)/shard_map/pallas_call | solution.py:503
  318.8 6.9 convolution_convert_fusion.5
  325.8 0.7 constant_dynamic-slice_fusion
  326.5 0.8 fusion.44
  327.5 2.3 collective-permute-start
  329.9 1.6 slice_convert_fusion
  331.4 3.4 copy.38
  335.0 1.9 subtract_convert_fusion.1
  337.3 8.6 fusion.58
  346.0 7.4 fusion.27
  353.3 6.2 multiply_reduce_fusion.2
  359.6 23.9 %fusion.56 = f32[256,11264]{1,0:T(8,128)} fusion(bf16[2048,11264]{1,0:T(8,128)(2,1)} %get-tuple-element.26, f32[256,2048]{1,0:T(8,128)S(1)} %get-tuple-element.77, f32[2048]{0:T(1024)S(1)} %copy-done.28, f32[256]{0:T(256)S(1)} %get-tuple-element.71), kind=kOutput, calls=%fused_computation.120 | convolution fusion | flops 11812732928 | bytes 59778048 | tf_op jit(solution)/shard_map/dot_general | solution.py:50
  383.5 5.2 multiply_convert_fusion.2
  388.8 5.9 convolution_convert_fusion.3
  394.9 17.7 %multiply_convert_fusion.1 = (bf16[256,5632]{1,0:T(8,128)(2,1)}, bf16[256,5632]{1,0:T(8,128)(2,1)}) fusion(f32[256,11264]{1,0:T(8,128)} %fusion.56, bf16[256,2048]{1,0:T(8,128)(2,1)} %bitcast.117, bf16[5632,2048]{1,0:T(8,128)(2,1)} %get-tuple-element.27), kind=kOutput, calls=%fused_computation.20 | convolution fusion | flops 5924323328 | bytes 41418752 | tf_op jit(solution)/shard_map/dot_general | solution.py:54
  412.6 22.1 %multiply_reduce_fusion = (f32[2048]{0:T(1024)S(1)}, f32[256]{0:T(256)S(1)}, f32[256,2048]{1,0:T(8,128)}) fusion(f32[256,2048]{1,0:T(8,128)} %copy-done.6, f32[256]{0:T(256)S(1)} %get-tuple-element.71, f32[2048]{0:T(1024)S(1)} %copy-done.28, bf16[2048,11264]{1,0:T(8,128)(2,1)} %get-tuple-element.26, bf16[256,5632]{1,0:T(8,128)(2,1)} %get-tuple-element.48, ...), kind=kOutput, calls=%fused_computation.50 | convolution fusion | flops 11825838080 | bytes 56117248 | tf_op jit(solution)/shard_map/dot_general | solution.py:54
  434.7 3.2 subtract_add_fusion
  437.9 1.3 copy-done.7
  439.3 5.5 convolution_convert_fusion.4
  445.1 7.5 convolution_convert_fusion.6
  452.6 2.3 copy.40
  454.8 11.4 %fusion.1 = (f32[4,8,256]{2,1,0:T(8,128)S(1)}, f32[4,512,256,8]{2,1,3,0:T(8,128)}) fusion(f32[4,8,256,512]{2,3,1,0:T(8,128)} %get-tuple-element.75, f32[4,8,256]{2,1,0:T(8,128)S(1)} %get-tuple-element.74, bf16[512,4,64,1]{0,2,3,1:T(8,128)(2,1)S(1)} %bitcast.138, bf16[256,4,8,64]{0,3,2,1:T(8,128)(2,1)} %bitcast.130), kind=kOutput, calls=%fused_computation.4 | convolution fusion | flops 549445632 | bytes 34930688 | tf_op jit(solution)/shard_map/qgsd,kgd->gsqk/dot_general | solution.py:636
  466.2 12.0 %fusion.3 = bf16[4,8,256,512]{2,3,1,0:T(8,128)(2,1)S(1)} fusion(f32[4,512,256,8]{2,1,3,0:T(8,128)} %get-tuple-element.80, f32[4,8,256]{2,1,0:T(8,128)S(1)} %get-tuple-element.79, f32[4,8,256,512]{2,3,1,0:T(8,128)} %get-tuple-element.75, f32[4,8,256]{2,1,0:T(8,128)S(1)} %get-tuple-element.74), kind=kLoop, calls=%fused_computation.6 | loop fusion | flops 16777216 | bytes 42008576 | tf_op jit(solution)/shard_map/convert_element_type | solution.py:638
  478.2 2.6 fusion.30
  480.9 7.4 fusion.8
  488.4 1.6 collective-permute-start.1
  490.0 1.6 convolution_multiply_fusion
  492.1 4.4 collective-permute-done.1
  496.8 6.8 convolution_convert_fusion.1
  503.5 12.6 %reduce-scatter.4.cloned.1.call-done = bf16[704,1024]{1,0:T(8,128)(2,1)} async-done(((bf16[5632,1024]{1,0:T(8,128)(2,1)}), bf16[704,1024]{1,0:T(8,128)(2,1)}) %reduce-scatter.4.cloned.1.call-update) | async-done | bytes 1441808 | tf_op jit(solution)/shard_map/reduce_scatter | solution.py:531
  516.5 7.2 convolution_convert_fusion.2
  523.7 21.7 %convolution_convert_fusion = bf16[2048,11264]{1,0:T(8,128)(2,1)} fusion(bf16[256,5632]{1,0:T(8,128)(2,1)} %get-tuple-element.48, bf16[256,5632]{1,0:T(8,128)(2,1)} %get-tuple-element.47, f32[256,2048]{1,0:T(8,128)} %copy-done.6, f32[2048]{0:T(1024)S(1)} %copy-done.28, f32[256]{0:T(256)S(1)} %get-tuple-element.71), kind=kOutput, calls=%fused_computation.1 | convolution fusion | flops 11847335936 | bytes 54010880 | tf_op jit(solution)/shard_map/dot_general | solution.py:58
  545.4 8.5 fusion.24
  553.9 0.6 pad_maximum_fusion.20.small
  554.5 269.0 %shard_map.162 = (bf16[256,11264]{1,0:T(8,128)(2,1)}, bf16[11,4,256,1024]{3,2,1,0:T(8,128)(2,1)}, f32[32,128]{1,0:T(8,128)}) custom-call(bf16[4,2,256,11264]{3,2,1,0:T(8,128)(2,1)} %bitcast.109, f32[32,128]{1,0:T(8,128)} %pad_maximum_fusion.20.small), custom_call_target="tpu_custom_call" | custom-call | bytes 800000000 | tf_op jit(solution)/shard_map/pallas_call | solution.py:331
  823.6 1.7 copy-done.1
  825.3 13.2 %fusion.14 = bf16[1,256,2048]{2,1,0:T(8,128)(2,1)} fusion(f32[256,2048]{1,0:T(8,128)} %copy-done.6, bf16[256,5632]{1,0:T(8,128)(2,1)S(1)} %copy-done.1, bf16[5632,2048]{1,0:T(8,128)(2,1)} %get-tuple-element.27), kind=kOutput, calls=%fused_computation.39 | convolution fusion | flops 5906628608 | bytes 29097984 | tf_op jit(solution)/shard_map/dot_general | solution.py:50
  838.5 0.6 slice_bitcast_fusion
  839.2 1.6 fusion.31
  840.8 2.2 copy-done.11
  843.0 5.8 convert_element_type.136
  848.8 0.6 broadcast_in_dim.22.small
  849.4 123.6 %shard_map.163 = (bf16[704,1024]{1,0:T(8,128)(2,1)}, bf16[4,4,704,256]{3,2,1,0:T(8,128)(2,1)}, f32[8,128]{1,0:T(8,128)}) custom-call(bf16[4,2,704,1024]{3,2,1,0:T(8,128)(2,1)} %bitcast.110, f32[8,128]{1,0:T(8,128)} %broadcast_in_dim.22.small), custom_call_target="tpu_custom_call" | custom-call | bytes 800000000 | tf_op jit(solution)/shard_map/pallas_call | solution.py:331
  973.0 3.3 convert_element_type.134
  976.2 1.6 convert_element_type.135
  977.8 3.3 maximum_convert_fusion
  (107 shorter events, 2.6 us)
Async XLA Ops:
  7.2 509.0 %reduce-scatter.4.cloned.1.call-start = ((), (), s32[]{:S(2)}) async-start(), calls=%async_computation.3 | async-start | bytes 12976128 | tf_op jit(solution)/shard_map/reduce_scatter | solution.py:531
  9.3 309.4 %copy-start.32 = (f32[256]{0:T(256)}, f32[256]{0:T(256)S(1)}, u32[]{:S(2)}) copy-start(f32[256]{0:T(256)S(1)} %get-tuple-element.69) | copy-start | bytes 3076
  9.3 309.4 %copy-start.2 = (bf16[1,256,2048]{2,1,0:T(8,128)(2,1)S(1)}, bf16[1,256,2048]{2,1,0:T(8,128)(2,1)}, u32[]{:S(2)}) copy-start(bf16[1,256,2048]{2,1,0:T(8,128)(2,1)} %param.10) | copy-start | bytes 3145732
  9.3 309.4 %copy-start.30 = (f32[2048]{0:T(1024)S(1)}, f32[2048]{0:T(1024)}, u32[]{:S(2)}) copy-start(f32[2048]{0:T(1024)} %param.14) | copy-start | bytes 24580
  318.7 7.1 copy-start.36
  327.4 7.6 copy-start.26
  327.5 9.4 collective-permute-start
  336.9 9.1 copy-start.16
  336.9 9.1 copy-start.18
  337.3 8.6 copy-start.24
  353.3 6.2 copy-start.9
  353.3 6.3 copy-start.28
  359.6 23.9 %copy-start.6 = (f32[256,2048]{1,0:T(8,128)}, f32[256,2048]{1,0:T(8,128)S(1)}, u32[]{:S(2)}) copy-start(f32[256,2048]{1,0:T(8,128)S(1)} %get-tuple-element.77) | copy-start | bytes 6291460
  383.5 5.3 copy-start.12
  388.8 127.7 %copy-start = (bf16[256,5632]{1,0:T(8,128)(2,1)}, bf16[256,5632]{1,0:T(8,128)(2,1)S(1)}, u32[]{:S(2)}) copy-start(bf16[256,5632]{1,0:T(8,128)(2,1)S(1)} %multiply_convert_fusion.2) | copy-start | bytes 8650756
  394.7 428.8 %reduce-scatter.6.cloned.1.call-start = ((), (), s32[]{:S(2)}) async-start(), calls=%async_computation.4 | async-start | bytes 9437184 | tf_op jit(solution)/shard_map/reduce_scatter | solution.py:531
  434.7 4.6 copy-start.10
  437.9 1.3 copy-start.7
  444.8 378.7 %reduce-scatter.8.cloned.1.call-start = ((), (), s32[]{:S(2)}) async-start(), calls=%async_computation.5 | async-start | bytes 11796480 | tf_op jit(solution)/shard_map/reduce_scatter | solution.py:531
  466.2 12.0 %copy-start.17 = (bf16[256,32,32]{0,2,1:T(8,128)(2,1)S(1)}, bf16[256,32,32]{0,2,1:T(8,128)(2,1)}, u32[]{:S(2)}) copy-start(bf16[256,32,32]{0,2,1:T(8,128)(2,1)} %copy-done.16) | copy-start | bytes 1572868
  466.2 12.0 %copy-start.19 = (bf16[256,32,32]{0,2,1:T(8,128)(2,1)S(1)}, bf16[256,32,32]{0,2,1:T(8,128)(2,1)}, u32[]{:S(2)}) copy-start(bf16[256,32,32]{0,2,1:T(8,128)(2,1)} %copy-done.18) | copy-start | bytes 1572868
  478.2 2.6 copy-start.23
  480.9 9.2 copy-start.25
  488.3 3.2 copy-start.27
  488.3 3.2 copy-start.29
  488.4 8.2 collective-permute-start.1
  491.9 4.8 copy-start.3
  492.0 4.8 copy-start.31
  492.0 4.8 copy-start.33
  492.1 4.6 copy-start.13
  516.2 456.8 %all-reduce.3.cloned.1.call-start = ((), (), s32[]{:S(2)}) async-start(), calls=%async_computation.6 | async-start | bytes 7602176 | tf_op jit(solution)/shard_map/psum | solution.py:679
  523.7 21.7 %copy-start.4 = (bf16[1,256,2048]{2,1,0:T(8,128)(2,1)S(1)}, bf16[1,256,2048]{2,1,0:T(8,128)(2,1)}, u32[]{:S(2)}) copy-start(bf16[1,256,2048]{2,1,0:T(8,128)(2,1)} %param.10) | copy-start | bytes 3145732
  523.7 21.7 %copy-start.14 = (bf16[256,32,64]{0,2,1:T(8,128)(2,1)S(1)}, bf16[256,32,64]{0,2,1:T(8,128)(2,1)}, u32[]{:S(2)}) copy-start(bf16[256,32,64]{0,2,1:T(8,128)(2,1)} %copy-done.13) | copy-start | bytes 3145732
  823.5 1.8 copy-start.1
  825.3 13.2 %copy-start.34 = (f32[32,128]{1,0:T(8,128)S(1)}, f32[32,128]{1,0:T(8,128)}, u32[]{:S(2)}) copy-start(f32[32,128]{1,0:T(8,128)} %get-tuple-element.29) | copy-start | bytes 49156
  825.3 13.9 %copy-start.5 = (bf16[1,256,2048]{2,1,0:T(8,128)(2,1)S(1)}, bf16[1,256,2048]{2,1,0:T(8,128)(2,1)}, u32[]{:S(2)}) copy-start(bf16[1,256,2048]{2,1,0:T(8,128)(2,1)} %param.10) | copy-start | bytes 3145732
  825.3 13.9 %copy-start.8 = (f32[256,2048]{1,0:T(8,128)S(1)}, f32[256,2048]{1,0:T(8,128)}, u32[]{:S(2)}) copy-start(f32[256,2048]{1,0:T(8,128)} %copy-done.7) | copy-start | bytes 6291460
  825.3 13.9 %copy-start.15 = (f32[256,2048]{1,0:T(8,128)S(1)}, f32[256,2048]{1,0:T(8,128)}, u32[]{:S(2)}) copy-start(f32[256,2048]{1,0:T(8,128)} %get-tuple-element.81) | copy-start | bytes 6291460
  825.3 13.9 %copy-start.35 = (f32[256]{0:T(256)S(1)}, f32[256]{0:T(256)}, u32[]{:S(2)}) copy-start(f32[256]{0:T(256)} %get-tuple-element.68) | copy-start | bytes 3076
  839.2 3.8 copy-start.11
  972.9 3.3 copy-start.22
  973.0 4.8 copy-start.20
  973.0 4.8 copy-start.21
Sparse Core Ops, SparseCore 0:
  394.8 121.2 reduce-scatter.3
  518.5 93.7 reduce-scatter.5
  615.2 202.5 reduce-scatter.7
  823.7 141.0 all-reduce.2

commit v4 on v3

--- a/solution.py
+++ b/solution.py
@@ -527,6 +527,83 @@
     return tuple((which, i * (width // count), width // count) for i in range(count))
 
 
+class Plane:
+    def __init__(self):
+        self.seq = lax.axis_size("seq")
+        self.batch = lax.axis_size("batch")
+        self.chips = self.batch // 2
+        self.bits = self.seq.bit_length() - 1
+        self.core = lax.axis_index("batch") % 2
+        s = lax.axis_index("seq")
+        self.reversed = [self.reverse(i) for i in range(self.seq)]
+        self.part = jnp.where(self.core == 0, self.reverse(s), s)
+
+    def reverse(self, value):
+        return sum(((value >> bit) & 1) << (self.bits - 1 - bit) for bit in range(self.bits))
+
+    def send(self, array, target):
+        pairs = []
+        for s in range(self.seq):
+            for z in range(self.chips):
+                for core in range(2):
+                    there, to = target(core, s)
+                    pairs.append((s * self.batch + z * 2 + core, to * self.batch + z * 2 + there))
+        return lax.ppermute(array, ("seq", "batch"), pairs)
+
+    def swap_cores(self, array):
+        return self.send(array, lambda core, s: (1 - core, s))
+
+    def stage(self, array, step):
+        masks = (1 << step, 1 << (self.bits - 1 - step))
+        return self.send(array, lambda core, s: (core, s ^ masks[core]))
+
+
+class Fold:
+    def __init__(self, terms):
+        self.plane = Plane()
+        chips = self.plane.chips
+        self.rows, self.width = terms.shape[0] // (2 * chips), terms.shape[1]
+        self.terms = terms.reshape(chips, 2, self.rows, self.width)
+        self.first, self.size, self.step = 0, self.rows, 0
+        self.held = []
+        away = self.mine(1 - self.plane.core, 0, self.rows)
+        self.pending = self.plane.swap_cores(away)
+
+    def mine(self, core, first, size):
+        shape = (self.plane.chips, 1, size, self.width)
+        return lax.dynamic_slice(self.terms, (0, core, first, 0), shape)[:, 0]
+
+    def total(self, first, size):
+        shape = (self.plane.chips, size, self.width)
+        total = self.mine(self.plane.core, first, size).astype(F32)
+        for array, base in self.held:
+            total = total + lax.dynamic_slice(array, (0, first - base, 0), shape).astype(F32)
+        return total.astype(BF16)
+
+    def advance(self, *values):
+        pending, *values = lax.optimization_barrier((self.pending, *values))
+        self.held.append((pending, self.first))
+        half = self.size // 2
+        bit = (self.plane.part >> (self.plane.bits - 1 - self.step)) & 1
+        leave, *values = lax.optimization_barrier((self.total(self.first + (1 - bit) * half, half), *values))
+        self.first, self.size = self.first + bit * half, half
+        self.pending = self.plane.stage(leave, self.step)
+        self.step += 1
+        return values
+
+    def finish(self, *values):
+        while self.step < self.plane.bits:
+            values = self.advance(*values)
+        pending, *values = lax.optimization_barrier((self.pending, *values))
+        self.held.append((pending, self.first))
+        return self.total(self.first, self.size), *values
+
+    def spread(self, mine):
+        parts = lax.all_gather(mine, "seq")
+        turned = jnp.stack([parts[i] for i in self.plane.reversed])
+        return jnp.where(self.plane.core == 0, turned, parts).reshape(self.rows, self.width)
+
+
 def scatter_rows(terms):
     return lax.psum_scatter(terms, "batch", scatter_dimension=0, tiled=True)
 
@@ -615,20 +692,16 @@
 
     grad_out = cotangent[0].astype(F32)
     grad_down = cotangent[0]
-    early = model_width * 4 // 8
-    early_terms = dot_tn(hidden_low, grad_down[:, :early]).astype(BF16)
-    early_terms, grad_down = lax.optimization_barrier((early_terms, grad_down))
-    down_early = scatter_rows(early_terms)
-    down_terms = dot_tn(hidden_low, grad_down[:, early:]).astype(BF16)
+    down_terms, grad_down = lax.optimization_barrier((dot_tn(hidden_low, grad_down).astype(BF16), grad_down))
+    down_fold = Fold(down_terms)
     grad_hidden = dot_nt(grad_down, down_whole)
     grad_gate = grad_hidden * up_part * sigmoid_gate * (1.0 + gate_part * (1.0 - sigmoid_gate))
     grad_up = grad_hidden * gate_part * sigmoid_gate
     grad_gate_up = jnp.concatenate([grad_gate, grad_up], axis=1).astype(BF16)
-    gate_up_terms = dot_tn(normed_mlp_low, grad_gate_up).astype(BF16)
     grad_normed_mlp = dot_nt(grad_gate_up, gate_up_whole)
     mlp_term = jnp.sum(grad_normed_mlp * residual * inv_second, axis=0)
     grad_resid = grad_out + norm_back(grad_normed_mlp, residual, inv_second, mlp_gain)
-    grad_proj = grad_resid.astype(BF16)
+    (grad_proj,) = down_fold.advance(grad_resid.astype(BF16))
     out_part = scatter_rows(dot_tn(attended, grad_proj).astype(BF16))
     grad_heads = dot_nt(grad_proj, out_whole)
     grad_heads = grad_heads.astype(BF16).reshape(rows, KV, share, HD)
@@ -661,23 +734,26 @@
         ],
         axis=1,
     ).astype(BF16)
-    qkv_terms, down_early = lax.optimization_barrier((dot_tn(normed_low, grad_qkv).astype(BF16), down_early))
-    qkv_part = scatter_rows(qkv_terms)
+    if down_fold.step < bits:
+        (grad_qkv,) = down_fold.advance(grad_qkv)
+    qkv_part = scatter_rows(dot_tn(normed_low, grad_qkv).astype(BF16))
     grad_normed = dot_nt(grad_qkv, qkv_whole)
     attn_term = jnp.sum(grad_normed * inputs * inv_first, axis=0)
     tokens_grad = (grad_resid + norm_back(grad_normed, inputs, inv_first, attn_gain)).astype(BF16)
     gains = jnp.concatenate([attn_term, mlp_term]).reshape(-1, 128)
+    normed_mlp_low, gains = lax.optimization_barrier((normed_mlp_low, gains))
+    gate_up_terms = dot_tn(normed_mlp_low, grad_gate_up).astype(BF16)
+    out_grad = lax.psum(out_part, "seq")
+    down_part, gate_up_terms = down_fold.finish(gate_up_terms)
+    groups = [list(range(core, 2 * chips, 2)) for core in range(2)]
+    down_part = lax.psum_scatter(down_part, "batch", scatter_dimension=0, axis_index_groups=groups)
     gate_up_grad, gains = reduced(gate_up_terms, gains, chips, bits, 11, 0)
     gains = gains.reshape(-1)
-    gate_up_grad, down_early, out_part, qkv_part, down_terms = lax.optimization_barrier(
-        (gate_up_grad, down_early, out_part, qkv_part, down_terms)
-    )
-    if down_weight.shape[0] // seq % 16 == 0:
-        down_late, _ = reduced(down_terms, jnp.zeros((8, 128), F32), chips, bits, 4, 2)
-    else:
-        down_late = lax.psum(scatter_rows(down_terms), "seq")
-    down_early, out_grad, qkv_grad = lax.psum((down_early, out_part, qkv_part), "seq")
-    down_grad = jnp.concatenate([down_early, down_late], axis=1)
+    gate_up_grad, out_grad, qkv_part, down_part = lax.optimization_barrier(
+        (gate_up_grad, out_grad, qkv_part, down_part)
+    )
+    qkv_grad = lax.psum(qkv_part, "seq")
+    down_grad = down_fold.spread(down_part)
     return (
         output[None],
         tokens_grad[None],

time: 994 us -> 1050 us (1.056)
  waiting for transfers between devices: 17.2 us -> 136 us
  Pallas kernels: 702 us -> 602 us
  other arithmetic: 44.6 us -> 75.8 us
    pallas_call x2 -> x1, Pallas kernels: 393 us -> 293 us  [reduced(): pl.pallas_call(functools.partial(reduce_kernel, chips, bits, count), out_...]
    psum x1 -> x2, waiting for transfers between devices: 0.02 us -> 45.5 us  [the longest x1 45.5 us: local(): qkv_grad = lax.psum(qkv_part, 'seq')]
    all_gather x0 -> x1, waiting for transfers between devices: none -> 40.3 us  [spread(): parts = lax.all_gather(mine, 'seq')]
    convert_element_type x0 -> x5, other arithmetic: none -> 30.9 us  [the longest x3 26.6 us: total(): return total.astype(BF16)]
    ppermute x1, waiting for transfers between devices: 4.44 us -> 32.3 us  [local(): arrived = lax.ppermute(away, 'seq', swap)]
    dot_general x5 -> x4, matrix products: 47.1 us -> 43.9 us  [dot_tn(): lax.dot_general(left, right, (((0,), (0,)), ((), ())), preferred_element_...]
  transfers between devices with their start and end apart: 6 -> 11, of which waited for: 2 -> 6; matrix products, arithmetic and copies ran while one was open for 17% -> 17% of each run, Pallas kernels for 40% -> 28%
where the time goes in v4:
time: 1050 us
  Pallas kernels  602 us (57%)
  matrix products  191 us (18%)
  waiting for transfers between devices  136 us (13%)
  other arithmetic  75.8 us (7%)
  local copies, waits for them, and re-layouts  20 us (2%)
  between operations  15.1 us (1%)
    pallas_call x1, Pallas kernels, gathered(): pl.pallas_call(functools.partial(gather_kernel, chips, bits, units, weigh...  309 us
    pallas_call x1, Pallas kernels, reduced(): pl.pallas_call(functools.partial(reduce_kernel, chips, bits, count), out_...  293 us
    dot_general x4, matrix products, dot_nt(): lax.dot_general(left, right, (((1,), (1,)), ((), ())), preferred_element_...  58.7 us
    dot_general x4, matrix products, dot(): return jnp.dot(left, right, preferred_element_type=F32)  49.8 us
    psum x1, waiting for transfers between devices, local(): qkv_grad = lax.psum(qkv_part, 'seq')  45.5 us
    dot_general x4, matrix products, dot_tn(): lax.dot_general(left, right, (((0,), (0,)), ((), ())), preferred_element_...  43.9 us
    all_gather x1, waiting for transfers between devices, spread(): parts = lax.all_gather(mine, 'seq')  40.3 us
    ppermute x1, waiting for transfers between devices, local(): arrived = lax.ppermute(away, 'seq', swap)  32.3 us
  transfers between devices with their start and end apart: 11, of which 6 were waited for; matrix products, arithmetic and copies ran while one was open for 17% of the time, Pallas kernels for 28%

profile of v4, /device:TPU:0, one launch (start us, length us, event | category | flops | bytes accessed | tf_op | source)
XLA Modules:
  0.0 1045.8 jit_solution(12873069015173655708)
XLA Ops:
  7.2 1.5 fusion.21
  9.3 309.3 %shard_map.161 = (bf16[2048,2560]{1,0:T(8,128)(2,1)}, bf16[2048,2048]{1,0:T(8,128)(2,1)}, bf16[2048,11264]{1,0:T(8,128)(2,1)}, bf16[5632,2048]{1,0:T(8,128)(2,1)}) custom-call(bf16[256,2560]{1,0:T(8,128)(2,1)} %refs_0_.1, bf16[256,2048]{1,0:T(8,128)(2,1)} %refs_1_.1, bf16[256,11264]{1,0:T(8,128)(2,1)} %refs_2_.1, bf16[704,2048]{1,0:T(8,128)(2,1)} %refs_3_.1), custom_call_target="tpu_custom_call" | custom-call | bytes 900000000 | tf_op jit(solution)/shard_map/pallas_call | solution.py:503
  318.7 6.9 convolution_convert_fusion.4
  326.5 0.8 fusion.45
  327.5 2.3 collective-permute-start
  329.8 1.6 slice_convert_fusion
  331.4 3.0 copy.40
  334.6 1.9 subtract_convert_fusion.1
  337.1 8.7 fusion.59
  345.8 7.4 fusion.33
  353.2 6.2 multiply_reduce_fusion.2
  359.4 1.3 copy-done.2
  361.0 23.4 %fusion.60 = f32[256,11264]{1,0:T(8,128)} fusion(bf16[256,2048]{1,0:T(8,128)(2,1)S(1)} %multiply_convert_fusion.3, bf16[2048,11264]{1,0:T(8,128)(2,1)} %get-tuple-element.34), kind=kOutput, calls=%fused_computation.132 | convolution fusion | flops 11811160064 | bytes 58720256 | tf_op jit(solution)/shard_map/dot_general | solution.py:50
  384.4 5.2 multiply_convert_fusion.2
  389.7 11.1 %convolution_convert_fusion.1 = bf16[5632,2048]{1,0:T(8,128)(2,1)} fusion(bf16[256,5632]{1,0:T(8,128)(2,1)S(1)} %multiply_convert_fusion.2, bf16[1,256,2048]{2,1,0:T(8,128)(2,1)S(1)} %copy-done.10), kind=kOutput, calls=%fused_computation.2 | convolution fusion | flops 5917114368 | bytes 27000832 | tf_op jit(solution)/shard_map/dot_general | solution.py:58
  400.8 10.2 dynamic-slice_bitcast_fusion
  411.0 25.0 %multiply_convert_fusion.1 = (bf16[256,5632]{1,0:T(8,128)(2,1)}, bf16[256,5632]{1,0:T(8,128)(2,1)}) fusion(f32[256,11264]{1,0:T(8,128)} %fusion.60, bf16[256,2048]{1,0:T(8,128)(2,1)S(1)} %bitcast.161, bf16[5632,2048]{1,0:T(8,128)(2,1)} %get-tuple-element.35), kind=kOutput, calls=%fused_computation.29 | convolution fusion | flops 5924323328 | bytes 41418752 | tf_op jit(solution)/shard_map/dot_general | solution.py:54
  436.0 21.9 %multiply_reduce_fusion = (f32[2048]{0:T(1024)S(1)}, f32[256]{0:T(256)S(1)}, f32[256,2048]{1,0:T(8,128)}) fusion(f32[256,2048]{1,0:T(8,128)S(1)} %copy-done.3, f32[256]{0:T(256)S(1)} %get-tuple-element.90, f32[2048]{0:T(1024)S(1)} %copy-done.27, bf16[2048,11264]{1,0:T(8,128)(2,1)} %get-tuple-element.34, bf16[256,5632]{1,0:T(8,128)(2,1)} %get-tuple-element.63, ...), kind=kOutput, calls=%fused_computation.60 | convolution fusion | flops 11825838080 | bytes 56117248 | tf_op jit(solution)/shard_map/dot_general | solution.py:54
  457.9 4.1 fusion.57
  462.0 10.4 fusion.5
  472.4 3.4 convolution_convert_fusion.5
  475.7 5.7 convolution_convert_fusion.3
  481.5 1.7 collective-permute-start.2
  483.2 1.5 copy.44
  484.8 11.0 %fusion.1 = (f32[4,8,256]{2,1,0:T(8,128)S(1)}, f32[4,512,256,8]{2,1,3,0:T(8,128)}) fusion(f32[4,8,256,512]{2,3,1,0:T(8,128)} %get-tuple-element.94, f32[4,8,256]{2,1,0:T(8,128)S(1)} %copy-done.26, bf16[512,4,64,1]{0,2,3,1:T(8,128)(2,1)S(1)} %bitcast.178, bf16[256,4,8,64]{0,3,2,1:T(8,128)(2,1)S(1)} %bitcast.170), kind=kOutput, calls=%fused_computation.5 | convolution fusion | flops 549445632 | bytes 34930688 | tf_op jit(solution)/shard_map/qgsd,kgd->gsqk/dot_general | solution.py:709
  495.8 12.1 %fusion.3 = bf16[4,8,256,512]{2,3,1,0:T(8,128)(2,1)S(1)} fusion(f32[4,512,256,8]{2,1,3,0:T(8,128)} %get-tuple-element.99, f32[4,8,256]{2,1,0:T(8,128)S(1)} %get-tuple-element.98, f32[4,8,256,512]{2,3,1,0:T(8,128)} %get-tuple-element.94, f32[4,8,256]{2,1,0:T(8,128)S(1)} %copy-done.26), kind=kLoop, calls=%fused_computation.7 | loop fusion | flops 16777216 | bytes 42008576 | tf_op jit(solution)/shard_map/convert_element_type | solution.py:711
  507.9 2.6 fusion.36
  510.6 7.4 fusion.14
  518.3 1.6 convolution_multiply_fusion
  520.3 32.3 %collective-permute-done.3 = bf16[256,512]{0,1:T(8,128)(2,1)S(1)} collective-permute-done((bf16[256,512]{0,1:T(8,128)(2,1)S(1)}, bf16[256,512]{0,1:T(8,128)(2,1)S(1)}, u32[]{:S(2)}, u32[]{:S(2)}) %collective-permute-start.3) | collective-permute-done | bytes 262176 | tf_op jit(solution)/shard_map/ppermute | solution.py:725
  553.0 7.4 fusion.13
  560.4 1.2 collective-permute-start.4
  561.7 8.5 fusion.30
  570.7 21.3 %convolution_convert_fusion = bf16[2048,11264]{1,0:T(8,128)(2,1)} fusion(bf16[256,2048]{1,0:T(8,128)(2,1)} %copy-done.9, bf16[256,5632]{1,0:T(8,128)(2,1)} %get-tuple-element.63, bf16[256,5632]{1,0:T(8,128)(2,1)} %get-tuple-element.62), kind=kOutput, calls=%fused_computation.1 | convolution fusion | flops 11845763072 | bytes 52953088 | tf_op jit(solution)/shard_map/dot_general | solution.py:58
  592.0 3.1 collective-permute-done.4
  595.2 8.8 fusion.11
  604.8 5.8 convolution_convert_fusion.2
  610.7 292.8 %shard_map.162 = (bf16[256,11264]{1,0:T(8,128)(2,1)}, bf16[11,4,256,1024]{3,2,1,0:T(8,128)(2,1)}, f32[32,128]{1,0:T(8,128)}) custom-call(bf16[4,2,256,11264]{3,2,1,0:T(8,128)(2,1)} %bitcast.146, f32[32,128]{1,0:T(8,128)} %pad_maximum_fusion.18.small), custom_call_target="tpu_custom_call" | custom-call | bytes 800000000 | tf_op jit(solution)/shard_map/pallas_call | solution.py:331
  903.6 13.2 %reduce-scatter.6.cloned.1.call-done = bf16[256,2560]{1,0:T(8,128)(2,1)} async-done(((bf16[2048,2560]{1,0:T(8,128)(2,1)}), bf16[256,2560]{1,0:T(8,128)(2,1)}) %reduce-scatter.6.cloned.1.call-update) | async-done | bytes 1310736 | tf_op jit(solution)/shard_map/reduce_scatter | solution.py:608
  917.4 13.3 %fusion.20 = bf16[1,256,2048]{2,1,0:T(8,128)(2,1)} fusion(f32[256,2048]{1,0:T(8,128)} %copy-done.2, bf16[256,5632]{1,0:T(8,128)(2,1)} %copy-done.4, bf16[5632,2048]{1,0:T(8,128)(2,1)} %get-tuple-element.35), kind=kOutput, calls=%fused_computation.49 | convolution fusion | flops 5906628608 | bytes 29097984 | tf_op jit(solution)/shard_map/dot_general | solution.py:50
  930.7 1.6 fusion.37
  932.9 1.6 convert_element_type.194
  934.5 8.4 convert_element_type.195
  942.9 45.5 %all-reduce.5.cloned.1.call-done = bf16[256,2560]{1,0:T(8,128)(2,1)} async-done(((bf16[256,2560]{1,0:T(8,128)(2,1)}), bf16[256,2560]{1,0:T(8,128)(2,1)}) %all-reduce.5.cloned.1.call-update) | async-done | bytes 1310736 | tf_op jit(solution)/shard_map/psum | solution.py:755
  988.4 3.1 convert_element_type.193
  991.5 40.3 %all-gather.3.cloned.1.call-done = bf16[704,2048]{1,0:T(8,128)(2,1)} async-done(((bf16[176,2048]{1,0:T(8,128)(2,1)}), bf16[704,2048]{1,0:T(8,128)(2,1)}) %all-gather.3.cloned.1.call-update) | async-done | bytes 2883600 | tf_op jit(solution)/shard_map/all_gather | solution.py:602
  1031.8 2.1 slice_bitcast_fusion.3
  1035.1 3.5 bitcast_convert_fusion
  (121 shorter events, 7.6 us)
Async XLA Ops:
  7.2 597.0 %reduce-scatter.4.cloned.1.call-start = ((), (), s32[]{:S(2)}) async-start(), calls=%async_computation.3 | async-start | bytes 9437184 | tf_op jit(solution)/shard_map/reduce_scatter | solution.py:608
  8.7 309.9 %copy-start = (bf16[1,256,2048]{2,1,0:T(8,128)(2,1)S(1)}, bf16[1,256,2048]{2,1,0:T(8,128)(2,1)}, u32[]{:S(2)}) copy-start(bf16[1,256,2048]{2,1,0:T(8,128)(2,1)} %param.10) | copy-start | bytes 3145732
  8.8 309.9 %copy-start.23 = (f32[2048]{0:T(1024)S(1)}, f32[2048]{0:T(1024)}, u32[]{:S(2)}) copy-start(f32[2048]{0:T(1024)} %param.14) | copy-start | bytes 24580
  9.3 316.3 %copy-start.28 = (f32[256]{0:T(256)}, f32[256]{0:T(256)S(1)}, u32[]{:S(2)}) copy-start(f32[256]{0:T(256)S(1)} %get-tuple-element.88) | copy-start | bytes 3076
  318.7 7.1 copy-start.32
  327.3 9.2 copy-start.20
  327.5 9.2 collective-permute-start
  336.5 9.3 copy-start.13
  336.5 9.3 copy-start.15
  337.0 8.7 copy-start.18
  345.8 7.4 copy-start.25
  353.2 6.2 copy-start.7
  353.2 7.6 copy-start.27
  359.4 1.3 copy-start.2
  361.0 23.4 %copy-start.9 = (bf16[256,2048]{1,0:T(8,128)(2,1)}, bf16[256,2048]{1,0:T(8,128)(2,1)S(1)}, u32[]{:S(2)}) copy-start(bf16[256,2048]{1,0:T(8,128)(2,1)S(1)} %multiply_convert_fusion.3) | copy-start | bytes 3145732
  384.4 5.3 copy-start.10
  389.7 11.1 %copy-start.4 = (bf16[256,5632]{1,0:T(8,128)(2,1)}, bf16[256,5632]{1,0:T(8,128)(2,1)S(1)}, u32[]{:S(2)}) copy-start(bf16[256,5632]{1,0:T(8,128)(2,1)S(1)} %multiply_convert_fusion.2) | copy-start | bytes 8650756
  411.0 51.0 %collective-permute-start.1 = (bf16[4,704,2048]{2,1,0:T(8,128)(2,1)}, bf16[4,704,2048]{2,1,0:T(8,128)(2,1)}, u32[]{:S(2)}, u32[]{:S(2)}) collective-permute-start(bf16[4,704,2048]{2,1,0:T(8,128)(2,1)} %dynamic-slice_bitcast_fusion), channel_id=1, source_target_pairs={{0,1},{1,0},{2,3},{3,2},{4,5},{5,4},{6,7},{7,6},{8,9},{9,8},{10,11... | collective-permute-start | bytes 34603016 | tf_op jit(solution)/shard_map/ppermute | solution.py:551
  411.0 25.0 %copy-start.3 = (f32[256,2048]{1,0:T(8,128)S(1)}, f32[256,2048]{1,0:T(8,128)}, u32[]{:S(2)}) copy-start(f32[256,2048]{1,0:T(8,128)} %copy-done.2) | copy-start | bytes 6291460
  457.9 14.5 %slice-start = ((s8[8388608]{0:T(1024)(128)(4,1)}), s8[4194304]{0:T(1024)(128)(4,1)S(1)}, s32[]{:S(2)}) async-start(s8[8388608]{0:T(1024)(128)(4,1)} %bitcast.151), calls=%async_computation.9 | async-start | bytes 8388608
  461.9 10.4 slice-start.1
  461.9 10.4 copy-start.11
  472.3 3.4 copy-start.8
  481.5 3.3 copy-start.26
  481.5 71.5 %collective-permute-start.2 = (bf16[4,352,2048]{2,1,0:T(8,128)(2,1)}, bf16[4,352,2048]{2,1,0:T(8,128)(2,1)}, u32[]{:S(2)}, u32[]{:S(2)}) collective-permute-start(bf16[4,352,2048]{2,1,0:T(8,128)(2,1)} %fusion.5), channel_id=1, source_target_pairs={{0,8},{1,17},{2,10},{3,19},{4,12},{5,21},{6,14},{7,23},{8,0},{9,25... | collective-permute-start | bytes 17301512 | tf_op jit(solution)/shard_map/ppermute | solution.py:551
  484.7 418.8 %reduce-scatter.8.cloned.1.call-start = ((), (), s32[]{:S(2)}) async-start(), calls=%async_computation.6 | async-start | bytes 3604480 | tf_op jit(solution)/shard_map/reduce_scatter | solution.py:749
  495.8 12.1 %copy-start.14 = (bf16[256,32,32]{0,2,1:T(8,128)(2,1)S(1)}, bf16[256,32,32]{0,2,1:T(8,128)(2,1)}, u32[]{:S(2)}) copy-start(bf16[256,32,32]{0,2,1:T(8,128)(2,1)} %copy-done.13) | copy-start | bytes 1572868
  495.8 12.1 %copy-start.16 = (bf16[256,32,32]{0,2,1:T(8,128)(2,1)S(1)}, bf16[256,32,32]{0,2,1:T(8,128)(2,1)}, u32[]{:S(2)}) copy-start(bf16[256,32,32]{0,2,1:T(8,128)(2,1)} %copy-done.15) | copy-start | bytes 1572868
  510.5 7.8 copy-start.19
  518.0 1.9 copy-start.21
  518.0 1.9 copy-start.22
  518.0 34.6 %collective-permute-start.3 = (bf16[256,512]{0,1:T(8,128)(2,1)S(1)}, bf16[256,512]{0,1:T(8,128)(2,1)S(1)}, u32[]{:S(2)}, u32[]{:S(2)}) collective-permute-start(bf16[256,512]{0,1:T(8,128)(2,1)S(1)} %fusion.40), channel_id=1, source_target_pairs={{0,8},{8,0},{16,24},{24,16},{1,9},{9,1},{17,25},{25,17},{2,10},{10... | collective-permute-start | bytes 786440 | tf_op jit(solution)/shard_map/ppermute | solution.py:725
  552.9 8.7 copy-start.1
  553.0 8.7 copy-start.24
  553.0 8.7 copy-start.29
  560.4 34.8 %collective-permute-start.4 = (bf16[4,176,2048]{2,1,0:T(8,128)(2,1)}, bf16[4,176,2048]{2,1,0:T(8,128)(2,1)}, u32[]{:S(2)}, u32[]{:S(2)}) collective-permute-start(bf16[4,176,2048]{2,1,0:T(8,128)(2,1)} %fusion.13), channel_id=1, source_target_pairs={{0,16},{1,9},{2,18},{3,11},{4,20},{5,13},{6,22},{7,15},{8,24},{9,1... | collective-permute-start | bytes 8650760 | tf_op jit(solution)/shard_map/ppermute | solution.py:551
  604.1 299.5 %all-reduce.3.cloned.1.call-start = ((), (), s32[]{:S(2)}) async-start(), calls=%async_computation.4 | async-start | bytes 2097152 | tf_op jit(solution)/shard_map/psum | solution.py:746
  604.8 312.0 %reduce-scatter.6.cloned.1.call-start = ((), (), s32[]{:S(2)}) async-start(), calls=%async_computation.5 | async-start | bytes 11796480 | tf_op jit(solution)/shard_map/reduce_scatter | solution.py:608
  610.7 377.8 %all-reduce.5.cloned.1.call-start = ((), (), s32[]{:S(2)}) async-start(), calls=%async_computation.7 | async-start | bytes 2621440 | tf_op jit(solution)/shard_map/psum | solution.py:755
  916.8 115.0 %all-gather.3.cloned.1.call-start = ((), (), s32[]{:S(2)}) async-start(), calls=%async_computation.8 | async-start | bytes 3604480 | tf_op jit(solution)/shard_map/all_gather | solution.py:602
  917.4 13.3 %copy-start.6 = (f32[256,2048]{1,0:T(8,128)S(1)}, f32[256,2048]{1,0:T(8,128)}, u32[]{:S(2)}) copy-start(f32[256,2048]{1,0:T(8,128)} %get-tuple-element.61) | copy-start | bytes 6291460
  917.4 13.3 %copy-start.12 = (f32[256,2048]{1,0:T(8,128)S(1)}, f32[256,2048]{1,0:T(8,128)}, u32[]{:S(2)}) copy-start(f32[256,2048]{1,0:T(8,128)} %get-tuple-element.100) | copy-start | bytes 6291460
  917.4 13.3 %copy-start.31 = (f32[256]{0:T(256)S(1)}, f32[256]{0:T(256)}, u32[]{:S(2)}) copy-start(f32[256]{0:T(256)} %get-tuple-element.87) | copy-start | bytes 3076
  930.7 1.7 copy-start.30
  930.7 2.3 copy-start.17
  1031.8 2.7 copy-start.5
Sparse Core Ops, SparseCore 0:
  484.8 91.4 reduce-scatter.3
  604.2 63.9 reduce-scatter.7
  671.3 70.5 all-reduce.2
  744.6 172.1 reduce-scatter.5
  919.7 68.6 all-reduce.4
  990.1 41.6 all-gather.2

commit v5 on v4

--- a/solution.py
+++ b/solution.py
@@ -100,7 +100,9 @@
         return part
 
 
-def reduce_kernel(chips, bits, count, terms, small, out, arrived, small_out, *scratch):
+def reduce_kernel(chips, bits, counts, *refs):
+    terms, small, outs, arrived, small_out, scratch = refs[:2], refs[2], refs[3:5], refs[5], refs[6], refs[7:]
+    count = sum(counts)
     halves = scratch[:bits]
     own, got, along, final = scratch[bits : bits + 4]
     (own_sem, got_sem, core_out, core_in, half_out, half_in, along_out, along_in, spread_out, spread_in, local_sem) = (
@@ -120,12 +122,21 @@
         pl.semaphore_signal(barrier, inc=1, device_id=peer, device_id_type=pl.DeviceIdType.MESH)
     pl.semaphore_wait(barrier, len(peers))
 
-    def columns(j):
-        return pl.ds(pl.multiple_of(j * width, 128), width)
-
-    def core_copy(j):
+    def columns(column):
+        return pl.ds(pl.multiple_of(column * width, 128), width)
+
+    def launch(make, j):
+        @pl.when(j < counts[0])
+        def _():
+            make(j, 0, j).start()
+
+        @pl.when(j >= counts[0])
+        def _():
+            make(j, 1, j - counts[0]).start()
+
+    def core_copy(j, which=0, column=0):
         return pltpu.make_async_remote_copy(
-            src_ref=terms.at[:, 1 - here.core, :, columns(j)],
+            src_ref=terms[which].at[:, 1 - here.core, :, columns(column)],
             dst_ref=arrived.at[j],
             send_sem=core_out.at[j],
             recv_sem=core_in.at[j],
@@ -133,8 +144,10 @@
             device_id_type=pl.DeviceIdType.MESH,
         )
 
-    def own_load(j):
-        return pltpu.make_async_copy(terms.at[:, here.core, :, columns(j)], own.at[j % slots], own_sem.at[j])
+    def own_load(j, which=0, column=0):
+        return pltpu.make_async_copy(
+            terms[which].at[:, here.core, :, columns(column)], own.at[j % slots], own_sem.at[j]
+        )
 
     def got_load(j):
         return pltpu.make_async_copy(arrived.at[j], got.at[j % 2], got_sem.at[j])
@@ -168,33 +181,34 @@
             device_id_type=pl.DeviceIdType.MESH,
         )
 
-    def place_of(j, subset):
-        return out.at[pl.ds(pl.multiple_of(here.part_of(subset) * piece, piece), piece), columns(j)]
-
-    def spread_copy(j, subset):
+    def place_of(which, column, subset):
+        first = pl.multiple_of(here.part_of(subset) * piece, piece)
+        return outs[which].at[pl.ds(first, piece), columns(column)]
+
+    def spread_copy(subset, j, which=0, column=0):
         last = subset.bit_length() - 1
         parent = subset ^ (1 << last)
         return pltpu.make_async_remote_copy(
-            src_ref=final.at[j] if parent == 0 else place_of(j, parent),
-            dst_ref=place_of(j, parent),
+            src_ref=final.at[j] if parent == 0 else place_of(which, column, parent),
+            dst_ref=place_of(which, column, parent),
             send_sem=spread_out.at[j, subset - 1],
             recv_sem=spread_in.at[j, subset - 1],
             device_id=here.partner(last),
             device_id_type=pl.DeviceIdType.MESH,
         )
 
-    def local_copy(j):
-        return pltpu.make_async_copy(final.at[j], place_of(j, 0), local_sem.at[j])
+    def local_copy(j, which=0, column=0):
+        return pltpu.make_async_copy(final.at[j], place_of(which, column, 0), local_sem.at[j])
 
     def level(size):
         return [subset for subset in range(1, seq) if bin(subset).count("1") == size]
 
     def fresh(j):
-        core_copy(j).start()
+        launch(core_copy, j)
 
     def loads(j):
         core_copy(j).wait()
-        own_load(j).start()
+        launch(own_load, j)
         got_load(j).start()
 
     def first_sum(j):
@@ -255,15 +269,15 @@
             return carry
 
         lax.fori_loop(0, piece // block, body, 0)
-        local_copy(j).start()
+        launch(local_copy, j)
         for subset in level(1):
-            spread_copy(j, subset).start()
+            launch(functools.partial(spread_copy, subset), j)
 
     def pass_on(j, size):
         for subset in level(size):
-            spread_copy(j, subset).wait()
+            spread_copy(subset, j).wait()
         for subset in level(size + 1):
-            spread_copy(j, subset).start()
+            launch(functools.partial(spread_copy, subset), j)
 
     def small_copy(step):
         return pltpu.make_async_remote_copy(
@@ -321,22 +335,25 @@
     lax.fori_loop(0, count + len(stages) - 1, round_of, 0)
 
 
-def reduced(terms, small, chips, bits, count, number):
-    rows, width = terms.shape[0] // (2 * chips), terms.shape[1]
-    seq, wide = 1 << bits, width // count
+def reduced(terms, small, chips, bits, wide):
+    rows = terms[0].shape[0] // (2 * chips)
+    widths = [one.shape[1] for one in terms]
+    counts = [width // wide for width in widths]
+    count, seq = sum(counts), 1 << bits
     piece = rows // seq
     slots = bits + 5
     dma = pltpu.SemaphoreType.DMA
     steps = 1 + bits + (chips - 1).bit_length()
-    out, _, small_out = pl.pallas_call(
-        functools.partial(reduce_kernel, chips, bits, count),
+    *outs, _, small_out = pl.pallas_call(
+        functools.partial(reduce_kernel, chips, bits, counts),
         out_shape=(
-            jax.ShapeDtypeStruct((rows, width), BF16),
+            *[jax.ShapeDtypeStruct((rows, width), BF16) for width in widths],
             jax.ShapeDtypeStruct((count, chips, rows, wide), BF16),
             jax.ShapeDtypeStruct(small.shape, F32),
         ),
-        in_specs=[pl.BlockSpec(memory_space=pl.ANY), pl.BlockSpec(memory_space=pltpu.VMEM)],
+        in_specs=[pl.BlockSpec(memory_space=pl.ANY)] * 2 + [pl.BlockSpec(memory_space=pltpu.VMEM)],
         out_specs=(
+            pl.BlockSpec(memory_space=pl.ANY),
             pl.BlockSpec(memory_space=pl.ANY),
             pl.BlockSpec(memory_space=pl.ANY),
             pl.BlockSpec(memory_space=pltpu.VMEM),
@@ -364,11 +381,11 @@
             dma((steps,)),
         ],
         compiler_params=pltpu.CompilerParams(
-            collective_id=number, has_side_effects=True, vmem_limit_bytes=62 * 1024 * 1024
+            collective_id=0, has_side_effects=True, vmem_limit_bytes=62 * 1024 * 1024
         ),
         cost_estimate=pl.CostEstimate(flops=0, bytes_accessed=800_000_000, transcendentals=0),
-    )(terms.reshape(chips, 2, rows, width), small)
-    return out, small_out
+    )(*[one.reshape(chips, 2, rows, -1) for one in terms], small)
+    return *outs, small_out
 
 
 def gather_kernel(chips, bits, units, weights, ahead, *refs):
@@ -697,11 +714,12 @@
     grad_hidden = dot_nt(grad_down, down_whole)
     grad_gate = grad_hidden * up_part * sigmoid_gate * (1.0 + gate_part * (1.0 - sigmoid_gate))
     grad_up = grad_hidden * gate_part * sigmoid_gate
-    grad_gate_up = jnp.concatenate([grad_gate, grad_up], axis=1).astype(BF16)
+    grad_gate, grad_up = down_fold.advance(grad_gate.astype(BF16), grad_up.astype(BF16))
+    grad_gate_up = jnp.concatenate([grad_gate, grad_up], axis=1)
     grad_normed_mlp = dot_nt(grad_gate_up, gate_up_whole)
     mlp_term = jnp.sum(grad_normed_mlp * residual * inv_second, axis=0)
     grad_resid = grad_out + norm_back(grad_normed_mlp, residual, inv_second, mlp_gain)
-    (grad_proj,) = down_fold.advance(grad_resid.astype(BF16))
+    grad_proj = grad_resid.astype(BF16)
     out_part = scatter_rows(dot_tn(attended, grad_proj).astype(BF16))
     grad_heads = dot_nt(grad_proj, out_whole)
     grad_heads = grad_heads.astype(BF16).reshape(rows, KV, share, HD)
@@ -736,7 +754,7 @@
     ).astype(BF16)
     if down_fold.step < bits:
         (grad_qkv,) = down_fold.advance(grad_qkv)
-    qkv_part = scatter_rows(dot_tn(normed_low, grad_qkv).astype(BF16))
+    qkv_terms = dot_tn(normed_low, grad_qkv).astype(BF16)
     grad_normed = dot_nt(grad_qkv, qkv_whole)
     attn_term = jnp.sum(grad_normed * inputs * inv_first, axis=0)
     tokens_grad = (grad_resid + norm_back(grad_normed, inputs, inv_first, attn_gain)).astype(BF16)
@@ -747,12 +765,9 @@
     down_part, gate_up_terms = down_fold.finish(gate_up_terms)
     groups = [list(range(core, 2 * chips, 2)) for core in range(2)]
     down_part = lax.psum_scatter(down_part, "batch", scatter_dimension=0, axis_index_groups=groups)
-    gate_up_grad, gains = reduced(gate_up_terms, gains, chips, bits, 11, 0)
+    gate_up_grad, qkv_grad, gains = reduced((gate_up_terms, qkv_terms), gains, chips, bits, 512)
     gains = gains.reshape(-1)
-    gate_up_grad, out_grad, qkv_part, down_part = lax.optimization_barrier(
-        (gate_up_grad, out_grad, qkv_part, down_part)
-    )
-    qkv_grad = lax.psum(qkv_part, "seq")
+    gate_up_grad, down_part = lax.optimization_barrier((gate_up_grad, down_part))
     down_grad = down_fold.spread(down_part)
     return (
         output[None],

time: 1050 us -> 1020 us (0.971)
  waiting for transfers between devices: 136 us -> 59.1 us
  Pallas kernels: 602 us -> 645 us
    psum x1 -> x0, waiting for transfers between devices: 45.5 us -> none  [local(): qkv_grad = lax.psum(qkv_part, 'seq')]
    pallas_call x1, Pallas kernels: 293 us -> 336 us  [reduced(): pl.pallas_call(functools.partial(reduce_kernel, chips, bits, counts), out...]
    all_gather x1, waiting for transfers between devices: 40.3 us -> 12.2 us  [spread(): parts = lax.all_gather(mine, 'seq')]
    reduce_scatter x2 -> x1, waiting for transfers between devices: 13.2 us -> 0.02 us  [scatter_rows(): return lax.psum_scatter(terms, 'batch', scatter_dimension=0, tiled=True)]
  transfers between devices with their start and end apart: 11 -> 9, of which waited for: 6 -> 4; matrix products, arithmetic and copies ran while one was open for 17% -> 15% of each run, Pallas kernels for 28% -> 33%
where the time goes in v5:
time: 1020 us; the launch traced here: 1010 us
  Pallas kernels  645 us (63%)
  matrix products  191 us (19%)
  other arithmetic  75.3 us (7%)
  waiting for transfers between devices  59.1 us (6%)
  local copies, waits for them, and re-layouts  22.6 us (2%)
  between operations  14.7 us (1%)
    pallas_call x1, Pallas kernels, reduced(): pl.pallas_call(functools.partial(reduce_kernel, chips, bits, counts), out...  336 us
    pallas_call x1, Pallas kernels, gathered(): pl.pallas_call(functools.partial(gather_kernel, chips, bits, units, weigh...  309 us
    dot_general x4, matrix products, dot_nt(): lax.dot_general(left, right, (((1,), (1,)), ((), ())), preferred_element_...  58.7 us
    dot_general x4, matrix products, dot(): return jnp.dot(left, right, preferred_element_type=F32)  50.5 us
    dot_general x4, matrix products, dot_tn(): lax.dot_general(left, right, (((0,), (0,)), ((), ())), preferred_element_...  43.8 us
    ppermute x1, waiting for transfers between devices, local(): arrived = lax.ppermute(away, 'seq', swap)  33.6 us
    convert_element_type x3, other arithmetic, total(): return total.astype(BF16)  27.4 us
  transfers between devices with their start and end apart: 9, of which 4 were waited for; matrix products, arithmetic and copies ran while one was open for 15% of the time, Pallas kernels for 33%

profile of v5, /device:TPU:0, one launch (start us, length us, event | category | flops | bytes accessed | tf_op | source)
XLA Modules:
  0.0 1014.6 jit_solution(17656917287874160706)
XLA Ops:
  7.2 1.5 fusion.20
  9.3 309.3 %shard_map.161 = (bf16[2048,2560]{1,0:T(8,128)(2,1)}, bf16[2048,2048]{1,0:T(8,128)(2,1)}, bf16[2048,11264]{1,0:T(8,128)(2,1)}, bf16[5632,2048]{1,0:T(8,128)(2,1)}) custom-call(bf16[256,2560]{1,0:T(8,128)(2,1)} %refs_0_.1, bf16[256,2048]{1,0:T(8,128)(2,1)} %refs_1_.1, bf16[256,11264]{1,0:T(8,128)(2,1)} %refs_2_.1, bf16[704,2048]{1,0:T(8,128)(2,1)} %refs_3_.1), custom_call_target="tpu_custom_call" | custom-call | bytes 900000000 | tf_op jit(solution)/shard_map/pallas_call | solution.py:520
  318.7 6.9 convolution_convert_fusion.4
  326.5 0.8 fusion.46
  327.5 2.3 collective-permute-start
  329.8 1.6 slice_convert_fusion
  331.4 3.0 copy.40
  334.6 1.9 subtract_convert_fusion.1
  337.0 8.7 fusion.57
  345.8 7.4 fusion.32
  353.2 6.2 multiply_reduce_fusion.2
  359.4 1.3 copy-done.4
  361.0 23.4 %fusion.58 = f32[256,11264]{1,0:T(8,128)} fusion(bf16[256,2048]{1,0:T(8,128)(2,1)S(1)} %multiply_convert_fusion.3, bf16[2048,11264]{1,0:T(8,128)(2,1)} %get-tuple-element.35), kind=kOutput, calls=%fused_computation.131 | convolution fusion | flops 11811160064 | bytes 58720256 | tf_op jit(solution)/shard_map/dot_general | solution.py:50
  384.4 5.2 multiply_convert_fusion.2
  389.7 11.1 %convolution_convert_fusion.1 = bf16[5632,2048]{1,0:T(8,128)(2,1)} fusion(bf16[256,5632]{1,0:T(8,128)(2,1)S(1)} %multiply_convert_fusion.2, bf16[1,256,2048]{2,1,0:T(8,128)(2,1)S(1)} %copy-done.11), kind=kOutput, calls=%fused_computation.2 | convolution fusion | flops 5917114368 | bytes 27000832 | tf_op jit(solution)/shard_map/dot_general | solution.py:58
  400.7 10.1 dynamic-slice_bitcast_fusion
  410.8 22.6 %multiply_convert_fusion = (bf16[256,5632]{1,0:T(8,128)(2,1)S(1)}, bf16[256,5632]{1,0:T(8,128)(2,1)S(1)}) fusion(f32[256,11264]{1,0:T(8,128)} %fusion.58, bf16[256,2048]{1,0:T(8,128)(2,1)S(1)} %bitcast.158, bf16[5632,2048]{1,0:T(8,128)(2,1)} %get-tuple-element.36), kind=kOutput, calls=%fused_computation.27 | convolution fusion | flops 5924323328 | bytes 41418752 | tf_op jit(solution)/shard_map/dot_general | solution.py:54
  433.4 10.2 %fusion.5 = bf16[4,352,2048]{2,1,0:T(8,128)(2,1)} fusion(bf16[4,704,2048]{2,1,0:T(8,128)(2,1)} %collective-permute-done.1, s32[]{:T(128)S(6)} %select_n.61, bf16[4,2,704,2048]{3,2,1,0:T(8,128)(2,1)} %bitcast.147, s32[]{:T(128)S(6)} %select_n.59), kind=kLoop, calls=%fused_computation.12 | loop fusion | flops 11534336 | bytes 17301512 | tf_op jit(solution)/shard_map/convert_element_type | solution.py:598
  443.7 1.8 constant_dynamic-update-slice_fusion.1
  445.4 1.8 constant_dynamic-update-slice_fusion
  447.2 21.7 %multiply_reduce_fusion = (f32[2048]{0:T(1024)S(1)}, f32[256]{0:T(256)S(1)}, f32[256,2048]{1,0:T(8,128)}) fusion(f32[256,2048]{1,0:T(8,128)S(1)} %copy-done.5, f32[256]{0:T(256)S(1)} %get-tuple-element.90, f32[2048]{0:T(1024)S(1)} %copy-done.29, bf16[256,11264]{1,0:T(8,128)(2,1)} %constant_dynamic-update-slice_fusion, bf16[2048,11264]{1,0:T(8,128)(2,1)} %get-tuple-element.35), kind=kOutput, calls=%fused_computation.58 | convolution fusion | flops 11814303744 | bytes 56117248 | tf_op jit(solution)/shard_map/dot_general | solution.py:54
  468.9 2.9 subtract_add_fusion
  471.9 5.7 convolution_convert_fusion.3
  477.7 5.8 convolution_convert_fusion.5
  483.5 0.7 copy.44
  484.2 1.8 collective-permute-start.2
  486.0 10.9 %fusion.1 = (f32[4,8,256]{2,1,0:T(8,128)S(1)}, f32[4,512,256,8]{2,1,3,0:T(8,128)}) fusion(f32[4,8,256,512]{2,3,1,0:T(8,128)} %get-tuple-element.94, f32[4,8,256]{2,1,0:T(8,128)S(1)} %copy-done.28, bf16[512,4,64,1]{0,2,3,1:T(8,128)(2,1)S(1)} %bitcast.176, bf16[256,4,8,64]{0,3,2,1:T(8,128)(2,1)S(1)} %bitcast.168), kind=kOutput, calls=%fused_computation.5 | convolution fusion | flops 549445632 | bytes 34930688 | tf_op jit(solution)/shard_map/qgsd,kgd->gsqk/dot_general | solution.py:727
  496.9 12.1 %fusion.3 = bf16[4,8,256,512]{2,3,1,0:T(8,128)(2,1)S(1)} fusion(f32[4,512,256,8]{2,1,3,0:T(8,128)} %get-tuple-element.99, f32[4,8,256]{2,1,0:T(8,128)S(1)} %get-tuple-element.98, f32[4,8,256,512]{2,3,1,0:T(8,128)} %get-tuple-element.94, f32[4,8,256]{2,1,0:T(8,128)S(1)} %copy-done.28), kind=kLoop, calls=%fused_computation.7 | loop fusion | flops 16777216 | bytes 42008576 | tf_op jit(solution)/shard_map/convert_element_type | solution.py:729
  509.0 2.6 fusion.35
  511.7 7.4 fusion.14
  519.8 1.5 convolution_multiply_fusion
  521.9 33.6 %collective-permute-done.3 = bf16[256,512]{0,1:T(8,128)(2,1)S(1)} collective-permute-done((bf16[256,512]{0,1:T(8,128)(2,1)S(1)}, bf16[256,512]{0,1:T(8,128)(2,1)S(1)}, u32[]{:S(2)}, u32[]{:S(2)}) %collective-permute-start.3) | collective-permute-done | bytes 262176 | tf_op jit(solution)/shard_map/ppermute | solution.py:743
  555.8 8.3 fusion.13
  564.1 8.6 fusion.29
  573.3 1.2 collective-permute-start.4
  574.6 21.2 %convolution_convert_fusion = bf16[2048,11264]{1,0:T(8,128)(2,1)} fusion(bf16[256,2048]{1,0:T(8,128)(2,1)S(1)} %copy-done.13, bf16[256,11264]{1,0:T(8,128)(2,1)} %constant_dynamic-update-slice_fusion), kind=kOutput, calls=%fused_computation.1 | convolution fusion | flops 11834228736 | bytes 52953088 | tf_op jit(solution)/shard_map/dot_general | solution.py:58
  595.7 12.4 %collective-permute-done.4 = bf16[4,176,2048]{2,1,0:T(8,128)(2,1)} collective-permute-done((bf16[4,176,2048]{2,1,0:T(8,128)(2,1)}, bf16[4,176,2048]{2,1,0:T(8,128)(2,1)}, u32[]{:S(2)}, u32[]{:S(2)}) %collective-permute-start.4) | collective-permute-done | bytes 2883616 | tf_op jit(solution)/shard_map/ppermute | solution.py:568
  608.1 8.8 fusion.11
  617.8 5.8 convolution_convert_fusion.2
  623.6 336.0 %shard_map.162 = (bf16[256,11264]{1,0:T(8,128)(2,1)}, bf16[256,2560]{1,0:T(8,128)(2,1)}, bf16[27,4,256,512]{3,2,1,0:T(8,128)(2,1)}, f32[32,128]{1,0:T(8,128)}) custom-call(bf16[4,2,256,11264]{3,2,1,0:T(8,128)(2,1)} %bitcast.145, bf16[4,2,256,2560]{3,2,1,0:T(8,128)(2,1)} %bitcast.150, f32[32,128]{1,0:T(8,128)} %pad_maximum_fusion.15.refs_2_), custom_call_target="tpu_custom_call" | custom-call | bytes 800000000 | tf_op jit(solution)/shard_map/pallas_call | solution.py:347
  959.6 13.9 %fusion.19 = bf16[1,256,2048]{2,1,0:T(8,128)(2,1)} fusion(f32[256,2048]{1,0:T(8,128)} %copy-done.4, bf16[256,5632]{1,0:T(8,128)(2,1)} %copy-done.6, bf16[5632,2048]{1,0:T(8,128)(2,1)} %get-tuple-element.36), kind=kOutput, calls=%fused_computation.47 | convolution fusion | flops 5906628608 | bytes 29097984 | tf_op jit(solution)/shard_map/dot_general | solution.py:50
  973.6 1.6 fusion.36
  975.2 1.8 convert_element_type.193
  977.6 8.4 convert_element_type.202
  986.1 2.8 convert_element_type.195
  988.9 12.2 %all-gather.3.cloned.1.call-done = bf16[704,2048]{1,0:T(8,128)(2,1)} async-done(((bf16[176,2048]{1,0:T(8,128)(2,1)}), bf16[704,2048]{1,0:T(8,128)(2,1)}) %all-gather.3.cloned.1.call-update) | async-done | bytes 2883600 | tf_op jit(solution)/shard_map/all_gather | solution.py:619
  1001.0 2.1 slice_bitcast_fusion.3
  1004.4 3.5 bitcast_convert_fusion
  (116 shorter events, 7.4 us)
Async XLA Ops:
  7.2 609.9 %reduce-scatter.3.cloned.1.call-start = ((), (), s32[]{:S(2)}) async-start(), calls=%async_computation.2 | async-start | bytes 9437184 | tf_op jit(solution)/shard_map/reduce_scatter | solution.py:625
  8.7 309.9 %copy-start = (bf16[1,256,2048]{2,1,0:T(8,128)(2,1)S(1)}, bf16[1,256,2048]{2,1,0:T(8,128)(2,1)}, u32[]{:S(2)}) copy-start(bf16[1,256,2048]{2,1,0:T(8,128)(2,1)} %param.10) | copy-start | bytes 3145732
  8.8 309.9 %copy-start.25 = (f32[2048]{0:T(1024)S(1)}, f32[2048]{0:T(1024)}, u32[]{:S(2)}) copy-start(f32[2048]{0:T(1024)} %param.14) | copy-start | bytes 24580
  9.3 316.3 %copy-start.30 = (f32[256]{0:T(256)}, f32[256]{0:T(256)S(1)}, u32[]{:S(2)}) copy-start(f32[256]{0:T(256)S(1)} %get-tuple-element.88) | copy-start | bytes 3076
  318.7 7.1 copy-start.34
  327.3 9.2 copy-start.22
  327.5 9.2 collective-permute-start
  336.5 9.3 copy-start.15
  336.5 9.2 copy-start.17
  336.9 8.9 copy-start.20
  345.7 7.4 copy-start.27
  353.1 6.2 copy-start.8
  353.1 7.6 copy-start.29
  359.4 1.3 copy-start.4
  360.9 23.4 %copy-start.12 = (bf16[256,2048]{1,0:T(8,128)(2,1)}, bf16[256,2048]{1,0:T(8,128)(2,1)S(1)}, u32[]{:S(2)}) copy-start(bf16[256,2048]{1,0:T(8,128)(2,1)S(1)} %multiply_convert_fusion.3) | copy-start | bytes 3145732
  384.4 5.3 copy-start.11
  389.7 11.1 %copy-start.6 = (bf16[256,5632]{1,0:T(8,128)(2,1)}, bf16[256,5632]{1,0:T(8,128)(2,1)S(1)}, u32[]{:S(2)}) copy-start(bf16[256,5632]{1,0:T(8,128)(2,1)S(1)} %multiply_convert_fusion.2) | copy-start | bytes 8650756
  410.8 22.6 %collective-permute-start.1 = (bf16[4,704,2048]{2,1,0:T(8,128)(2,1)}, bf16[4,704,2048]{2,1,0:T(8,128)(2,1)}, u32[]{:S(2)}, u32[]{:S(2)}) collective-permute-start(bf16[4,704,2048]{2,1,0:T(8,128)(2,1)} %dynamic-slice_bitcast_fusion), channel_id=1, source_target_pairs={{0,1},{1,0},{2,3},{3,2},{4,5},{5,4},{6,7},{7,6},{8,9},{9,8},{10,11... | collective-permute-start | bytes 34603016 | tf_op jit(solution)/shard_map/ppermute | solution.py:568
  443.7 3.5 copy-start.5
  468.9 2.9 copy-start.9
  471.9 5.8 copy-start.2
  477.7 481.9 %reduce-scatter.5.cloned.1.call-start = ((), (), s32[]{:S(2)}) async-start(), calls=%async_computation.4 | async-start | bytes 3604480 | tf_op jit(solution)/shard_map/reduce_scatter | solution.py:767
  477.7 8.3 copy-start.28
  484.2 71.6 %collective-permute-start.2 = (bf16[4,352,2048]{2,1,0:T(8,128)(2,1)}, bf16[4,352,2048]{2,1,0:T(8,128)(2,1)S(1)}, u32[]{:S(2)}, u32[]{:S(2)}) collective-permute-start(bf16[4,352,2048]{2,1,0:T(8,128)(2,1)} %fusion.5), channel_id=1, source_target_pairs={{0,8},{1,17},{2,10},{3,19},{4,12},{5,21},{6,14},{7,23},{8,0},{9,25... | collective-permute-start | bytes 17301512 | tf_op jit(solution)/shard_map/ppermute | solution.py:568
  496.9 12.1 %copy-start.16 = (bf16[256,32,32]{0,2,1:T(8,128)(2,1)S(1)}, bf16[256,32,32]{0,2,1:T(8,128)(2,1)}, u32[]{:S(2)}) copy-start(bf16[256,32,32]{0,2,1:T(8,128)(2,1)} %copy-done.15) | copy-start | bytes 1572868
  496.9 12.1 %copy-start.18 = (bf16[256,32,32]{0,2,1:T(8,128)(2,1)S(1)}, bf16[256,32,32]{0,2,1:T(8,128)(2,1)}, u32[]{:S(2)}) copy-start(bf16[256,32,32]{0,2,1:T(8,128)(2,1)} %copy-done.17) | copy-start | bytes 1572868
  511.7 8.2 copy-start.21
  519.1 2.3 copy-start.23
  519.1 2.3 copy-start.24
  519.2 36.3 %collective-permute-start.3 = (bf16[256,512]{0,1:T(8,128)(2,1)S(1)}, bf16[256,512]{0,1:T(8,128)(2,1)S(1)}, u32[]{:S(2)}, u32[]{:S(2)}) collective-permute-start(bf16[256,512]{0,1:T(8,128)(2,1)S(1)} %fusion.39), channel_id=1, source_target_pairs={{0,8},{8,0},{16,24},{24,16},{1,9},{9,1},{17,25},{25,17},{2,10},{10... | collective-permute-start | bytes 786440 | tf_op jit(solution)/shard_map/ppermute | solution.py:743
  555.8 8.4 copy-start.1
  555.8 8.3 copy-start.26
  555.8 8.3 copy-start.31
  555.8 8.3 copy-start.10
  564.1 10.5 %copy-start.13 = (bf16[256,2048]{1,0:T(8,128)(2,1)S(1)}, bf16[256,2048]{1,0:T(8,128)(2,1)}, u32[]{:S(2)}) copy-start(bf16[256,2048]{1,0:T(8,128)(2,1)} %copy-done.12) | copy-start | bytes 3145732
  573.3 34.8 %collective-permute-start.4 = (bf16[4,176,2048]{2,1,0:T(8,128)(2,1)}, bf16[4,176,2048]{2,1,0:T(8,128)(2,1)}, u32[]{:S(2)}, u32[]{:S(2)}) collective-permute-start(bf16[4,176,2048]{2,1,0:T(8,128)(2,1)} %fusion.13), channel_id=1, source_target_pairs={{0,16},{1,9},{2,18},{3,11},{4,20},{5,13},{6,22},{7,15},{8,24},{9,1... | collective-permute-start | bytes 8650760 | tf_op jit(solution)/shard_map/ppermute | solution.py:568
  617.0 369.1 %all-reduce.2.cloned.1.call-start = ((), (), s32[]{:S(2)}) async-start(), calls=%async_computation.3 | async-start | bytes 2097152 | tf_op jit(solution)/shard_map/psum | solution.py:764
  617.7 383.3 %all-gather.3.cloned.1.call-start = ((), (), s32[]{:S(2)}) async-start(), calls=%async_computation.5 | async-start | bytes 3604480 | tf_op jit(solution)/shard_map/all_gather | solution.py:619
  959.6 14.0 %copy-start.3 = (f32[256,2048]{1,0:T(8,128)S(1)}, f32[256,2048]{1,0:T(8,128)}, u32[]{:S(2)}) copy-start(f32[256,2048]{1,0:T(8,128)} %copy-done.2) | copy-start | bytes 6291460
  959.6 14.0 %copy-start.14 = (f32[256,2048]{1,0:T(8,128)S(1)}, f32[256,2048]{1,0:T(8,128)}, u32[]{:S(2)}) copy-start(f32[256,2048]{1,0:T(8,128)} %get-tuple-element.100) | copy-start | bytes 6291460
  959.6 14.0 %copy-start.33 = (f32[256]{0:T(256)S(1)}, f32[256]{0:T(256)}, u32[]{:S(2)}) copy-start(f32[256]{0:T(256)} %get-tuple-element.87) | copy-start | bytes 3076
  973.6 1.7 copy-start.19
  973.6 3.5 copy-start.32
  1001.0 2.7 copy-start.7
Sparse Core Ops, SparseCore 0:
  477.8 92.0 reduce-scatter.2
  617.1 74.4 reduce-scatter.4
  694.7 76.5 all-reduce.1
  959.7 41.2 all-gather.2

commit v6 on v3

--- a/solution.py
+++ b/solution.py
@@ -611,7 +611,6 @@
     up_part = gate_up[:, ff_width:]
     sigmoid_gate = jax.nn.sigmoid(gate_part)
     hidden_low = (gate_part * sigmoid_gate * up_part).astype(BF16)
-    output = (residual + dot(hidden_low, down_whole)).astype(BF16)
 
     grad_out = cotangent[0].astype(F32)
     grad_down = cotangent[0]
@@ -661,12 +660,13 @@
         ],
         axis=1,
     ).astype(BF16)
-    qkv_terms, down_early = lax.optimization_barrier((dot_tn(normed_low, grad_qkv).astype(BF16), down_early))
+    qkv_terms = dot_tn(normed_low, grad_qkv).astype(BF16)
     qkv_part = scatter_rows(qkv_terms)
     grad_normed = dot_nt(grad_qkv, qkv_whole)
     attn_term = jnp.sum(grad_normed * inputs * inv_first, axis=0)
     tokens_grad = (grad_resid + norm_back(grad_normed, inputs, inv_first, attn_gain)).astype(BF16)
     gains = jnp.concatenate([attn_term, mlp_term]).reshape(-1, 128)
+    gains, down_early = lax.optimization_barrier((gains, down_early))
     gate_up_grad, gains = reduced(gate_up_terms, gains, chips, bits, 11, 0)
     gains = gains.reshape(-1)
     gate_up_grad, down_early, out_part, qkv_part, down_terms = lax.optimization_barrier(
@@ -676,6 +676,8 @@
         down_late, _ = reduced(down_terms, jnp.zeros((8, 128), F32), chips, bits, 4, 2)
     else:
         down_late = lax.psum(scatter_rows(down_terms), "seq")
+    down_late, gate_up_grad, hidden_low = lax.optimization_barrier((down_late, gate_up_grad, hidden_low))
+    output = (residual + dot(hidden_low, down_whole)).astype(BF16)
     down_early, out_grad, qkv_grad = lax.psum((down_early, out_part, qkv_part), "seq")
     down_grad = jnp.concatenate([down_early, down_late], axis=1)
     return (

time: 994 us -> 1000 us (level)
  Pallas kernels: 702 us -> 720 us
  waiting for transfers between devices: 17.2 us -> 6.07 us
    pallas_call x2, Pallas kernels: 393 us -> 411 us  [reduced(): pl.pallas_call(functools.partial(reduce_kernel, chips, bits, count), out_...]
    reduce_scatter x3, waiting for transfers between devices: 12.7 us -> 1.56 us  [scatter_rows(): return lax.psum_scatter(terms, 'batch', scatter_dimension=0, tiled=True)]
  transfers between devices with their start and end apart: 6 -> 6, of which waited for: 2 -> 2; matrix products, arithmetic and copies ran while one was open for 17% -> 17% of each run, Pallas kernels for 40% -> 41%
where the time goes in v6:
time: 1000 us; the launch traced here: 996 us
  Pallas kernels  720 us (72%)
  matrix products  192 us (19%)
  other arithmetic  49.5 us (5%)
  between operations  14.9 us (1%)
    pallas_call x2, Pallas kernels, reduced(): pl.pallas_call(functools.partial(reduce_kernel, chips, bits, count), out_...  411 us
    pallas_call x1, Pallas kernels, gathered(): pl.pallas_call(functools.partial(gather_kernel, chips, bits, units, weigh...  309 us
    dot_general x4, matrix products, dot_nt(): lax.dot_general(left, right, (((1,), (1,)), ((), ())), preferred_element_...  55.7 us
    dot_general x4, matrix products, dot(): return jnp.dot(left, right, preferred_element_type=F32)  49.4 us
    dot_general x5, matrix products, dot_tn(): lax.dot_general(left, right, (((0,), (0,)), ((), ())), preferred_element_...  47.9 us
  transfers between devices with their start and end apart: 6, of which 2 were waited for; matrix products, arithmetic and copies ran while one was open for 17% of the time, Pallas kernels for 41%

profile of v6, /device:TPU:0, one launch (start us, length us, event | category | flops | bytes accessed | tf_op | source)
XLA Modules:
  0.0 996.1 jit_solution(9830816487266061547)
XLA Ops:
  7.2 1.5 fusion.15
  8.7 0.6 multiply_multiply_fusion
  9.3 309.4 %shard_map.161 = (bf16[2048,2560]{1,0:T(8,128)(2,1)}, bf16[2048,2048]{1,0:T(8,128)(2,1)}, bf16[2048,11264]{1,0:T(8,128)(2,1)}, bf16[5632,2048]{1,0:T(8,128)(2,1)}) custom-call(bf16[256,2560]{1,0:T(8,128)(2,1)} %refs_0_.1, bf16[256,2048]{1,0:T(8,128)(2,1)} %refs_1_.1, bf16[256,11264]{1,0:T(8,128)(2,1)} %refs_2_.1, bf16[704,2048]{1,0:T(8,128)(2,1)} %refs_3_.1), custom_call_target="tpu_custom_call" | custom-call | bytes 900000000 | tf_op jit(solution)/shard_map/pallas_call | solution.py:503
  318.7 6.9 convolution_convert_fusion.5
  325.8 0.7 constant_dynamic-slice_fusion
  326.5 0.8 fusion.44
  327.5 2.3 collective-permute-start
  329.8 1.6 slice_convert_fusion
  331.4 3.4 copy.38
  335.0 1.9 subtract_convert_fusion.1
  337.3 8.8 fusion.58
  346.1 7.4 fusion.27
  353.6 6.2 multiply_reduce_fusion.2
  359.8 23.9 %fusion.56 = f32[256,11264]{1,0:T(8,128)} fusion(bf16[2048,11264]{1,0:T(8,128)(2,1)} %get-tuple-element.29, f32[256,2048]{1,0:T(8,128)S(1)} %get-tuple-element.83, f32[2048]{0:T(1024)S(1)} %copy-done.25, f32[256]{0:T(256)S(1)} %get-tuple-element.77), kind=kOutput, calls=%fused_computation.120 | convolution fusion | flops 11812732928 | bytes 59778048 | tf_op jit(solution)/shard_map/dot_general | solution.py:50
  383.7 5.2 multiply_convert_fusion.2
  389.0 6.1 convolution_convert_fusion.3
  395.3 17.6 %multiply_convert_fusion.1 = (bf16[256,5632]{1,0:T(8,128)(2,1)}, bf16[256,5632]{1,0:T(8,128)(2,1)}) fusion(f32[256,11264]{1,0:T(8,128)} %fusion.56, bf16[256,2048]{1,0:T(8,128)(2,1)} %bitcast.117, bf16[5632,2048]{1,0:T(8,128)(2,1)} %get-tuple-element.31), kind=kOutput, calls=%fused_computation.20 | convolution fusion | flops 5924323328 | bytes 41418752 | tf_op jit(solution)/shard_map/dot_general | solution.py:54
  412.9 22.1 %multiply_reduce_fusion.1 = (f32[256]{0:T(256)S(1)}, f32[2048]{0:T(1024)S(1)}, f32[256,2048]{1,0:T(8,128)}) fusion(f32[256,2048]{1,0:T(8,128)} %copy-done.5, f32[2048]{0:T(1024)S(1)} %copy-done.25, f32[256]{0:T(256)S(1)} %get-tuple-element.77, bf16[2048,11264]{1,0:T(8,128)(2,1)} %get-tuple-element.29, bf16[256,5632]{1,0:T(8,128)(2,1)} %get-tuple-element.54, ...), kind=kOutput, calls=%fused_computation.52 | convolution fusion | flops 11825838080 | bytes 56117248 | tf_op jit(solution)/shard_map/dot_general | solution.py:54
  435.0 3.2 subtract_add_fusion
  438.2 1.3 copy-done.7
  439.5 5.7 convolution_convert_fusion.4
  445.5 7.5 convolution_convert_fusion.6
  453.0 2.3 copy.40
  455.2 11.3 %fusion.1 = (f32[4,8,256]{2,1,0:T(8,128)S(1)}, f32[4,512,256,8]{2,1,3,0:T(8,128)}) fusion(f32[4,8,256,512]{2,3,1,0:T(8,128)} %get-tuple-element.81, f32[4,8,256]{2,1,0:T(8,128)S(1)} %get-tuple-element.80, bf16[512,4,64,1]{0,2,3,1:T(8,128)(2,1)S(1)} %bitcast.138, bf16[256,4,8,64]{0,3,2,1:T(8,128)(2,1)} %bitcast.130), kind=kOutput, calls=%fused_computation.4 | convolution fusion | flops 549445632 | bytes 34930688 | tf_op jit(solution)/shard_map/qgsd,kgd->gsqk/dot_general | solution.py:635
  466.5 12.0 %fusion.3 = bf16[4,8,256,512]{2,3,1,0:T(8,128)(2,1)S(1)} fusion(f32[4,512,256,8]{2,1,3,0:T(8,128)} %get-tuple-element.86, f32[4,8,256]{2,1,0:T(8,128)S(1)} %get-tuple-element.85, f32[4,8,256,512]{2,3,1,0:T(8,128)} %get-tuple-element.81, f32[4,8,256]{2,1,0:T(8,128)S(1)} %get-tuple-element.80), kind=kLoop, calls=%fused_computation.6 | loop fusion | flops 16777216 | bytes 42008576 | tf_op jit(solution)/shard_map/convert_element_type | solution.py:637
  478.5 2.6 fusion.30
  481.2 7.4 fusion.8
  488.7 1.7 collective-permute-start.1
  490.4 1.6 convolution_multiply_fusion
  491.9 0.4 subtract_convert_fusion
  492.4 4.4 collective-permute-done.1
  497.1 6.8 convolution_convert_fusion.1
  504.0 0.3 all-reduce.3.cloned.1.call-start
  504.3 7.2 convolution_convert_fusion.2
  511.5 22.1 %convolution_convert_fusion = bf16[2048,11264]{1,0:T(8,128)(2,1)} fusion(bf16[256,5632]{1,0:T(8,128)(2,1)} %get-tuple-element.54, bf16[256,5632]{1,0:T(8,128)(2,1)} %get-tuple-element.53, f32[256,2048]{1,0:T(8,128)} %copy-done.5, f32[2048]{0:T(1024)S(1)} %copy-done.25, f32[256]{0:T(256)S(1)} %get-tuple-element.77), kind=kOutput, calls=%fused_computation.1 | convolution fusion | flops 11847335936 | bytes 54010880 | tf_op jit(solution)/shard_map/dot_general | solution.py:58
  533.6 8.5 fusion.24
  542.1 0.6 pad_maximum_fusion.20.small
  542.7 276.8 %shard_map.162 = (bf16[256,11264]{1,0:T(8,128)(2,1)}, bf16[11,4,256,1024]{3,2,1,0:T(8,128)(2,1)}, f32[32,128]{1,0:T(8,128)}) custom-call(bf16[4,2,256,11264]{3,2,1,0:T(8,128)(2,1)} %bitcast.109, f32[32,128]{1,0:T(8,128)} %pad_maximum_fusion.20.small), custom_call_target="tpu_custom_call" | custom-call | bytes 800000000 | tf_op jit(solution)/shard_map/pallas_call | solution.py:331
  819.5 1.5 reduce-scatter.8.cloned.1.call-done
  821.1 3.8 fusion.31
  824.9 0.6 broadcast_in_dim.16.small
  825.5 133.8 %shard_map.163 = (bf16[704,1024]{1,0:T(8,128)(2,1)}, bf16[4,4,704,256]{3,2,1,0:T(8,128)(2,1)}, f32[8,128]{1,0:T(8,128)}) custom-call(bf16[4,2,704,1024]{3,2,1,0:T(8,128)(2,1)} %bitcast.110, f32[8,128]{1,0:T(8,128)} %broadcast_in_dim.16.small), custom_call_target="tpu_custom_call" | custom-call | bytes 800000000 | tf_op jit(solution)/shard_map/pallas_call | solution.py:331
  959.4 8.6 convert_element_type.136
  967.9 0.6 slice_bitcast_fusion
  968.6 12.4 %fusion.14 = bf16[1,256,2048]{2,1,0:T(8,128)(2,1)} fusion(f32[256,2048]{1,0:T(8,128)S(1)} %copy-done.6, bf16[256,5632]{1,0:T(8,128)(2,1)S(1)} %copy-done.1, bf16[5632,2048]{1,0:T(8,128)(2,1)} %get-tuple-element.31), kind=kOutput, calls=%fused_computation.39 | convolution fusion | flops 5906628608 | bytes 29097984 | tf_op jit(solution)/shard_map/dot_general | solution.py:50
  981.0 3.3 convert_element_type.134
  984.2 1.6 convert_element_type.135
  985.8 3.3 maximum_convert_fusion
  (101 shorter events, 1.9 us)
Async XLA Ops:
  7.2 535.5 %reduce-scatter.4.cloned.1.call-start = ((), (), s32[]{:S(2)}) async-start(), calls=%async_computation.3 | async-start | bytes 12976128 | tf_op jit(solution)/shard_map/reduce_scatter | solution.py:531
  9.3 309.4 %copy-start.29 = (f32[256]{0:T(256)}, f32[256]{0:T(256)S(1)}, u32[]{:S(2)}) copy-start(f32[256]{0:T(256)S(1)} %get-tuple-element.75) | copy-start | bytes 3076
  9.3 309.4 %copy-start.2 = (bf16[1,256,2048]{2,1,0:T(8,128)(2,1)S(1)}, bf16[1,256,2048]{2,1,0:T(8,128)(2,1)}, u32[]{:S(2)}) copy-start(bf16[1,256,2048]{2,1,0:T(8,128)(2,1)} %param.10) | copy-start | bytes 3145732
  9.3 309.4 %copy-start.27 = (f32[2048]{0:T(1024)S(1)}, f32[2048]{0:T(1024)}, u32[]{:S(2)}) copy-start(f32[2048]{0:T(1024)} %param.14) | copy-start | bytes 24580
  318.7 7.1 copy-start.33
  327.3 7.6 copy-start.23
  327.5 9.4 collective-permute-start
  336.9 9.2 copy-start.13
  336.9 9.2 copy-start.15
  337.1 8.9 copy-start.21
  353.5 6.2 copy-start.8
  353.5 6.3 copy-start.25
  359.8 23.9 %copy-start.5 = (f32[256,2048]{1,0:T(8,128)}, f32[256,2048]{1,0:T(8,128)S(1)}, u32[]{:S(2)}) copy-start(f32[256,2048]{1,0:T(8,128)S(1)} %get-tuple-element.83) | copy-start | bytes 6291460
  383.7 5.3 copy-start.10
  389.0 115.3 %copy-start = (bf16[256,5632]{1,0:T(8,128)(2,1)}, bf16[256,5632]{1,0:T(8,128)(2,1)S(1)}, u32[]{:S(2)}) copy-start(bf16[256,5632]{1,0:T(8,128)(2,1)S(1)} %multiply_convert_fusion.2) | copy-start | bytes 8650756
  395.1 424.4 %reduce-scatter.6.cloned.1.call-start = ((), (), s32[]{:S(2)}) async-start(), calls=%async_computation.4 | async-start | bytes 9437184 | tf_op jit(solution)/shard_map/reduce_scatter | solution.py:531
  435.0 4.6 copy-start.9
  438.2 1.3 copy-start.7
  445.2 375.8 %reduce-scatter.8.cloned.1.call-start = ((), (), s32[]{:S(2)}) async-start(), calls=%async_computation.5 | async-start | bytes 11796480 | tf_op jit(solution)/shard_map/reduce_scatter | solution.py:531
  466.5 12.0 %copy-start.14 = (bf16[256,32,32]{0,2,1:T(8,128)(2,1)S(1)}, bf16[256,32,32]{0,2,1:T(8,128)(2,1)}, u32[]{:S(2)}) copy-start(bf16[256,32,32]{0,2,1:T(8,128)(2,1)} %copy-done.13) | copy-start | bytes 1572868
  466.5 12.0 %copy-start.16 = (bf16[256,32,32]{0,2,1:T(8,128)(2,1)S(1)}, bf16[256,32,32]{0,2,1:T(8,128)(2,1)}, u32[]{:S(2)}) copy-start(bf16[256,32,32]{0,2,1:T(8,128)(2,1)} %copy-done.15) | copy-start | bytes 1572868
  478.5 2.6 copy-start.20
  481.2 9.2 copy-start.22
  488.7 3.3 copy-start.24
  488.7 3.3 copy-start.26
  488.7 8.2 collective-permute-start.1
  492.3 4.8 copy-start.3
  492.3 4.8 copy-start.28
  492.3 4.8 copy-start.30
  492.4 4.6 copy-start.11
  504.0 477.0 %all-reduce.3.cloned.1.call-start = ((), (), s32[]{:S(2)}) async-start(), calls=%async_computation.6 | async-start | bytes 7602176 | tf_op jit(solution)/shard_map/psum | solution.py:681
  511.5 22.1 %copy-start.4 = (bf16[1,256,2048]{2,1,0:T(8,128)(2,1)S(1)}, bf16[1,256,2048]{2,1,0:T(8,128)(2,1)}, u32[]{:S(2)}) copy-start(bf16[1,256,2048]{2,1,0:T(8,128)(2,1)} %param.10) | copy-start | bytes 3145732
  511.5 22.1 %copy-start.12 = (bf16[256,32,64]{0,2,1:T(8,128)(2,1)S(1)}, bf16[256,32,64]{0,2,1:T(8,128)(2,1)}, u32[]{:S(2)}) copy-start(bf16[256,32,64]{0,2,1:T(8,128)(2,1)} %copy-done.11) | copy-start | bytes 3145732
  819.5 1.6 copy-start.32
  959.3 8.6 copy-start.31
  959.3 9.2 copy-start.1
  959.4 9.2 copy-start.6
  981.0 3.3 copy-start.19
  981.0 4.8 copy-start.17
  981.0 4.8 copy-start.18
Sparse Core Ops, SparseCore 0:
  395.2 121.2 reduce-scatter.3
  518.8 103.0 reduce-scatter.5
  624.2 196.7 reduce-scatter.7
  824.3 141.9 all-reduce.2

commit v7 on v3

--- a/solution.py
+++ b/solution.py
@@ -611,7 +611,6 @@
     up_part = gate_up[:, ff_width:]
     sigmoid_gate = jax.nn.sigmoid(gate_part)
     hidden_low = (gate_part * sigmoid_gate * up_part).astype(BF16)
-    output = (residual + dot(hidden_low, down_whole)).astype(BF16)
 
     grad_out = cotangent[0].astype(F32)
     grad_down = cotangent[0]
@@ -619,7 +618,6 @@
     early_terms = dot_tn(hidden_low, grad_down[:, :early]).astype(BF16)
     early_terms, grad_down = lax.optimization_barrier((early_terms, grad_down))
     down_early = scatter_rows(early_terms)
-    down_terms = dot_tn(hidden_low, grad_down[:, early:]).astype(BF16)
     grad_hidden = dot_nt(grad_down, down_whole)
     grad_gate = grad_hidden * up_part * sigmoid_gate * (1.0 + gate_part * (1.0 - sigmoid_gate))
     grad_up = grad_hidden * gate_part * sigmoid_gate
@@ -663,19 +661,29 @@
     ).astype(BF16)
     qkv_terms, down_early = lax.optimization_barrier((dot_tn(normed_low, grad_qkv).astype(BF16), down_early))
     qkv_part = scatter_rows(qkv_terms)
-    grad_normed = dot_nt(grad_qkv, qkv_whole)
-    attn_term = jnp.sum(grad_normed * inputs * inv_first, axis=0)
-    tokens_grad = (grad_resid + norm_back(grad_normed, inputs, inv_first, attn_gain)).astype(BF16)
-    gains = jnp.concatenate([attn_term, mlp_term]).reshape(-1, 128)
+    def finish(grad_qkv):
+        grad_normed = dot_nt(grad_qkv, qkv_whole)
+        attn_term = jnp.sum(grad_normed * inputs * inv_first, axis=0)
+        back = norm_back(grad_normed, inputs, inv_first, attn_gain)
+        gains = jnp.concatenate([attn_term, mlp_term]).reshape(-1, 128)
+        return (grad_resid + back).astype(BF16), gains
+
+    two = down_weight.shape[0] // seq % 16 == 0
+    gains = jnp.zeros((8, 128), F32)
+    if not two:
+        tokens_grad, gains = finish(grad_qkv)
     gate_up_grad, gains = reduced(gate_up_terms, gains, chips, bits, 11, 0)
-    gains = gains.reshape(-1)
-    gate_up_grad, down_early, out_part, qkv_part, down_terms = lax.optimization_barrier(
-        (gate_up_grad, down_early, out_part, qkv_part, down_terms)
-    )
-    if down_weight.shape[0] // seq % 16 == 0:
-        down_late, _ = reduced(down_terms, jnp.zeros((8, 128), F32), chips, bits, 4, 2)
+    gate_up_grad, down_early, out_part, qkv_part, hidden_low, grad_qkv = lax.optimization_barrier(
+        (gate_up_grad, down_early, out_part, qkv_part, hidden_low, grad_qkv)
+    )
+    output = (residual + dot(hidden_low, down_whole)).astype(BF16)
+    down_terms = dot_tn(hidden_low, grad_down[:, early:]).astype(BF16)
+    if two:
+        tokens_grad, gains = finish(grad_qkv)
+        down_late, gains = reduced(down_terms, gains, chips, bits, 4, 2)
     else:
         down_late = lax.psum(scatter_rows(down_terms), "seq")
+    gains = gains.reshape(-1)
     down_early, out_grad, qkv_grad = lax.psum((down_early, out_part, qkv_part), "seq")
     down_grad = jnp.concatenate([down_early, down_late], axis=1)
     return (

time: 994 us -> 1010 us (1.016)
  transfers between devices with their start and end apart: 6 -> 6, of which waited for: 2 -> 3; matrix products, arithmetic and copies ran while one was open for 17% -> 17% of each run, Pallas kernels for 40% -> 40%
where the time goes in v7:
time: 1010 us
  Pallas kernels  710 us (70%)
  matrix products  197 us (20%)
  other arithmetic  51.8 us (5%)
  waiting for transfers between devices  14.9 us (1%)
  between operations  14.9 us (1%)
  local copies, waits for them, and re-layouts  12 us (1%)
    pallas_call x2, Pallas kernels, reduced(): pl.pallas_call(functools.partial(reduce_kernel, chips, bits, count), out_...  401 us
    pallas_call x1, Pallas kernels, gathered(): pl.pallas_call(functools.partial(gather_kernel, chips, bits, units, weigh...  309 us
    dot_general x4, matrix products, dot_nt(): lax.dot_general(left, right, (((1,), (1,)), ((), ())), preferred_element_...  61 us
    dot_general x4, matrix products, dot(): return jnp.dot(left, right, preferred_element_type=F32)  49.4 us
    dot_general x5, matrix products, dot_tn(): lax.dot_general(left, right, (((0,), (0,)), ((), ())), preferred_element_...  47.7 us
  transfers between devices with their start and end apart: 6, of which 3 were waited for; matrix products, arithmetic and copies ran while one was open for 17% of the time, Pallas kernels for 40%

profile of v7, /device:TPU:0, one launch (start us, length us, event | category | flops | bytes accessed | tf_op | source)
XLA Modules:
  0.0 1005.1 jit_solution(7728243591818247462)
XLA Ops:
  7.2 1.5 fusion.15
  9.3 309.4 %shard_map.161 = (bf16[2048,2560]{1,0:T(8,128)(2,1)}, bf16[2048,2048]{1,0:T(8,128)(2,1)}, bf16[2048,11264]{1,0:T(8,128)(2,1)}, bf16[5632,2048]{1,0:T(8,128)(2,1)}) custom-call(bf16[256,2560]{1,0:T(8,128)(2,1)} %refs_0_.1, bf16[256,2048]{1,0:T(8,128)(2,1)} %refs_1_.1, bf16[256,11264]{1,0:T(8,128)(2,1)} %refs_2_.1, bf16[704,2048]{1,0:T(8,128)(2,1)} %refs_3_.1), custom_call_target="tpu_custom_call" | custom-call | bytes 900000000 | tf_op jit(solution)/shard_map/pallas_call | solution.py:503
  318.7 6.9 convolution_convert_fusion.5
  325.8 0.7 constant_dynamic-slice_fusion
  326.5 0.8 fusion.43
  327.5 2.3 collective-permute-start
  329.8 1.6 slice_convert_fusion
  331.4 3.4 copy.38
  335.0 1.9 subtract_convert_fusion.1
  337.3 8.8 fusion.55
  346.1 7.4 fusion.27
  353.6 6.2 multiply_reduce_fusion.2
  359.8 23.9 %fusion.53 = f32[256,11264]{1,0:T(8,128)} fusion(bf16[2048,11264]{1,0:T(8,128)(2,1)} %get-tuple-element.27, f32[256,2048]{1,0:T(8,128)S(1)} %get-tuple-element.79, f32[2048]{0:T(1024)S(1)} %copy-done.26, f32[256]{0:T(256)S(1)} %get-tuple-element.73), kind=kOutput, calls=%fused_computation.117 | convolution fusion | flops 11812732928 | bytes 59778048 | tf_op jit(solution)/shard_map/dot_general | solution.py:50
  383.7 5.2 multiply_convert_fusion.2
  389.0 1.6 copy-done
  390.6 6.1 convolution_convert_fusion.3
  396.9 24.9 %multiply_convert_fusion.1 = (bf16[256,5632]{1,0:T(8,128)(2,1)}, bf16[256,5632]{1,0:T(8,128)(2,1)}) fusion(f32[256,11264]{1,0:T(8,128)} %fusion.53, bf16[256,2048]{1,0:T(8,128)(2,1)S(1)} %bitcast.121, bf16[5632,2048]{1,0:T(8,128)(2,1)} %get-tuple-element.29), kind=kOutput, calls=%fused_computation.20 | convolution fusion | flops 5924323328 | bytes 41418752 | tf_op jit(solution)/shard_map/dot_general | solution.py:54
  421.8 21.8 %multiply_reduce_fusion = (f32[2048]{0:T(1024)S(1)}, f32[256]{0:T(256)S(1)}, f32[256,2048]{1,0:T(8,128)}) fusion(f32[256,2048]{1,0:T(8,128)S(1)} %copy-done.5, f32[256]{0:T(256)S(1)} %get-tuple-element.73, f32[2048]{0:T(1024)S(1)} %copy-done.26, bf16[2048,11264]{1,0:T(8,128)(2,1)} %get-tuple-element.27, bf16[256,5632]{1,0:T(8,128)(2,1)} %get-tuple-element.50, ...), kind=kOutput, calls=%fused_computation.50 | convolution fusion | flops 11825838080 | bytes 56117248 | tf_op jit(solution)/shard_map/dot_general | solution.py:54
  443.6 2.4 subtract_add_fusion
  446.0 1.3 copy-done.7
  447.3 5.6 convolution_convert_fusion.4
  453.2 1.3 copy-done.8
  454.5 5.9 convolution_convert_fusion.6
  460.9 10.8 %fusion.1 = (f32[4,8,256]{2,1,0:T(8,128)S(1)}, f32[4,512,256,8]{2,1,3,0:T(8,128)}) fusion(f32[4,8,256,512]{2,3,1,0:T(8,128)} %get-tuple-element.77, f32[4,8,256]{2,1,0:T(8,128)S(1)} %copy-done.31, bf16[512,4,64,1]{0,2,3,1:T(8,128)(2,1)S(1)} %bitcast.139, bf16[256,4,8,64]{0,3,2,1:T(8,128)(2,1)S(1)} %bitcast.133), kind=kOutput, calls=%fused_computation.4 | convolution fusion | flops 549445632 | bytes 34930688 | tf_op jit(solution)/shard_map/qgsd,kgd->gsqk/dot_general | solution.py:634
  471.8 12.0 %fusion.3 = bf16[4,8,256,512]{2,3,1,0:T(8,128)(2,1)S(1)} fusion(f32[4,512,256,8]{2,1,3,0:T(8,128)} %get-tuple-element.82, f32[4,8,256]{2,1,0:T(8,128)S(1)} %get-tuple-element.81, f32[4,8,256,512]{2,3,1,0:T(8,128)} %get-tuple-element.77, f32[4,8,256]{2,1,0:T(8,128)S(1)} %copy-done.31), kind=kLoop, calls=%fused_computation.6 | loop fusion | flops 16777216 | bytes 42008576 | tf_op jit(solution)/shard_map/convert_element_type | solution.py:636
  483.8 2.6 fusion.30
  486.5 7.4 fusion.8
  494.0 1.6 collective-permute-start.1
  495.6 1.5 convolution_multiply_fusion
  497.7 4.5 collective-permute-done.1
  502.4 6.7 convolution_convert_fusion.1
  509.1 9.0 reduce-scatter.4.cloned.1.call-done
  518.4 21.5 %convolution_convert_fusion = bf16[2048,11264]{1,0:T(8,128)(2,1)} fusion(bf16[256,5632]{1,0:T(8,128)(2,1)} %get-tuple-element.50, bf16[256,5632]{1,0:T(8,128)(2,1)} %get-tuple-element.49, f32[256,2048]{1,0:T(8,128)} %copy-done.4, f32[2048]{0:T(1024)S(1)} %copy-done.26, f32[256]{0:T(256)S(1)} %get-tuple-element.73), kind=kOutput, calls=%fused_computation.1 | convolution fusion | flops 11847335936 | bytes 54010880 | tf_op jit(solution)/shard_map/dot_general | solution.py:58
  540.5 273.0 %shard_map.162 = (bf16[256,11264]{1,0:T(8,128)(2,1)}, bf16[11,4,256,1024]{3,2,1,0:T(8,128)(2,1)}, f32[8,128]{1,0:T(8,128)}) custom-call(bf16[4,2,256,11264]{3,2,1,0:T(8,128)(2,1)} %bitcast.110, f32[8,128]{1,0:T(8,128)} %broadcast_in_dim.16.small), custom_call_target="tpu_custom_call" | custom-call | bytes 800000000 | tf_op jit(solution)/shard_map/pallas_call | solution.py:331
  813.5 2.5 pad_maximum_fusion.3
  816.0 1.3 reduce-scatter.8.cloned.1.call-done
  817.3 7.9 convolution_convert_fusion.2
  825.3 1.3 copy-done.20
  826.5 8.4 fusion.24
  835.0 9.1 convert_element_type.136
  844.0 0.6 pad_maximum_fusion.18.small
  844.6 127.6 %shard_map.163 = (bf16[704,1024]{1,0:T(8,128)(2,1)}, bf16[4,4,704,256]{3,2,1,0:T(8,128)(2,1)}, f32[32,128]{1,0:T(8,128)}) custom-call(bf16[4,2,704,1024]{3,2,1,0:T(8,128)(2,1)} %bitcast.111, f32[32,128]{1,0:T(8,128)} %pad_maximum_fusion.18.small), custom_call_target="tpu_custom_call" | custom-call | bytes 800000000 | tf_op jit(solution)/shard_map/pallas_call | solution.py:331
  972.2 1.3 slice_bitcast_fusion
  973.6 4.0 fusion.31
  977.5 12.4 %fusion.14 = bf16[1,256,2048]{2,1,0:T(8,128)(2,1)} fusion(f32[256,2048]{1,0:T(8,128)S(1)} %copy-done.6, bf16[256,5632]{1,0:T(8,128)(2,1)S(1)} %copy-done.1, bf16[5632,2048]{1,0:T(8,128)(2,1)} %get-tuple-element.29), kind=kOutput, calls=%fused_computation.39 | convolution fusion | flops 5906628608 | bytes 29097984 | tf_op jit(solution)/shard_map/dot_general | solution.py:50
  989.9 3.3 convert_element_type.134
  993.2 1.6 convert_element_type.135
  994.8 3.3 maximum_convert_fusion
  (106 shorter events, 4.2 us)
Async XLA Ops:
  7.2 510.9 %reduce-scatter.4.cloned.1.call-start = ((), (), s32[]{:S(2)}) async-start(), calls=%async_computation.3 | async-start | bytes 12976128 | tf_op jit(solution)/shard_map/reduce_scatter | solution.py:531
  9.3 309.4 %copy-start.32 = (f32[256]{0:T(256)}, f32[256]{0:T(256)S(1)}, u32[]{:S(2)}) copy-start(f32[256]{0:T(256)S(1)} %get-tuple-element.71) | copy-start | bytes 3076
  9.3 309.4 %copy-start.2 = (bf16[1,256,2048]{2,1,0:T(8,128)(2,1)S(1)}, bf16[1,256,2048]{2,1,0:T(8,128)(2,1)}, u32[]{:S(2)}) copy-start(bf16[1,256,2048]{2,1,0:T(8,128)(2,1)} %param.10) | copy-start | bytes 3145732
  9.3 309.4 %copy-start.28 = (f32[2048]{0:T(1024)S(1)}, f32[2048]{0:T(1024)}, u32[]{:S(2)}) copy-start(f32[2048]{0:T(1024)} %param.14) | copy-start | bytes 24580
  318.7 7.1 copy-start.35
  327.3 7.6 copy-start.24
  327.5 9.4 collective-permute-start
  336.9 9.2 copy-start.14
  336.9 9.2 copy-start.16
  337.1 8.9 copy-start.22
  346.1 7.5 copy-start.30
  353.5 6.2 copy-start.10
  353.6 6.3 copy-start.26
  359.8 23.9 %copy-start.4 = (f32[256,2048]{1,0:T(8,128)}, f32[256,2048]{1,0:T(8,128)S(1)}, u32[]{:S(2)}) copy-start(f32[256,2048]{1,0:T(8,128)S(1)} %get-tuple-element.79) | copy-start | bytes 6291460
  383.7 6.8 copy-start.12
  389.0 1.6 copy-start
  396.7 419.3 %reduce-scatter.6.cloned.1.call-start = ((), (), s32[]{:S(2)}) async-start(), calls=%async_computation.4 | async-start | bytes 9437184 | tf_op jit(solution)/shard_map/reduce_scatter | solution.py:531
  396.9 25.0 %copy-start.5 = (f32[256,2048]{1,0:T(8,128)S(1)}, f32[256,2048]{1,0:T(8,128)}, u32[]{:S(2)}) copy-start(f32[256,2048]{1,0:T(8,128)} %copy-done.4) | copy-start | bytes 6291460
  443.6 3.7 copy-start.11
  446.0 1.3 copy-start.7
  452.9 1.6 copy-start.8
  452.9 8.0 copy-start.31
  453.0 364.4 %reduce-scatter.8.cloned.1.call-start = ((), (), s32[]{:S(2)}) async-start(), calls=%async_computation.5 | async-start | bytes 11796480 | tf_op jit(solution)/shard_map/reduce_scatter | solution.py:531
  471.8 12.0 %copy-start.15 = (bf16[256,32,32]{0,2,1:T(8,128)(2,1)S(1)}, bf16[256,32,32]{0,2,1:T(8,128)(2,1)}, u32[]{:S(2)}) copy-start(bf16[256,32,32]{0,2,1:T(8,128)(2,1)} %copy-done.14) | copy-start | bytes 1572868
  471.8 12.0 %copy-start.17 = (bf16[256,32,32]{0,2,1:T(8,128)(2,1)S(1)}, bf16[256,32,32]{0,2,1:T(8,128)(2,1)}, u32[]{:S(2)}) copy-start(bf16[256,32,32]{0,2,1:T(8,128)(2,1)} %copy-done.16) | copy-start | bytes 1572868
  486.5 9.1 copy-start.23
  494.0 3.2 copy-start.25
  494.0 3.2 copy-start.27
  494.0 8.2 collective-permute-start.1
  497.5 4.8 copy-start.3
  497.5 4.8 copy-start.29
  497.5 4.8 copy-start.33
  497.6 4.7 copy-start.9
  518.1 471.8 %all-reduce.3.cloned.1.call-start = ((), (), s32[]{:S(2)}) async-start(), calls=%async_computation.6 | async-start | bytes 7602176 | tf_op jit(solution)/shard_map/psum | solution.py:687
  813.5 3.8 copy-start.13
  825.2 1.3 copy-start.20
  844.6 128.9 %copy-start.34 = (f32[256]{0:T(256)S(1)}, f32[256]{0:T(256)}, u32[]{:S(2)}) copy-start(f32[256]{0:T(256)} %get-tuple-element.70) | copy-start | bytes 3076
  973.6 4.0 copy-start.1
  973.6 4.0 copy-start.6
  989.9 3.3 copy-start.21
  989.9 4.8 copy-start.18
  989.9 4.8 copy-start.19
Sparse Core Ops, SparseCore 0:
  396.8 121.2 reduce-scatter.3
  520.4 107.1 reduce-scatter.5
  630.5 186.7 reduce-scatter.7
  825.4 140.2 all-reduce.2
